TPU v7x, 256 devices: a whole 4x4x8 slice. The times are simulated.
256 devices in a mesh: grp: 8 (over y, x_lo), brick: 32 (over z, x_hi, core).
Axes of the slice: x: 4 (x_hi: 2, x_lo: 2; x = x_hi * 2 + x_lo), y: 4, z: 8, core: 2. Of those that a mesh axis runs over, the one named last changes fastest.
Arguments:
- positions: float32 [3, 8388608], P(None, ('grp', 'brick')), may hold values from -4 to 4
- charges: float32 [8388608], P(('grp', 'brick')), may hold values from -5 to 5
- cluster_fill: int32 [65536], P(('grp', 'brick')), may hold values from 1 to 128, as said below
- cluster_cell: int32 [65536], P(('grp', 'brick')), may hold values from 0 to 131071
- send_index: int32 [1792, 32], P(('grp', 'brick')), may hold values from 0 to 255
- send_count: int32 [256, 7], P(('grp', 'brick')), may hold values from 1 to 32, as said below
- pair_local: int32 [262144], P(('grp', 'brick')), may hold values from 0 to 255
- pair_dir: int32 [262144], P(('grp', 'brick')), may hold values from 0 to 6, as said below
- pair_slot: int32 [262144], P(('grp', 'brick')), may hold values from 0 to 31
- ion_density: float32 [128, 1024, 256], P('grp', 'brick'), may hold values from 0.2 to 2
- potential_prev: float32 [128, 1024, 256], P('grp', 'brick'), may hold values from -6 to 6
- screening: float32 [128, 1024, 256], P('grp', 'brick'), may hold values from 0.05 to 0.5
Outputs:
- forces: float32 [3, 8388608], P(None, ('grp', 'brick'))
- potential: float32 [128, 1024, 256], P('grp', 'brick')
- ion_next: float32 [128, 1024, 256], P('grp', 'brick')
Inputs may be any that keep to these rules, and one draw needn't show every extreme that they name: `cluster_fill`: live particles of a cluster; later slots are padding; some cluster is full. `send_count`: every device sends 32 live slots in some direction. `send_index`: local cluster indices; row e * 7 + k lists what device e sends to the device at minus the offset of direction k. `pair_local`: local cluster indices. `pair_dir`: a direction never names a device outside the room. `pair_slot`: slot indices; a slot at or past the sender's count carries no charge. `cluster_cell`: cell indices within a device's block.
All inputs are finite; a program needn't handle non-finite values.
Results may differ from a plain program's by a relative error of at most 0.0001.
Values sent between devices are 32-bit elements; how exact they have to be, the bound alone decides.
A program may use at most 192 MiB of HBM per device.

v0:
```python
import math

import jax
import jax.numpy as jnp
from jax import lax
from jax.sharding import PartitionSpec as P

SWEEPS = 4


coulomb_scale = 0.02
softening = 0.1
field_scale = 0.5
deposit_scale = 0.2
lowest_eig = 0.01
highest_eig = 1.99
mobility = 0.3
diffusion = 0.2
time_step = 0.2


def extended(shard, sides, width):
    for axis, dim in sides:
        devices, length = (lax.axis_size(axis), shard.shape[dim])
        up = [(i, (i + 1) % devices) for i in range(devices - 1)]
        down = [(j, i) for i, j in up]
        last = lax.slice_in_dim(shard, length - width, length, axis=dim)
        initial = lax.slice_in_dim(shard, 0, width, axis=dim)
        before = lax.ppermute(last, axis, up)
        after = lax.ppermute(initial, axis, down)
        shard = jnp.concatenate([before, shard, after], axis=dim)
    return shard


def passed_along(shard, axis, by):
    devices = lax.axis_size(axis)
    pairs = [(i, i + by) for i in range(devices) if 0 <= i + by < devices]
    return lax.ppermute(shard, axis, pairs)


def stencil_core(padded, center, screen):
    beside = padded[2:, 1:-1, 1:-1] + padded[:-2, 1:-1, 1:-1]
    beside = beside + padded[1:-1, 2:, 1:-1] + padded[1:-1, :-2, 1:-1]
    beside = beside + padded[1:-1, 1:-1, 2:] + padded[1:-1, 1:-1, :-2]
    return (6.0 + screen) * center - beside


def operate_rim(field, screen):
    rimmed = extended(field, (("grp", 0), ("brick", 1)), 1)
    padded = jnp.pad(rimmed, ((0, 0), (0, 0), (1, 1)))
    return stencil_core(padded, field, screen)


def chebyshev(start, rhs, screen, operate, inside):
    middle = 0.5 * (highest_eig + lowest_eig)
    spread = 0.5 * (highest_eig - lowest_eig)
    ratio_ms = middle / spread
    weight_now = 1.0 / ratio_ms
    inverse = 1.0 / (6.0 + screen)
    solution = start
    resid = rhs - operate(solution, screen)
    update = inside * (inverse * resid / middle)
    for turn in range(SWEEPS):
        solution = solution + update
        if turn + 1 < SWEEPS:
            resid = resid - operate(update, screen)
            weight_next = 1.0 / (2.0 * ratio_ms - weight_now)
            update = inside * (
                weight_next * weight_now * update + 2.0 * weight_next / spread * (inverse * resid)
            )
            weight_now = weight_next
    return solution


def tile_forces(own, other):
    diff = own[:, :3, :, None] - other[:, :3, None, :]
    dist = jnp.sum(diff * diff, axis=1) + softening
    weight = coulomb_scale * own[:, 3, :, None] * other[:, 3, None, :] / (dist * jnp.sqrt(dist))
    pull = diff * weight[:, None]
    return (jnp.sum(pull, axis=3), jnp.sum(pull, axis=2))


def face_div(pot, ions, axis):
    inner = [slice(1, -1), slice(1, -1), slice(1, -1)]
    inner[axis] = slice(None)
    pot = pot[tuple(inner)]
    ions = ions[tuple(inner)]

    def upper(arr):
        return lax.slice_in_dim(arr, 1, arr.shape[axis], axis=axis)

    def lower(arr):
        return lax.slice_in_dim(arr, 0, arr.shape[axis] - 1, axis=axis)

    speed = -mobility * (upper(pot) - lower(pot))
    flux = (
        jnp.maximum(speed, 0.0) * lower(ions)
        + jnp.minimum(speed, 0.0) * upper(ions)
        - diffusion * (upper(ions) - lower(ions))
    )
    return upper(flux) - lower(flux)


def field_of(padded):
    along_x = -(padded[2:, 1:-1, 1:-1] - padded[:-2, 1:-1, 1:-1]) * 0.5
    along_y = -(padded[1:-1, 2:, 1:-1] - padded[1:-1, :-2, 1:-1]) * 0.5
    along_z = -(padded[1:-1, 1:-1, 2:] - padded[1:-1, 1:-1, :-2]) * 0.5
    return jnp.stack([along_x, along_y, along_z])


def shards(
    positions,
    charges,
    cluster_fill,
    cluster_cell,
    send_index,
    send_count,
    pair_local,
    pair_dir,
    pair_slot,
    ion_density,
    potential_prev,
    screening,
):
    clusters = cluster_fill.shape[0]
    psize = charges.shape[0] // clusters
    directions = send_index.shape[0]
    slots = send_index.shape[1]
    lanes = jnp.arange(psize, dtype=jnp.int32)
    qmask = charges.reshape(clusters, psize) * (lanes[None, :] < cluster_fill[:, None]).astype(
        jnp.float32
    )
    cluster_data = jnp.concatenate(
        [positions.reshape(3, clusters, psize).transpose(1, 0, 2), qmask[:, None, :]], axis=1
    )
    cells_x, cells_y, cells_z = ion_density.shape
    deposit = (
        jnp.zeros(cells_x * cells_y * cells_z, jnp.float32)
        .at[cluster_cell]
        .add(jnp.sum(qmask, axis=1))
    )
    rhs = ion_density + deposit_scale * deposit.reshape(cells_x, cells_y, cells_z)
    pairs = pair_local.shape[0]
    slot_ids = jnp.arange(slots, dtype=jnp.int32)
    slot_live = (slot_ids[None, :] < send_count.reshape(directions, 1)).astype(jnp.float32)
    outgoing = cluster_data[send_index]
    outgoing = jnp.concatenate(
        [outgoing[:, :, :3], (outgoing[:, :, 3] * slot_live[:, :, None])[:, :, None]], axis=2
    )
    pieces = [outgoing[0]]
    for offset in (-1, 1, -2, 2):
        pieces.append(passed_along(outgoing[len(pieces)], "brick", -offset))
    for offset in (-1, 1):
        pieces.append(passed_along(outgoing[len(pieces)], "grp", -offset))
    arrived = jnp.stack(pieces).reshape(directions * slots, 4, psize)
    partner_row = pair_dir * slots + pair_slot
    block = math.gcd(pairs, 32)

    def visit(carry, items):
        own_force, react = carry
        own_rows, other_rows = items
        own = cluster_data[own_rows]
        other = arrived[other_rows]
        pull_own, pull_other = tile_forces(own, other)
        return ((own_force.at[own_rows].add(pull_own), react.at[other_rows].add(-pull_other)), None)

    start_carry = (
        jnp.zeros((clusters, 3, psize), jnp.float32),
        jnp.zeros((directions * slots, 3, psize), jnp.float32),
    )
    (own_force, react), _ = lax.scan(
        visit, start_carry, (pair_local.reshape(-1, block), partner_row.reshape(-1, block))
    )
    react = react.reshape(directions, slots, 3, psize)
    backs = [react[0]]
    for offset in (-1, 1, -2, 2):
        backs.append(passed_along(react[len(backs)], "brick", offset))
    for offset in (-1, 1):
        backs.append(passed_along(react[len(backs)], "grp", offset))
    returned = jnp.stack(backs).reshape(directions * slots, 3, psize)
    coulomb = own_force.at[send_index.reshape(-1)].add(returned)
    potential = chebyshev(potential_prev, rhs, screening, operate_rim, 1.0)
    rimmed = extended(jnp.stack([potential, ion_density]), (("grp", 1), ("brick", 2)), 1)
    rimmed = jnp.pad(rimmed, ((0, 0), (0, 0), (0, 0), (1, 1)))
    padded_pot = rimmed[0]
    padded_ion = rimmed[1]
    ion_next = ion_density - time_step * (
        face_div(padded_pot, padded_ion, 0)
        + face_div(padded_pot, padded_ion, 1)
        + face_div(padded_pot, padded_ion, 2)
    )
    ecell = field_of(padded_pot).reshape(3, -1)[:, cluster_cell]
    forces = coulomb.transpose(1, 0, 2) + field_scale * qmask[None] * ecell[:, :, None]
    return (forces.reshape(3, -1), potential, ion_next)


def solution(mesh):
    in_specs = (
        P(None, ("grp", "brick")),
        P(("grp", "brick")),
        P(("grp", "brick")),
        P(("grp", "brick")),
        P(("grp", "brick"), None),
        P(("grp", "brick"), None),
        P(("grp", "brick")),
        P(("grp", "brick")),
        P(("grp", "brick")),
        P("grp", "brick", None),
        P("grp", "brick", None),
        P("grp", "brick", None),
    )
    out_specs = (P(None, ("grp", "brick")), P("grp", "brick", None), P("grp", "brick", None))
    return jax.shard_map(shards, mesh=mesh, in_specs=in_specs, out_specs=out_specs, check_vma=False)
```

profile of v0, /device:TPU:138, one launch (start us, length us, event | category | flops | bytes accessed | tf_op | source)
XLA Modules:
  0.0 680.7 jit_solution(15968245639226863285)
XLA Ops:
  16.8 7.3 %collective-permute-start.1 = (f32[32,4,128]{2,1,0:T(4,128)}, f32[32,4,128]{2,1,0:T(4,128)}, u32[]{:S(2)}, u32[]{:S(2)}) collective-permute-start(f32[32,4,128]{2,1,0:T(4,128)} %get-tuple-element.85), channel_id=1, source_target_pairs={{1,0},{2,1},{3,2},{4,3},{5,4},{6,5},{7,6},{8,7},{9,8},{10,9},{11,1... | collective-permute-start | bytes 196616 | tf_op jit(solution)/shard_map/ppermute | solution.py:38
  37.1 6.3 collective-permute-start.3
  43.4 4.4 collective-permute-start.4
  61.7 466.6 %while.12 = (s32[]{:T(128)}, f32[256,3,128]{2,1,0:T(4,128)S(1)}, f32[224,3,128]{2,1,0:T(4,128)S(1)}, s32[32,32]{1,0:T(8,128)}, f32[256,4,128]{2,1,0:T(4,128)}, /...) while((s32[]{:T(128)}, f32[256,3,128]{2,1,0:T(4,128)S(1)}, f32[224,3,128]{2,1,0:T(4,128)S(1)}, ...), condition=%wide.region_6.0_spmd, body=%wide.region_0.6_spmd.sunk | while | flops 12601538 | bytes 9446745 | solution.py:171
  69.0 4.0 fusion.80
  83.5 4.0 fusion.80
  98.1 4.0 fusion.80
  112.7 4.0 fusion.80
  127.3 4.0 fusion.80
  141.9 4.0 fusion.80
  185.7 4.0 fusion.80
  200.3 4.0 fusion.80
  214.8 4.0 fusion.80
  229.4 4.0 fusion.80
  244.0 4.0 fusion.80
  389.8 4.0 fusion.80
  404.4 4.0 fusion.80
  448.1 4.0 fusion.80
  462.7 4.0 fusion.80
  477.3 4.0 fusion.80
  491.9 4.0 fusion.80
  533.7 7.0 %collective-permute-start.6 = (f32[32,3,128]{2,1,0:T(4,128)S(1)}, f32[32,3,128]{2,1,0:T(4,128)S(1)}, u32[]{:S(2)}, u32[]{:S(2)}) collective-permute-start(f32[32,3,128]{2,1,0:T(4,128)S(1)} %get-tuple-element.102), channel_id=1, source_target_pairs={{1,0},{2,1},{3,2},{4,3},{5,4},{6,5},{7,6},{8,7},{9,8},{10,9},{11,1... | collective-permute-start | bytes 147464 | tf_op jit(solution)/shard_map/ppermute | solution.py:38
  544.9 5.0 collective-permute-start.9
  561.0 7.8 %collective-permute-start.22 = (f32[18,1,256]{2,1,0:T(1,128)S(1)}, f32[18,1,256]{2,1,0:T(1,128)S(1)}, u32[]{:S(2)}, u32[]{:S(2)}) collective-permute-start(f32[18,1,256]{2,1,0:T(1,128)S(1)} %get-tuple-element.77), channel_id=1, source_target_pairs={{1,0},{2,1},{3,2},{4,3},{5,4},{6,5},{7,6},{8,7},{9,8},{10,9},{11,1... | collective-permute-start | bytes 55304 | tf_op jit(solution)/shard_map/ppermute | solution.py:30
  570.9 5.1 collective-permute-start.11
  578.6 4.2 collective-permute-start.24
  593.1 6.3 collective-permute-done.27
  601.0 5.4 collective-permute-start.28
  608.4 5.1 collective-permute-done.29
  615.5 7.3 %collective-permute-start.31 = (f32[2,18,1,256]{3,2,1,0:T(1,128)S(1)}, f32[2,18,1,256]{3,2,1,0:T(1,128)S(1)}, u32[]{:S(2)}, u32[]{:S(2)}) collective-permute-start(f32[2,18,1,256]{3,2,1,0:T(1,128)S(1)} %get-tuple-element.68), channel_id=1, source_target_pairs={{1,0},{2,1},{3,2},{4,3},{5,4},{6,5},{7,6},{8,7},{9,8},{10,9},{11,1... | collective-permute-start | bytes 110600 | tf_op jit(solution)/shard_map/ppermute | solution.py:30
  622.8 8.2 %scatter_fusion.2 = f32[256,3,128]{2,1,0:T(4,128)S(1)} fusion(f32[256,3,128]{2,1,0:T(4,128)S(1)} %get-tuple-element.41, s32[224]{0:T(256)S(1)} %bitcast.110, f32[224,3,128]{2,1,0:T(4,128)S(1)} %bitcast.105), kind=kCustom, calls=%fused_computation.6 | custom fusion | flops 86016 | bytes 1033088 | tf_op jit(solution)/shard_map/scatter-add | solution.py:181
  643.7 30.5 %copy.22 = f32[3,131072]{0,1:T(8,128)} copy(f32[3,131072]{1,0:T(4,128)S(1)} %pad_maximum_fusion) | data formatting | bytes 3145728 | tf_op jit(solution)/shard_map/stack | solution.py:108
  (570 shorter events, 498.4 us)
Async XLA Ops:
  1.4 27.6 %collective-permute-start.13 = (f32[1,32,256]{2,1,0:T(8,128)S(1)}, f32[1,32,256]{2,1,0:T(8,128)S(1)}, u32[]{:S(2)}, u32[]{:S(2)}) collective-permute-start(f32[1,32,256]{2,1,0:T(8,128)S(1)} %get-tuple-element.96), channel_id=1, source_target_pairs={{0,32},{32,64},{64,96},{96,128},{128,160},{160,192},{192,224},{1,3... | collective-permute-start | bytes 98312 | tf_op jit(solution)/shard_map/ppermute | solution.py:29
  4.9 24.2 %collective-permute-start.12 = (f32[1,32,256]{2,1,0:T(8,128)S(1)}, f32[1,32,256]{2,1,0:T(8,128)S(1)}, u32[]{:S(2)}, u32[]{:S(2)}) collective-permute-start(f32[1,32,256]{2,1,0:T(8,128)S(1)} %get-tuple-element.95), channel_id=1, source_target_pairs={{32,0},{64,32},{96,64},{128,96},{160,128},{192,160},{224,192},{33,... | collective-permute-start | bytes 98312 | tf_op jit(solution)/shard_map/ppermute | solution.py:30
  14.7 34.9 %collective-permute-start = (f32[32,4,128]{2,1,0:T(4,128)}, f32[32,4,128]{2,1,0:T(4,128)}, u32[]{:S(2)}, u32[]{:S(2)}) collective-permute-start(f32[32,4,128]{2,1,0:T(4,128)} %get-tuple-element.84), channel_id=1, source_target_pairs={{0,1},{1,2},{2,3},{3,4},{4,5},{5,6},{6,7},{7,8},{8,9},{9,10},{10,1... | collective-permute-start | bytes 196616 | tf_op jit(solution)/shard_map/ppermute | solution.py:38
  16.8 35.6 %collective-permute-start.1 = (f32[32,4,128]{2,1,0:T(4,128)}, f32[32,4,128]{2,1,0:T(4,128)}, u32[]{:S(2)}, u32[]{:S(2)}) collective-permute-start(f32[32,4,128]{2,1,0:T(4,128)} %get-tuple-element.85), channel_id=1, source_target_pairs={{1,0},{2,1},{3,2},{4,3},{5,4},{6,5},{7,6},{8,7},{9,8},{10,9},{11,1... | collective-permute-start | bytes 196616 | tf_op jit(solution)/shard_map/ppermute | solution.py:38
  24.1 33.0 %collective-permute-start.2 = (f32[32,4,128]{2,1,0:T(4,128)}, f32[32,4,128]{2,1,0:T(4,128)}, u32[]{:S(2)}, u32[]{:S(2)}) collective-permute-start(f32[32,4,128]{2,1,0:T(4,128)} %get-tuple-element.86), channel_id=1, source_target_pairs={{0,2},{1,3},{2,4},{3,5},{4,6},{5,7},{6,8},{7,9},{8,10},{9,11},{10,... | collective-permute-start | bytes 196616 | tf_op jit(solution)/shard_map/ppermute | solution.py:38
  29.1 8.0 %collective-permute-start.14 = (f32[18,1,256]{2,1,0:T(1,128)S(1)}, f32[18,1,256]{2,1,0:T(1,128)S(1)}, u32[]{:S(2)}, u32[]{:S(2)}) collective-permute-start(f32[18,1,256]{2,1,0:T(1,128)S(1)} %get-tuple-element.81), channel_id=1, source_target_pairs={{1,0},{2,1},{3,2},{4,3},{5,4},{6,5},{7,6},{8,7},{9,8},{10,9},{11,1... | collective-permute-start | bytes 55304 | tf_op jit(solution)/shard_map/ppermute | solution.py:30
  32.9 10.5 %collective-permute-start.15 = (f32[18,1,256]{2,1,0:T(1,128)S(1)}, f32[18,1,256]{2,1,0:T(1,128)S(1)}, u32[]{:S(2)}, u32[]{:S(2)}) collective-permute-start(f32[18,1,256]{2,1,0:T(1,128)S(1)} %get-tuple-element.80), channel_id=1, source_target_pairs={{0,1},{1,2},{2,3},{3,4},{4,5},{5,6},{6,7},{7,8},{8,9},{9,10},{10,1... | collective-permute-start | bytes 55304 | tf_op jit(solution)/shard_map/ppermute | solution.py:29
  37.1 23.7 %collective-permute-start.3 = (f32[32,4,128]{2,1,0:T(4,128)S(1)}, f32[32,4,128]{2,1,0:T(4,128)S(1)}, u32[]{:S(2)}, u32[]{:S(2)}) collective-permute-start(f32[32,4,128]{2,1,0:T(4,128)S(1)} %get-tuple-element.87), channel_id=1, source_target_pairs={{2,0},{3,1},{4,2},{5,3},{6,4},{7,5},{8,6},{9,7},{10,8},{11,9},{12,... | collective-permute-start | bytes 196616 | tf_op jit(solution)/shard_map/ppermute | solution.py:38
  43.4 17.4 %collective-permute-start.4 = (f32[32,4,128]{2,1,0:T(4,128)S(1)}, f32[32,4,128]{2,1,0:T(4,128)S(1)}, u32[]{:S(2)}, u32[]{:S(2)}) collective-permute-start(f32[32,4,128]{2,1,0:T(4,128)S(1)} %get-tuple-element.88), channel_id=1, source_target_pairs={{0,32},{32,64},{64,96},{96,128},{128,160},{160,192},{192,224},{1,3... | collective-permute-start | bytes 196616 | tf_op jit(solution)/shard_map/ppermute | solution.py:38
  49.6 11.3 %collective-permute-start.5 = (f32[32,4,128]{2,1,0:T(4,128)S(1)}, f32[32,4,128]{2,1,0:T(4,128)S(1)}, u32[]{:S(2)}, u32[]{:S(2)}) collective-permute-start(f32[32,4,128]{2,1,0:T(4,128)S(1)} %get-tuple-element.82), channel_id=1, source_target_pairs={{32,0},{64,32},{96,64},{128,96},{160,128},{192,160},{224,192},{33,... | collective-permute-start | bytes 196616 | tf_op jit(solution)/shard_map/ppermute | solution.py:38
  52.4 476.0 %collective-permute-start.16 = (f32[1,32,256]{2,1,0:T(8,128)}, f32[1,32,256]{2,1,0:T(8,128)S(1)}, u32[]{:S(2)}, u32[]{:S(2)}) collective-permute-start(f32[1,32,256]{2,1,0:T(8,128)} %get-tuple-element.94), channel_id=1, source_target_pairs={{32,0},{64,32},{96,64},{128,96},{160,128},{192,160},{224,192},{33,... | collective-permute-start | bytes 98312 | tf_op jit(solution)/shard_map/ppermute | solution.py:30
  57.1 471.4 %collective-permute-start.17 = (f32[1,32,256]{2,1,0:T(8,128)}, f32[1,32,256]{2,1,0:T(8,128)S(1)}, u32[]{:S(2)}, u32[]{:S(2)}) collective-permute-start(f32[1,32,256]{2,1,0:T(8,128)} %get-tuple-element.93), channel_id=1, source_target_pairs={{0,32},{32,64},{64,96},{96,128},{128,160},{160,192},{192,224},{1,3... | collective-permute-start | bytes 98312 | tf_op jit(solution)/shard_map/ppermute | solution.py:29
  528.5 16.4 %collective-permute-start.18 = (f32[18,1,256]{2,1,0:T(1,128)S(1)}, f32[18,1,256]{2,1,0:T(1,128)S(1)}, u32[]{:S(2)}, u32[]{:S(2)}) collective-permute-start(f32[18,1,256]{2,1,0:T(1,128)S(1)} %get-tuple-element.79), channel_id=1, source_target_pairs={{1,0},{2,1},{3,2},{4,3},{5,4},{6,5},{7,6},{8,7},{9,8},{10,9},{11,1... | collective-permute-start | bytes 55304 | tf_op jit(solution)/shard_map/ppermute | solution.py:30
  531.5 18.5 %collective-permute-start.19 = (f32[18,1,256]{2,1,0:T(1,128)S(1)}, f32[18,1,256]{2,1,0:T(1,128)S(1)}, u32[]{:S(2)}, u32[]{:S(2)}) collective-permute-start(f32[18,1,256]{2,1,0:T(1,128)S(1)} %get-tuple-element.78), channel_id=1, source_target_pairs={{0,1},{1,2},{2,3},{3,4},{4,5},{5,6},{6,7},{7,8},{8,9},{9,10},{10,1... | collective-permute-start | bytes 55304 | tf_op jit(solution)/shard_map/ppermute | solution.py:29
  533.7 21.4 %collective-permute-start.6 = (f32[32,3,128]{2,1,0:T(4,128)S(1)}, f32[32,3,128]{2,1,0:T(4,128)S(1)}, u32[]{:S(2)}, u32[]{:S(2)}) collective-permute-start(f32[32,3,128]{2,1,0:T(4,128)S(1)} %get-tuple-element.102), channel_id=1, source_target_pairs={{1,0},{2,1},{3,2},{4,3},{5,4},{6,5},{7,6},{8,7},{9,8},{10,9},{11,1... | collective-permute-start | bytes 147464 | tf_op jit(solution)/shard_map/ppermute | solution.py:38
  540.7 28.2 %collective-permute-start.7 = (f32[32,3,128]{2,1,0:T(4,128)S(1)}, f32[32,3,128]{2,1,0:T(4,128)S(1)}, u32[]{:S(2)}, u32[]{:S(2)}) collective-permute-start(f32[32,3,128]{2,1,0:T(4,128)S(1)} %get-tuple-element.101), channel_id=1, source_target_pairs={{0,1},{1,2},{2,3},{3,4},{4,5},{5,6},{6,7},{7,8},{8,9},{9,10},{10,1... | collective-permute-start | bytes 147464 | tf_op jit(solution)/shard_map/ppermute | solution.py:38
  542.6 40.2 %collective-permute-start.8 = (f32[32,3,128]{2,1,0:T(4,128)S(1)}, f32[32,3,128]{2,1,0:T(4,128)S(1)}, u32[]{:S(2)}, u32[]{:S(2)}) collective-permute-start(f32[32,3,128]{2,1,0:T(4,128)S(1)} %get-tuple-element.100), channel_id=1, source_target_pairs={{2,0},{3,1},{4,2},{5,3},{6,4},{7,5},{8,6},{9,7},{10,8},{11,9},{12,... | collective-permute-start | bytes 147464 | tf_op jit(solution)/shard_map/ppermute | solution.py:38
  544.9 48.1 %collective-permute-start.9 = (f32[32,3,128]{2,1,0:T(4,128)S(1)}, f32[32,3,128]{2,1,0:T(4,128)S(1)}, u32[]{:S(2)}, u32[]{:S(2)}) collective-permute-start(f32[32,3,128]{2,1,0:T(4,128)S(1)} %get-tuple-element.99), channel_id=1, source_target_pairs={{0,2},{1,3},{2,4},{3,5},{4,6},{5,7},{6,8},{7,9},{8,10},{9,11},{10,... | collective-permute-start | bytes 147464 | tf_op jit(solution)/shard_map/ppermute | solution.py:38
  551.9 6.8 collective-permute-start.20
  555.1 5.9 collective-permute-start.21
  558.7 49.7 %collective-permute-start.10 = (f32[32,3,128]{2,1,0:T(4,128)S(1)}, f32[32,3,128]{2,1,0:T(4,128)S(1)}, u32[]{:S(2)}, u32[]{:S(2)}) collective-permute-start(f32[32,3,128]{2,1,0:T(4,128)S(1)} %get-tuple-element.98), channel_id=1, source_target_pairs={{32,0},{64,32},{96,64},{128,96},{160,128},{192,160},{224,192},{33,... | collective-permute-start | bytes 147464 | tf_op jit(solution)/shard_map/ppermute | solution.py:38
  561.0 9.8 %collective-permute-start.22 = (f32[18,1,256]{2,1,0:T(1,128)S(1)}, f32[18,1,256]{2,1,0:T(1,128)S(1)}, u32[]{:S(2)}, u32[]{:S(2)}) collective-permute-start(f32[18,1,256]{2,1,0:T(1,128)S(1)} %get-tuple-element.77), channel_id=1, source_target_pairs={{1,0},{2,1},{3,2},{4,3},{5,4},{6,5},{7,6},{8,7},{9,8},{10,9},{11,1... | collective-permute-start | bytes 55304 | tf_op jit(solution)/shard_map/ppermute | solution.py:30
  568.9 8.7 %collective-permute-start.23 = (f32[18,1,256]{2,1,0:T(1,128)S(1)}, f32[18,1,256]{2,1,0:T(1,128)S(1)}, u32[]{:S(2)}, u32[]{:S(2)}) collective-permute-start(f32[18,1,256]{2,1,0:T(1,128)S(1)} %get-tuple-element.76), channel_id=1, source_target_pairs={{0,1},{1,2},{2,3},{3,4},{4,5},{5,6},{6,7},{7,8},{8,9},{9,10},{10,1... | collective-permute-start | bytes 55304 | tf_op jit(solution)/shard_map/ppermute | solution.py:29
  570.9 51.9 %collective-permute-start.11 = (f32[32,3,128]{2,1,0:T(4,128)S(1)}, f32[32,3,128]{2,1,0:T(4,128)S(1)}, u32[]{:S(2)}, u32[]{:S(2)}) collective-permute-start(f32[32,3,128]{2,1,0:T(4,128)S(1)} %get-tuple-element.97), channel_id=1, source_target_pairs={{0,32},{32,64},{64,96},{96,128},{128,160},{160,192},{192,224},{1,3... | collective-permute-start | bytes 147464 | tf_op jit(solution)/shard_map/ppermute | solution.py:38
  578.6 7.4 %collective-permute-start.24 = (f32[1,32,256]{2,1,0:T(8,128)S(1)}, f32[1,32,256]{2,1,0:T(8,128)S(1)}, u32[]{:S(2)}, u32[]{:S(2)}) collective-permute-start(f32[1,32,256]{2,1,0:T(8,128)S(1)} %get-tuple-element.90), channel_id=1, source_target_pairs={{32,0},{64,32},{96,64},{128,96},{160,128},{192,160},{224,192},{33,... | collective-permute-start | bytes 98312 | tf_op jit(solution)/shard_map/ppermute | solution.py:30
  582.9 5.8 collective-permute-start.25
  588.7 4.4 collective-permute-start.26
  590.7 8.7 %collective-permute-start.27 = (f32[18,1,256]{2,1,0:T(1,128)S(1)}, f32[18,1,256]{2,1,0:T(1,128)S(1)}, u32[]{:S(2)}, u32[]{:S(2)}) collective-permute-start(f32[18,1,256]{2,1,0:T(1,128)S(1)} %get-tuple-element.74), channel_id=1, source_target_pairs={{0,1},{1,2},{2,3},{3,4},{4,5},{5,6},{6,7},{7,8},{8,9},{9,10},{10,1... | collective-permute-start | bytes 55304 | tf_op jit(solution)/shard_map/ppermute | solution.py:29
  601.0 7.4 %collective-permute-start.28 = (f32[2,1,32,256]{3,2,1,0:T(8,128)S(1)}, f32[2,1,32,256]{3,2,1,0:T(8,128)S(1)}, u32[]{:S(2)}, u32[]{:S(2)}) collective-permute-start(f32[2,1,32,256]{3,2,1,0:T(8,128)S(1)} %get-tuple-element.72), channel_id=1, source_target_pairs={{0,32},{32,64},{64,96},{96,128},{128,160},{160,192},{192,224},{1,3... | collective-permute-start | bytes 196616 | tf_op jit(solution)/shard_map/ppermute | solution.py:29
  606.5 7.1 %collective-permute-start.29 = (f32[2,1,32,256]{3,2,1,0:T(8,128)S(1)}, f32[2,1,32,256]{3,2,1,0:T(8,128)S(1)}, u32[]{:S(2)}, u32[]{:S(2)}) collective-permute-start(f32[2,1,32,256]{3,2,1,0:T(8,128)S(1)} %get-tuple-element.73), channel_id=1, source_target_pairs={{32,0},{64,32},{96,64},{128,96},{160,128},{192,160},{224,192},{33,... | collective-permute-start | bytes 196616 | tf_op jit(solution)/shard_map/ppermute | solution.py:30
  613.6 17.5 %collective-permute-start.30 = (f32[2,18,1,256]{3,2,1,0:T(1,128)S(1)}, f32[2,18,1,256]{3,2,1,0:T(1,128)S(1)}, u32[]{:S(2)}, u32[]{:S(2)}) collective-permute-start(f32[2,18,1,256]{3,2,1,0:T(1,128)S(1)} %get-tuple-element.67), channel_id=1, source_target_pairs={{0,1},{1,2},{2,3},{3,4},{4,5},{5,6},{6,7},{7,8},{8,9},{9,10},{10,1... | collective-permute-start | bytes 110600 | tf_op jit(solution)/shard_map/ppermute | solution.py:29
  615.5 15.6 %collective-permute-start.31 = (f32[2,18,1,256]{3,2,1,0:T(1,128)S(1)}, f32[2,18,1,256]{3,2,1,0:T(1,128)S(1)}, u32[]{:S(2)}, u32[]{:S(2)}) collective-permute-start(f32[2,18,1,256]{3,2,1,0:T(1,128)S(1)} %get-tuple-element.68), channel_id=1, source_target_pairs={{1,0},{2,1},{3,2},{4,3},{5,4},{6,5},{7,6},{8,7},{9,8},{10,9},{11,1... | collective-permute-start | bytes 110600 | tf_op jit(solution)/shard_map/ppermute | solution.py:30
  (25 other events, 774.4 us)
where the time goes:
time: 686 us; the launch traced here: 681 us
  other arithmetic  394 us (57%)
  local copies, waits for them, and re-layouts  151 us (22%)
  starting transfers between devices  116 us (17%)
  waiting for transfers between devices  15.6 us (2%)
    reduce_sum x32, other arithmetic, tile_forces(): return (jnp.sum(pull, axis=3), jnp.sum(pull, axis=2))  128 us
    reduce_sum x32, other arithmetic, tile_forces(): dist = jnp.sum(diff * diff, axis=1) + softening  66 us
    gather x32, local copies, waits for them, and re-layouts, visit(): own = cluster_data[own_rows]  52.9 us
    scatter-add x32, other arithmetic, visit(): react.at[other_rows].add(-pull_other)  52.5 us
    scatter-add x32, other arithmetic, visit(): own_force.at[own_rows].add(pull_own)  52.5 us
    gather x32, local copies, waits for them, and re-layouts, visit(): other = arrived[other_rows]  52.1 us
    ppermute x12, starting transfers between devices, passed_along(): return lax.ppermute(shard, axis, pairs)  47.6 us
    ppermute x10, starting transfers between devices, extended(): after = lax.ppermute(initial, axis, down)  39.3 us
  transfers between devices with their start and end apart: 32, of which 4 were waited for; matrix products, arithmetic and copies ran while one was open for 73% of the time, Pallas kernels for 0%

commit v1 on v0

v1 whole, which is shorter than its diff:
```python
import functools

import jax
import jax.numpy as jnp
from jax import lax
from jax.experimental import pallas as pl
from jax.experimental.pallas import tpu as pltpu
from jax.sharding import PartitionSpec as P

F32, BF16, I32 = jnp.float32, jnp.bfloat16, jnp.int32
SWEEPS = 4
ROUNDS = SWEEPS + 1
coulomb_scale = 0.02
softening = 0.1
field_scale = 0.5
deposit_scale = 0.2
lowest_eig = 0.01
highest_eig = 1.99
mobility = 0.3
diffusion = 0.2
time_step = 0.2
OFFSETS = ((0, 0), (0, -1), (0, 1), (0, -2), (0, 2), (-1, 0), (1, 0))
MESH = pl.DeviceIdType.MESH
PAIRS_AT_ONCE = 8
GROUPS = 2
TOP = 8


def split3(v):
    high = v.astype(BF16).astype(F32)
    rest = v - high
    mid = rest.astype(BF16).astype(F32)
    return high, mid, (rest - mid).astype(BF16).astype(F32)


def dot(a, b, dims=((1,), (0,))):
    return lax.dot_general(a, b, (dims, ((), ())), preferred_element_type=F32)


def select_rows(chooser, data, dims=((1,), (0,)), parts=3):
    pieces = split3(data)[:parts]
    total = dot(chooser, pieces[0].astype(BF16), dims)
    for piece in pieces[1:]:
        total = total + dot(chooser, piece.astype(BF16), dims)
    return total


def neighbour(step_g, step_b, groups, bricks):
    g = lax.axis_index("grp")
    b = lax.axis_index("brick")
    return (lax.rem(g + step_g + groups, groups), lax.rem(b + step_b + bricks, bricks))


def greet(groups, bricks):
    barrier = pltpu.get_barrier_semaphore()
    for step in OFFSETS[1:]:
        pl.semaphore_signal(
            barrier, inc=1, device_id=neighbour(*step, groups, bricks), device_id_type=MESH
        )
    return barrier


def slot_row(index_ref):
    return jnp.concatenate([index_ref[k : k + 1, :] for k in range(index_ref.shape[0])], axis=1)


def column(row):
    return jnp.transpose(jnp.broadcast_to(row, (128, 128)))


def columns(values):
    vals = values.astype(F32)
    return jnp.concatenate([column(vals[i : i + 1, :]) for i in range(vals.shape[0])], axis=0)


def neighbours_sum(pad, i):
    rows = pad.shape[1] - 16
    centre = pad[i + 1, TOP : TOP + rows, :]
    total = pad[i + 2, TOP : TOP + rows, :] + pad[i, TOP : TOP + rows, :]
    total = total + pad[i + 1, TOP + 1 : TOP + rows + 1, :] + pad[i + 1, TOP - 1 : TOP + rows - 1, :]
    above, below = z_shifts(centre)
    return centre, total + above + below


def z_shifts(v):
    depth = v.shape[1]
    lane = lax.broadcasted_iota(I32, v.shape, 1)
    above = jnp.where(lane == depth - 1, 0.0, pltpu.roll(v, depth - 1, 1))
    below = jnp.where(lane == 0, 0.0, pltpu.roll(v, 1, 1))
    return above, below


def face_flux(pot_low, pot_high, ion_low, ion_high):
    speed = -mobility * (pot_high - pot_low)
    return (
        jnp.maximum(speed, 0.0) * ion_low
        + jnp.minimum(speed, 0.0) * ion_high
        - diffusion * (ion_high - ion_low)
    )


def field_kernel(
    groups,
    bricks,
    count_ref,
    pos_ref,
    charge_ref,
    fill_ref,
    cell_ref,
    index_ref,
    ion_ref,
    prev_ref,
    screen_ref,
    data_ref,
    arrived_ref,
    push_ref,
    pot_ref,
    next_ref,
    out_rows,
    in_rows,
    x_in,
    y_out,
    y_in,
    x_first,
    ion_pad,
    pad,
    resid,
    efield,
    row_send,
    row_recv,
    halo_send,
    halo_recv,
):
    clusters = charge_ref.shape[0]
    nx, ny, nz = ion_ref.shape
    g = lax.axis_index("grp")
    b = lax.axis_index("brick")
    barrier = greet(groups, bricks)

    fill_col = columns(fill_ref[...])
    lane = lax.broadcasted_iota(I32, (clusters, 128), 1).astype(F32)
    charge = charge_ref[...] * jnp.where(lane < fill_col, 1.0, 0.0)
    for d in range(3):
        data_ref[:, d * 128 : (d + 1) * 128] = pos_ref[:, d, :]
    data_ref[:, 384:512] = charge
    slots = index_ref.shape[1]
    wanted = slot_row(index_ref)
    total_slots = wanted.shape[1]
    chooser = jnp.where(
        lax.broadcasted_iota(I32, (clusters, total_slots), 0) == wanted, 1.0, 0.0
    ).astype(BF16)
    out_rows[...] = select_rows(chooser, data_ref[...], ((0,), (0,)))
    slot_id = lax.broadcasted_iota(I32, (slots, 128), 0)
    for k in range(len(OFFSETS)):
        live = jnp.where(slot_id < count_ref[0, k], 1.0, 0.0)
        out_rows[k * slots : (k + 1) * slots, 384:512] = (
            out_rows[k * slots : (k + 1) * slots, 384:512] * live
        )
    for i in range(nx):
        pad[0, i + 1, TOP : TOP + ny, :] = prev_ref[i]
        ion_pad[i + 1, TOP : TOP + ny, :] = ion_ref[i]
    y_out[0, 0, 0] = prev_ref[:, 0, :]
    y_out[0, 1, 0] = prev_ref[:, ny - 1, :]
    y_out[0, 0, 1] = ion_ref[:, 0, :]
    y_out[0, 1, 1] = ion_ref[:, ny - 1, :]
    for f, ref in enumerate((prev_ref, ion_ref)):
        x_first[0, f] = ref[0]
        x_first[1, f] = ref[nx - 1]
    pl.semaphore_wait(barrier, len(OFFSETS) - 1)

    def halo_copies(turn):
        held = turn % 2
        copies = []
        for side in range(2):
            step = 2 * side - 1
            if turn == 0:
                src, dst = x_first.at[side], x_in.at[0, 1 - side]
                ysrc, ydst = y_out.at[0, side], y_in.at[0, 1 - side]
            else:
                src = pad.at[held, 1 if side == 0 else nx, pl.ds(TOP, ny), :]
                dst = x_in.at[turn, 1 - side, 0]
                ysrc, ydst = y_out.at[turn, side, 0], y_in.at[turn, 1 - side, 0]
            copies.append(
                pltpu.make_async_remote_copy(
                    src_ref=src,
                    dst_ref=dst,
                    send_sem=halo_send.at[turn, side],
                    recv_sem=halo_recv.at[turn, 1 - side],
                    device_id=neighbour(step, 0, groups, bricks),
                    device_id_type=MESH,
                )
            )
            copies.append(
                pltpu.make_async_remote_copy(
                    src_ref=ysrc,
                    dst_ref=ydst,
                    send_sem=halo_send.at[turn, 2 + side],
                    recv_sem=halo_recv.at[turn, 3 - side],
                    device_id=neighbour(0, step, groups, bricks),
                    device_id_type=MESH,
                )
            )
        return copies

    def start_halos(turn):
        held = turn % 2
        if turn:
            y_out[turn, 0, 0] = pad[held, 1 : nx + 1, TOP, :]
            y_out[turn, 1, 0] = pad[held, 1 : nx + 1, TOP + ny - 1, :]
        copies = halo_copies(turn)
        for copy in copies:
            copy.start()
        return copies

    inside = (
        jnp.where(g > 0, 1.0, 0.0),
        jnp.where(g < groups - 1, 1.0, 0.0),
        jnp.where(b > 0, 1.0, 0.0),
        jnp.where(b < bricks - 1, 1.0, 0.0),
    )

    def place(target, turn, field):
        target[0, TOP : TOP + ny, :] = x_in[turn, 0, field] * inside[0]
        target[nx + 1, TOP : TOP + ny, :] = x_in[turn, 1, field] * inside[1]
        target[1 : nx + 1, TOP - 1, :] = y_in[turn, 0, field] * inside[2]
        target[1 : nx + 1, TOP + ny, :] = y_in[turn, 1, field] * inside[3]

    halos = start_halos(0)
    sends = []
    for k in range(1, len(OFFSETS)):
        step_g, step_b = OFFSETS[k]
        copy = pltpu.make_async_remote_copy(
            src_ref=out_rows.at[pl.ds(k * slots, slots), :],
            dst_ref=in_rows.at[pl.ds((k - 1) * slots, slots), :],
            send_sem=row_send.at[k - 1],
            recv_sem=row_recv.at[k - 1],
            device_id=neighbour(-step_g, -step_b, groups, bricks),
            device_id_type=MESH,
        )
        copy.start()
        sends.append(copy)

    cell = cell_ref[...]
    row_of = cell // nz
    row_line = jnp.concatenate([row_of[i : i + 1, :] for i in range(row_of.shape[0])], axis=1)
    into = jnp.where(
        lax.broadcasted_iota(I32, (nx * ny, clusters), 0) == row_line, 1.0, 0.0
    ).astype(BF16)
    k_col = columns(cell - row_of * nz)
    k_col = jnp.concatenate([k_col, k_col], axis=1)
    at_depth = jnp.where(
        lax.broadcasted_iota(I32, (clusters, nz), 1).astype(F32) == k_col, 1.0, 0.0
    )
    deposit = select_rows(into, at_depth * jnp.sum(charge, axis=1, keepdims=True))
    resid[...] = ion_ref[...] + deposit_scale * deposit.reshape(nx, ny, nz)

    middle = 0.5 * (highest_eig + lowest_eig)
    spread = 0.5 * (highest_eig - lowest_eig)
    ratio_ms = middle / spread
    weight_now = 1.0 / ratio_ms
    for copy in halos:
        copy.wait()
    place(pad.at[0], 0, 0)
    place(ion_pad, 0, 1)

    def first(i, carry):
        centre, around = neighbours_sum(pad.at[0], i)
        diag = 6.0 + screen_ref[i]
        rest = resid[i] - (diag * centre - around)
        resid[i] = rest
        update = rest / diag / middle
        pad[1, i + 1, TOP : TOP + ny, :] = update
        pot_ref[i] = centre + update
        return carry

    lax.fori_loop(0, nx, first, 0, unroll=2)
    for turn in range(1, SWEEPS):
        halos = start_halos(turn)
        weight_next = 1.0 / (2.0 * ratio_ms - weight_now)
        last = turn == SWEEPS - 1
        for copy in halos:
            copy.wait()
        held = turn % 2
        place(pad.at[held], turn, 0)

        def sweep(i, carry, held=held, weight_next=weight_next, weight_now=weight_now, last=last):
            centre, around = neighbours_sum(pad.at[held], i)
            diag = 6.0 + screen_ref[i]
            rest = resid[i] - (diag * centre - around)
            resid[i] = rest
            update = weight_next * weight_now * centre + 2.0 * weight_next / spread * (rest / diag)
            done = pot_ref[i] + update
            pot_ref[i] = done
            pad[1 - held, i + 1, TOP : TOP + ny, :] = done if last else update
            return carry

        lax.fori_loop(0, nx, sweep, 0, unroll=2)
        weight_now = weight_next
    halos = start_halos(SWEEPS)
    for copy in halos:
        copy.wait()
    pot = pad.at[SWEEPS % 2]
    place(pot, SWEEPS, 0)

    def finish(i, carry):
        lo, hi = TOP, TOP + ny
        p, n = pot[i + 1, lo:hi, :], ion_pad[i + 1, lo:hi, :]
        px = (pot[i, lo:hi, :], pot[i + 2, lo:hi, :])
        py = (pot[i + 1, lo - 1 : hi - 1, :], pot[i + 1, lo + 1 : hi + 1, :])
        ix = (ion_pad[i, lo:hi, :], ion_pad[i + 2, lo:hi, :])
        iy = (ion_pad[i + 1, lo - 1 : hi - 1, :], ion_pad[i + 1, lo + 1 : hi + 1, :])
        pz = z_shifts(p)[::-1]
        iz = z_shifts(n)[::-1]
        out = jnp.zeros_like(p)
        for d, (ps, ns) in enumerate(((px, ix), (py, iy), (pz, iz))):
            out = out + (face_flux(p, ps[1], n, ns[1]) - face_flux(ps[0], p, ns[0], n))
            efield[d, pl.ds(pl.multiple_of(i * ny, ny), ny), :] = -(ps[1] - ps[0]) * 0.5
        next_ref[i] = n - time_step * out
        return carry

    lax.fori_loop(0, nx, finish, 0)
    for d in range(3):
        seen = select_rows(into, efield[d], ((0,), (0,)))
        here = jnp.sum(seen * at_depth, axis=1, keepdims=True)
        push_ref[:, d * 128 : (d + 1) * 128] = field_scale * data_ref[:, 384:512] * here
    for copy in sends:
        copy.wait()
    arrived_ref[0:slots, :] = out_rows[0:slots, :]
    arrived_ref[slots:, :] = in_rows[...]


def features(data_ref, feat, vals, own):
    spots = [data_ref[:, d * 128 : (d + 1) * 128] for d in range(3)]
    charge = data_ref[:, 384:512]
    square = jnp.zeros_like(charge)
    for d in range(3):
        high, mid, low = split3(spots[d])
        rows = (high, high, mid, mid, high, low) if own else (high, mid, high, mid, low, high)
        for f, row in enumerate(rows):
            feat[:, 6 * d + f, :] = -2.0 * row if own else row
        square = square + spots[d] * spots[d]
    if own:
        square = square + softening
    one = jnp.ones_like(square)
    for f, row in enumerate(split3(square)):
        feat[:, (18 if own else 21) + f, :] = row
        feat[:, (21 if own else 18) + f, :] = one
    for c, val in enumerate((charge, charge * spots[0], charge * spots[1], charge * spots[2])):
        for f, row in enumerate(split3(val)):
            vals[:, 4 * f + c, :] = row
    for f in range(12, 16):
        vals[:, f, :] = jnp.zeros_like(charge)


def tile_sums(own_ids, part_ids, own_feat, own_vals, part_feat, part_vals):
    left = jnp.concatenate([own_feat[o] for o in own_ids], axis=0).astype(BF16)
    blank = jnp.zeros((24, 128), F32)
    count = len(own_ids)
    right = jnp.concatenate(
        [
            jnp.concatenate([part_feat[r] if i == j else blank for i in range(count)], axis=0).astype(BF16)
            for j, r in enumerate(part_ids)
        ],
        axis=1,
    )
    dist = dot(left, right, ((0,), (0,)))
    sums = []
    for j in range(count):
        root = lax.rsqrt(dist[:, j * 128 : (j + 1) * 128])
        u = root * root * root
        high = u.astype(BF16)
        low = (u - high.astype(F32)).astype(BF16)
        mine = own_vals[own_ids[j]].astype(BF16)
        theirs = part_vals[part_ids[j]].astype(BF16)
        on_part = dot(jnp.concatenate([mine, mine], axis=1), jnp.concatenate([high, low], axis=0))
        on_own = dot(
            jnp.concatenate([theirs, theirs], axis=1),
            jnp.concatenate([high, low], axis=1),
            ((1,), (1,)),
        )
        sums.append((on_own, on_part))
    return sums


def pair_kernel(
    local_ref,
    dir_ref,
    slot_ref,
    data_ref,
    arrived_ref,
    own_ref,
    part_ref,
    own_feat,
    own_vals,
    part_feat,
    part_vals,
    own_acc,
    part_acc,
):
    features(data_ref, own_feat, own_vals, True)
    features(arrived_ref, part_feat, part_vals, False)
    own_acc[...] = jnp.zeros_like(own_acc)
    part_acc[...] = jnp.zeros_like(part_acc)
    slots = arrived_ref.shape[0] // len(OFFSETS)
    step = PAIRS_AT_ONCE * GROUPS

    @pl.loop(0, local_ref.shape[0] // step)
    def _(turn):
        done = []
        for group in range(GROUPS):
            base = turn * step + group * PAIRS_AT_ONCE
            own_ids = [local_ref[base + j] for j in range(PAIRS_AT_ONCE)]
            part_ids = [
                dir_ref[base + j] * slots + slot_ref[base + j] for j in range(PAIRS_AT_ONCE)
            ]
            done.append(
                (own_ids, part_ids, tile_sums(own_ids, part_ids, own_feat, own_vals, part_feat, part_vals))
            )
        for own_ids, part_ids, sums in done:
            for j, (on_own, on_part) in enumerate(sums):
                own_acc[own_ids[j]] += on_own
                part_acc[part_ids[j]] += on_part

    for acc, out in ((own_acc, own_ref), (part_acc, part_ref)):
        for c in range(4):
            out[:, c * 128 : (c + 1) * 128] = acc[:, c, :] + (acc[:, 4 + c, :] + acc[:, 8 + c, :])


def return_kernel(
    groups,
    bricks,
    count_ref,
    index_ref,
    data_ref,
    own_ref,
    part_ref,
    push_ref,
    out_ref,
    back,
    row_send,
    row_recv,
):
    clusters = data_ref.shape[0]
    slots = index_ref.shape[1]
    barrier = greet(groups, bricks)
    pl.semaphore_wait(barrier, len(OFFSETS) - 1)
    copies = []
    for k in range(1, len(OFFSETS)):
        copy = pltpu.make_async_remote_copy(
            src_ref=part_ref.at[pl.ds(k * slots, slots), :],
            dst_ref=back.at[pl.ds(k * slots, slots), :],
            send_sem=row_send.at[k - 1],
            recv_sem=row_recv.at[k - 1],
            device_id=neighbour(*OFFSETS[k], groups, bricks),
            device_id_type=MESH,
        )
        copy.start()
        copies.append(copy)
    back[0:slots, :] = part_ref[0:slots, :]
    wanted = slot_row(index_ref)
    total_slots = wanted.shape[1]
    spot = lax.broadcasted_iota(I32, (1, slots), 1)
    live = jnp.concatenate(
        [jnp.where(spot < count_ref[0, k], 1.0, 0.0) for k in range(len(OFFSETS))], axis=1
    )
    chooser = jnp.where(
        lax.broadcasted_iota(I32, (clusters, total_slots), 0) == wanted,
        jnp.broadcast_to(live, (clusters, total_slots)),
        0.0,
    ).astype(BF16)
    for copy in copies:
        copy.wait()
    sums = own_ref[...] + select_rows(chooser, back[...])
    charge = coulomb_scale * data_ref[:, 384:512]
    for d in range(3):
        pull = data_ref[:, d * 128 : (d + 1) * 128] * sums[:, 0:128] - sums[:, (d + 1) * 128 : (d + 2) * 128]
        out_ref[:, d, :] = charge * pull + push_ref[:, d * 128 : (d + 1) * 128]


def shards(
    groups,
    bricks,
    positions,
    charges,
    cluster_fill,
    cluster_cell,
    send_index,
    send_count,
    pair_local,
    pair_dir,
    pair_slot,
    ion_density,
    potential_prev,
    screening,
):
    clusters = cluster_fill.shape[0]
    psize = charges.shape[0] // clusters
    dirs, slots = send_index.shape
    nx, ny, nz = ion_density.shape
    placed = positions.reshape(3, clusters, psize).transpose(1, 0, 2)
    vmem = pl.BlockSpec(memory_space=pltpu.VMEM)
    smem = pl.BlockSpec(memory_space=pltpu.SMEM)
    shape = lambda *dims: jax.ShapeDtypeStruct(dims, F32)
    data, arrived, push, potential, ion_next = pl.pallas_call(
        functools.partial(field_kernel, groups, bricks),
        out_shape=(
            shape(clusters, 4 * psize),
            shape(dirs * slots, 4 * psize),
            shape(clusters, 3 * psize),
            shape(nx, ny, nz),
            shape(nx, ny, nz),
        ),
        in_specs=[smem] + [vmem] * 8,
        out_specs=[vmem] * 5,
        scratch_shapes=[
            pltpu.VMEM((dirs * slots, 4 * psize), F32),
            pltpu.VMEM(((dirs - 1) * slots, 4 * psize), F32),
            pltpu.VMEM((ROUNDS, 2, 2, ny, nz), F32),
            pltpu.VMEM((ROUNDS, 2, 2, nx, nz), F32),
            pltpu.VMEM((ROUNDS, 2, 2, nx, nz), F32),
            pltpu.VMEM((2, 2, ny, nz), F32),
            pltpu.VMEM((nx + 2, ny + 16, nz), F32),
            pltpu.VMEM((2, nx + 2, ny + 16, nz), F32),
            pltpu.VMEM((nx, ny, nz), F32),
            pltpu.VMEM((3, nx * ny, nz), F32),
            pltpu.SemaphoreType.DMA((dirs - 1,)),
            pltpu.SemaphoreType.DMA((dirs - 1,)),
            pltpu.SemaphoreType.DMA((ROUNDS, 4)),
            pltpu.SemaphoreType.DMA((ROUNDS, 4)),
        ],
        compiler_params=pltpu.CompilerParams(
            collective_id=0, has_side_effects=True, vmem_limit_bytes=48 << 20
        ),
        name="field",
    )(
        send_count,
        placed,
        charges.reshape(clusters, psize),
        cluster_fill.reshape(clusters // 128, 128),
        cluster_cell.reshape(clusters // 128, 128),
        send_index,
        ion_density,
        potential_prev,
        screening,
    )
    own_sums, part_sums = pl.pallas_call(
        pair_kernel,
        out_shape=(shape(clusters, 4 * psize), shape(dirs * slots, 4 * psize)),
        in_specs=[smem] * 3 + [vmem] * 2,
        out_specs=[vmem] * 2,
        scratch_shapes=[
            pltpu.VMEM((clusters, 24, psize), F32),
            pltpu.VMEM((clusters, 16, psize), F32),
            pltpu.VMEM((dirs * slots, 24, psize), F32),
            pltpu.VMEM((dirs * slots, 16, psize), F32),
            pltpu.VMEM((clusters, 16, psize), F32),
            pltpu.VMEM((dirs * slots, 16, psize), F32),
        ],
        compiler_params=pltpu.CompilerParams(vmem_limit_bytes=48 << 20),
        name="pairs",
    )(pair_local, pair_dir, pair_slot, data, arrived)
    forces = pl.pallas_call(
        functools.partial(return_kernel, groups, bricks),
        out_shape=shape(clusters, 3, psize),
        in_specs=[smem] + [vmem] * 5,
        out_specs=vmem,
        scratch_shapes=[
            pltpu.VMEM((dirs * slots, 4 * psize), F32),
            pltpu.SemaphoreType.DMA((dirs - 1,)),
            pltpu.SemaphoreType.DMA((dirs - 1,)),
        ],
        compiler_params=pltpu.CompilerParams(
            collective_id=1, has_side_effects=True, vmem_limit_bytes=48 << 20
        ),
        name="forces",
    )(send_count, send_index, data, own_sums, part_sums, push)
    return (forces.transpose(1, 0, 2).reshape(3, -1), potential, ion_next)


def solution(mesh):
    in_specs = (
        P(None, ("grp", "brick")),
        P(("grp", "brick")),
        P(("grp", "brick")),
        P(("grp", "brick")),
        P(("grp", "brick"), None),
        P(("grp", "brick"), None),
        P(("grp", "brick")),
        P(("grp", "brick")),
        P(("grp", "brick")),
        P("grp", "brick", None),
        P("grp", "brick", None),
        P("grp", "brick", None),
    )
    out_specs = (P(None, ("grp", "brick")), P("grp", "brick", None), P("grp", "brick", None))
    body = functools.partial(shards, mesh.shape["grp"], mesh.shape["brick"])
    return jax.shard_map(body, mesh=mesh, in_specs=in_specs, out_specs=out_specs, check_vma=False)
```

time: 686 us -> 131 us (0.19)
  the two profiles are of different devices: /device:TPU:138 before, /device:TPU:1 now
where the time goes in v1:
time: 131 us; the launch traced here: 130 us
  Pallas kernels  121 us (92%)
  local copies, waits for them, and re-layouts  8.83 us (7%)
    pallas_call x1, Pallas kernels, shards(): pl.pallas_call(pair_kernel, out_shape=(shape(clusters, 4 * psize), shape(...  65.6 us
    pallas_call x1, Pallas kernels, shards(): pl.pallas_call(functools.partial(field_kernel, groups, bricks), out_shape...  41.9 us
    pallas_call x1, Pallas kernels, shards(): pl.pallas_call(functools.partial(return_kernel, groups, bricks), out_shap...  13.4 us
    unnamed x27, local copies, waits for them, and re-layouts  8.83 us

profile of v1, /device:TPU:1, one launch (start us, length us, event | category | flops | bytes accessed | tf_op | source)
XLA Modules:
  0.0 130.4 jit_solution(7167463445117879000)
XLA Ops:
  0.6 0.0 copy-start.5
  0.6 0.0 copy-start.11
  0.7 0.0 copy-start.9
  0.7 0.0 copy-start.10
  0.7 0.6 copy-done.5
  1.3 0.0 copy-done.11
  1.3 0.0 copy-done.9
  1.3 0.0 copy-done.10
  1.4 0.0 copy-start
  1.4 1.0 copy-done
  2.4 0.0 copy-start.1
  2.4 1.0 copy-done.1
  3.4 0.0 copy-start.2
  3.4 1.0 copy-done.2
  4.5 0.0 copy-start.3
  4.5 1.0 copy-done.3
  5.5 0.0 copy-start.4
  5.5 0.9 copy-done.4
  6.4 0.0 copy-start.8
  6.4 41.9 %field.1 = (f32[256,512]{1,0:T(8,128)S(1)}, f32[224,512]{1,0:T(8,128)S(1)}, f32[256,384]{1,0:T(8,128)S(1)}, f32[16,32,256]{2,1,0:T(8,128)S(1)}, f32[16,32,256]{2,1,0:T(8,128)S(1)}) custom-call(s32[1,7]{1,0:T(1,128)S(1)} %copy-done.9, f32[256,3,128]{2,1,0:T(4,128)S(1)} %bitcast.10, f32[256,128]{1,0:T(8,128)S(1)} %bitcast.11, s32[2,128]{1,0:T(2,128)S(1)} %bitcast.12, ...), custom_call_target="tpu_custom_call" | custom-call | tf_op jit(solution)/shard_map/field/pallas_call | solution.py:504
  48.3 0.0 copy-start.7
  48.3 0.0 copy-start.6
  48.3 0.0 copy-done.8
  48.3 0.7 copy-done.7
  49.0 0.0 copy-done.6
  49.0 65.6 %pairs.1 = (f32[256,512]{1,0:T(8,128)S(1)}, f32[224,512]{1,0:T(8,128)S(1)}) custom-call(s32[1024]{0:T(1024)S(1)} %copy-done.6, s32[1024]{0:T(1024)S(1)} %copy-done.7, s32[1024]{0:T(1024)S(1)} %copy-done.8, f32[256,512]{1,0:T(8,128)S(1)} %get-tuple-element.10.data_ref, f32[224,512]{1,0:T(8,128)S(1)} %get-tuple-element.11.arrived_ref), custom_call_target="tpu_custom_call" | custom-call | tf_op jit(solution)/shard_map/pairs/pallas_call | solution.py:546
  114.6 13.4 %forces.1 = f32[256,3,128]{2,1,0:T(4,128)S(1)} custom-call(s32[1,7]{1,0:T(1,128)S(1)} %copy-done.9, s32[7,32]{1,0:T(8,128)S(1)} %copy-done.5, f32[256,512]{1,0:T(8,128)S(1)} %get-tuple-element.10.data_ref, f32[256,512]{1,0:T(8,128)S(1)} %get-tuple-element.12.own_ref, f32[224,512]{1,0:T(8,128)S(1)} %get-tuple-element.13.part_ref, ...), custom_call_target="tpu_custom_call" | custom-call | tf_op jit(solution)/shard_map/forces/pallas_call | solution.py:562
  128.0 0.8 copy.18
  128.8 0.8 copy.19
  129.6 0.8 copy.20
Async XLA Ops:
  0.6 0.7 copy-start.5
  0.6 0.7 copy-start.11
  0.7 0.7 copy-start.9
  0.7 0.7 copy-start.10
  1.4 1.0 copy-start
  2.4 1.0 copy-start.1
  3.4 1.0 copy-start.2
  4.5 1.0 copy-start.3
  5.5 0.9 copy-start.4
  6.4 41.9 %copy-start.8 = (s32[1024]{0:T(1024)S(1)}, s32[1024]{0:T(1024)}, u32[]{:S(2)}) copy-start(s32[1024]{0:T(1024)} %slot_ref.1) | copy-start | bytes 12292
  48.3 0.7 copy-start.7
  48.3 0.7 copy-start.6

commit v2 on v1

v2 whole, which is shorter than its diff:
```python
import functools

import jax
import jax.numpy as jnp
from jax import lax
from jax.experimental import pallas as pl
from jax.experimental.pallas import tpu as pltpu
from jax.sharding import PartitionSpec as P

F32, BF16, I32 = jnp.float32, jnp.bfloat16, jnp.int32
SWEEPS = 4
EARLY = 3
coulomb_scale = 0.02
softening = 0.1
field_scale = 0.5
deposit_scale = 0.2
lowest_eig = 0.01
highest_eig = 1.99
mobility = 0.3
diffusion = 0.2
time_step = 0.2
OFFSETS = ((0, 0), (0, -1), (0, 1), (0, -2), (0, 2), (-1, 0), (1, 0))
MESH = pl.DeviceIdType.MESH
PAIRS_AT_ONCE = 8
GROUPS = 4
TOP = 8


def split3(v):
    high = v.astype(BF16).astype(F32)
    rest = v - high
    mid = rest.astype(BF16).astype(F32)
    return high, mid, (rest - mid).astype(BF16).astype(F32)


def dot(a, b, dims=((1,), (0,))):
    return lax.dot_general(a, b, (dims, ((), ())), preferred_element_type=F32)


def select_rows(chooser, data, dims=((1,), (0,)), parts=3):
    pieces = split3(data)[:parts]
    total = dot(chooser, pieces[0].astype(BF16), dims)
    for piece in pieces[1:]:
        total = total + dot(chooser, piece.astype(BF16), dims)
    return total


def neighbour(step_g, step_b, groups, bricks):
    g = lax.axis_index("grp")
    b = lax.axis_index("brick")
    return (lax.rem(g + step_g + groups, groups), lax.rem(b + step_b + bricks, bricks))


def greet(groups, bricks):
    barrier = pltpu.get_barrier_semaphore()
    for step in OFFSETS[1:]:
        pl.semaphore_signal(
            barrier, inc=1, device_id=neighbour(*step, groups, bricks), device_id_type=MESH
        )
    return barrier


def slot_row(index_ref):
    return jnp.concatenate([index_ref[k : k + 1, :] for k in range(index_ref.shape[0])], axis=1)


def column(row):
    return jnp.transpose(jnp.broadcast_to(row, (128, 128)))


def columns(values):
    vals = values.astype(F32)
    return jnp.concatenate([column(vals[i : i + 1, :]) for i in range(vals.shape[0])], axis=0)


def neighbours_sum(pad, i):
    rows = pad.shape[1] - 16
    centre = pad[i + 1, TOP : TOP + rows, :]
    total = pad[i + 2, TOP : TOP + rows, :] + pad[i, TOP : TOP + rows, :]
    total = total + pad[i + 1, TOP + 1 : TOP + rows + 1, :] + pad[i + 1, TOP - 1 : TOP + rows - 1, :]
    above, below = z_shifts(centre)
    return centre, total + above + below


def z_shifts(v):
    depth = v.shape[1]
    lane = lax.broadcasted_iota(I32, v.shape, 1)
    above = jnp.where(lane == depth - 1, 0.0, pltpu.roll(v, depth - 1, 1))
    below = jnp.where(lane == 0, 0.0, pltpu.roll(v, 1, 1))
    return above, below


def face_flux(pot_low, pot_high, ion_low, ion_high):
    speed = -mobility * (pot_high - pot_low)
    return (
        jnp.maximum(speed, 0.0) * ion_low
        + jnp.minimum(speed, 0.0) * ion_high
        - diffusion * (ion_high - ion_low)
    )


def inside_flags(groups, bricks):
    g = lax.axis_index("grp")
    b = lax.axis_index("brick")
    return (
        jnp.where(g > 0, 1.0, 0.0),
        jnp.where(g < groups - 1, 1.0, 0.0),
        jnp.where(b > 0, 1.0, 0.0),
        jnp.where(b < bricks - 1, 1.0, 0.0),
    )


def start_halos(fields, turn, x_out, x_in, y_out, y_in, send, recv, groups, bricks):
    nx, ny = fields[0].shape[0] - 2, fields[0].shape[1] - 2 * TOP
    for f, field in enumerate(fields):
        y_out[turn, 0, f] = field[1 : nx + 1, TOP, :]
        y_out[turn, 1, f] = field[1 : nx + 1, TOP + ny - 1, :]
        x_out[turn, 0, f] = field[1, TOP : TOP + ny, :]
        x_out[turn, 1, f] = field[nx, TOP : TOP + ny, :]
    count = len(fields)
    copies = []
    for side in range(2):
        step = 2 * side - 1
        for axis, (out, into) in enumerate(((x_out, x_in), (y_out, y_in))):
            copy = pltpu.make_async_remote_copy(
                src_ref=out.at[turn, side, pl.ds(0, count)],
                dst_ref=into.at[turn, 1 - side, pl.ds(0, count)],
                send_sem=send.at[turn, 2 * axis + side],
                recv_sem=recv.at[turn, 2 * axis + 1 - side],
                device_id=neighbour(step * (1 - axis), step * axis, groups, bricks),
                device_id_type=MESH,
            )
            copy.start()
            copies.append(copy)
    return copies


def finish_halos(copies, fields, turn, x_in, y_in, inside):
    for copy in copies:
        copy.wait()
    nx, ny = fields[0].shape[0] - 2, fields[0].shape[1] - 2 * TOP
    for f, field in enumerate(fields):
        field[0, TOP : TOP + ny, :] = x_in[turn, 0, f] * inside[0]
        field[nx + 1, TOP : TOP + ny, :] = x_in[turn, 1, f] * inside[1]
        field[1 : nx + 1, TOP - 1, :] = y_in[turn, 0, f] * inside[2]
        field[1 : nx + 1, TOP + ny, :] = y_in[turn, 1, f] * inside[3]


def send_rows(source, target, towards, send, recv, groups, bricks):
    slots = source.shape[0] // len(OFFSETS)
    copies = []
    for k in range(1, len(OFFSETS)):
        step_g, step_b = OFFSETS[k]
        copy = pltpu.make_async_remote_copy(
            src_ref=source.at[pl.ds(k * slots, slots), :],
            dst_ref=target.at[pl.ds(k * slots, slots), :],
            send_sem=send.at[k - 1],
            recv_sem=recv.at[k - 1],
            device_id=neighbour(towards * step_g, towards * step_b, groups, bricks),
            device_id_type=MESH,
        )
        copy.start()
        copies.append(copy)
    return copies


def weights():
    middle = 0.5 * (highest_eig + lowest_eig)
    spread = 0.5 * (highest_eig - lowest_eig)
    ratio_ms = middle / spread
    now = 1.0 / ratio_ms
    table = [(0.0, 1.0 / middle)]
    for _ in range(SWEEPS - 1):
        after = 1.0 / (2.0 * ratio_ms - now)
        table.append((after * now, 2.0 * after / spread))
        now = after
    return table


def sweep(turn, held, other, resid, screen, total):
    keep, gain = weights()[turn]
    nx, ny, nz = resid.shape

    def plane(i, carry):
        centre, around = neighbours_sum(held, i)
        diag = 6.0 + screen[i]
        rest = resid[i] - (diag * centre - around)
        resid[i] = rest
        update = gain * (rest / diag)
        if turn:
            update = keep * centre + update
            total[i] = total[i] + update
        else:
            total[i] = centre + update
        other[i + 1, TOP : TOP + ny, :] = update
        return carry

    lax.fori_loop(0, nx, plane, 0, unroll=2)


def cell_tables(cell_ref, nx, ny, nz):
    cell = cell_ref[...]
    clusters = cell.shape[0] * cell.shape[1]
    row_of = cell // nz
    row_line = jnp.concatenate([row_of[i : i + 1, :] for i in range(cell.shape[0])], axis=1)
    into = jnp.where(
        lax.broadcasted_iota(I32, (nx * ny, clusters), 0) == row_line, 1.0, 0.0
    ).astype(BF16)
    k_col = columns(cell - row_of * nz)
    k_col = jnp.concatenate([k_col, k_col], axis=1)
    at_depth = jnp.where(
        lax.broadcasted_iota(I32, (clusters, nz), 1).astype(F32) == k_col, 1.0, 0.0
    )
    return into, at_depth


def send_kernel(
    groups,
    bricks,
    count_ref,
    pos_hbm,
    charge_hbm,
    fill_hbm,
    cell_hbm,
    index_hbm,
    ion_hbm,
    prev_hbm,
    screen_hbm,
    data_ref,
    arrived_ref,
    update_ref,
    resid_ref,
    total_ref,
    pos,
    charges,
    fill,
    cells,
    index,
    screen,
    out_rows,
    in_rows,
    x_out,
    x_in,
    y_out,
    y_in,
    pad,
    load,
    row_send,
    row_recv,
    halo_send,
    halo_recv,
):
    nx, ny, nz = ion_hbm.shape
    loads = [
        pltpu.make_async_copy(src, dst, load.at[i])
        for i, (src, dst) in enumerate(
            (
                (index_hbm, index),
                (fill_hbm, fill),
                (cell_hbm, cells),
                (prev_hbm, pad.at[0, pl.ds(1, nx), pl.ds(TOP, ny), :]),
                (pos_hbm, pos),
                (charge_hbm, charges),
                (ion_hbm, resid_ref),
                (screen_hbm, screen),
            )
        )
    ]
    for copy in loads:
        copy.start()
    barrier = greet(groups, bricks)
    inside = inside_flags(groups, bricks)
    for copy in loads[:4]:
        copy.wait()
    exchange = (x_out, x_in, y_out, y_in, halo_send, halo_recv, groups, bricks)
    clusters = charges.shape[0]
    slots = index.shape[1]
    wanted = slot_row(index)
    chooser = jnp.where(
        lax.broadcasted_iota(I32, (clusters, wanted.shape[1]), 0) == wanted, 1.0, 0.0
    ).astype(BF16)
    fill_col = columns(fill[...])
    lane = lax.broadcasted_iota(I32, (clusters, 128), 1).astype(F32)
    for copy in loads[4:]:
        copy.wait()
    charge = charges[...] * jnp.where(lane < fill_col, 1.0, 0.0)
    for d in range(3):
        data_ref[:, d * 128 : (d + 1) * 128] = pos[:, d, :]
    data_ref[:, 384:512] = charge
    pl.semaphore_wait(barrier, len(OFFSETS) - 1)
    halos = start_halos([pad.at[0]], 0, *exchange)
    out_rows[...] = select_rows(chooser, data_ref[...], ((0,), (0,)))
    slot_id = lax.broadcasted_iota(I32, (slots, 128), 0)
    for k in range(len(OFFSETS)):
        live = jnp.where(slot_id < count_ref[0, k], 1.0, 0.0)
        out_rows[k * slots : (k + 1) * slots, 384:512] = (
            out_rows[k * slots : (k + 1) * slots, 384:512] * live
        )
    sends = send_rows(out_rows, in_rows, -1, row_send, row_recv, groups, bricks)
    into, at_depth = cell_tables(cells, nx, ny, nz)
    deposit = select_rows(into, at_depth * jnp.sum(charge, axis=1, keepdims=True))
    resid_ref[...] = resid_ref[...] + deposit_scale * deposit.reshape(nx, ny, nz)
    for turn in range(EARLY):
        held, other = pad.at[turn % 2], pad.at[1 - turn % 2]
        if turn:
            halos = start_halos([held], turn, *exchange)
        finish_halos(halos, [held], turn, x_in, y_in, inside)
        sweep(turn, held, other, resid_ref, screen, total_ref)
    update_ref[...] = pad[EARLY % 2, 1 : nx + 1, TOP : TOP + ny, :]
    for copy in sends:
        copy.wait()
    arrived_ref[0:slots, :] = out_rows[0:slots, :]
    arrived_ref[slots:, :] = in_rows[slots:, :]


def return_kernel(
    groups,
    bricks,
    count_ref,
    cell_hbm,
    index_hbm,
    ion_hbm,
    screen_hbm,
    data_ref,
    own_ref,
    part_ref,
    update_ref,
    resid_ref,
    total_ref,
    force_ref,
    pot_ref,
    next_ref,
    cells,
    index,
    screen,
    back,
    resid,
    x_out,
    x_in,
    y_out,
    y_in,
    pad,
    ion,
    efield,
    load,
    row_send,
    row_recv,
    halo_send,
    halo_recv,
):
    nx, ny, nz = ion_hbm.shape
    loads = [
        pltpu.make_async_copy(src, dst, load.at[i])
        for i, (src, dst) in enumerate(
            (
                (ion_hbm, ion.at[pl.ds(1, nx), pl.ds(TOP, ny), :]),
                (screen_hbm, screen),
                (index_hbm, index),
                (cell_hbm, cells),
            )
        )
    ]
    for copy in loads:
        copy.start()
    barrier = greet(groups, bricks)
    inside = inside_flags(groups, bricks)
    pad[EARLY % 2, 1 : nx + 1, TOP : TOP + ny, :] = update_ref[...]
    resid[...] = resid_ref[...]
    pot_ref[...] = total_ref[...]
    for copy in loads:
        copy.wait()
    exchange = (x_out, x_in, y_out, y_in, halo_send, halo_recv, groups, bricks)
    pl.semaphore_wait(barrier, len(OFFSETS) - 1)
    halos = start_halos([pad.at[EARLY % 2], ion], 0, *exchange)
    sends = send_rows(part_ref, back, 1, row_send, row_recv, groups, bricks)
    clusters = data_ref.shape[0]
    slots = index.shape[1]
    back[0:slots, :] = part_ref[0:slots, :]
    wanted = slot_row(index)
    spot = lax.broadcasted_iota(I32, (1, slots), 1)
    live = jnp.concatenate(
        [jnp.where(spot < count_ref[0, k], 1.0, 0.0) for k in range(len(OFFSETS))], axis=1
    )
    chooser = jnp.where(
        lax.broadcasted_iota(I32, (clusters, wanted.shape[1]), 0) == wanted,
        jnp.broadcast_to(live, (clusters, wanted.shape[1])),
        0.0,
    ).astype(BF16)
    into, at_depth = cell_tables(cells, nx, ny, nz)
    for turn in range(EARLY, SWEEPS):
        held, other = pad.at[turn % 2], pad.at[1 - turn % 2]
        fields = [held, ion] if turn == EARLY else [held]
        if turn > EARLY:
            halos = start_halos(fields, turn - EARLY, *exchange)
        finish_halos(halos, fields, turn - EARLY, x_in, y_in, inside)
        sweep(turn, held, other, resid, screen, pot_ref)
    pot = pad.at[SWEEPS % 2]
    pot[1 : nx + 1, TOP : TOP + ny, :] = pot_ref[...]
    halos = start_halos([pot], SWEEPS - EARLY, *exchange)
    finish_halos(halos, [pot], SWEEPS - EARLY, x_in, y_in, inside)

    def finish(i, carry):
        lo, hi = TOP, TOP + ny
        p, n = pot[i + 1, lo:hi, :], ion[i + 1, lo:hi, :]
        px = (pot[i, lo:hi, :], pot[i + 2, lo:hi, :])
        py = (pot[i + 1, lo - 1 : hi - 1, :], pot[i + 1, lo + 1 : hi + 1, :])
        ix = (ion[i, lo:hi, :], ion[i + 2, lo:hi, :])
        iy = (ion[i + 1, lo - 1 : hi - 1, :], ion[i + 1, lo + 1 : hi + 1, :])
        pz = z_shifts(p)[::-1]
        iz = z_shifts(n)[::-1]
        out = jnp.zeros_like(p)
        for d, (ps, ns) in enumerate(((px, ix), (py, iy), (pz, iz))):
            out = out + (face_flux(p, ps[1], n, ns[1]) - face_flux(ps[0], p, ns[0], n))
            efield[d, pl.ds(pl.multiple_of(i * ny, ny), ny), :] = -(ps[1] - ps[0]) * 0.5
        next_ref[i] = n - time_step * out
        return carry

    lax.fori_loop(0, nx, finish, 0)
    push = []
    for d in range(3):
        seen = select_rows(into, efield[d], ((0,), (0,)))
        push.append(field_scale * jnp.sum(seen * at_depth, axis=1, keepdims=True))
    for copy in sends:
        copy.wait()
    sums = own_ref[...] + select_rows(chooser, back[...])
    charge = data_ref[:, 384:512]
    for d in range(3):
        pull = data_ref[:, d * 128 : (d + 1) * 128] * sums[:, 0:128] - sums[:, (d + 1) * 128 : (d + 2) * 128]
        force_ref[:, d, :] = charge * (coulomb_scale * pull + push[d])


def features(data_ref, feat, vals, own):
    spots = [data_ref[:, d * 128 : (d + 1) * 128] for d in range(3)]
    charge = data_ref[:, 384:512]
    square = jnp.zeros_like(charge)
    for d in range(3):
        high, mid, low = split3(spots[d])
        rows = (high, high, mid, mid, high, low) if own else (high, mid, high, mid, low, high)
        for f, row in enumerate(rows):
            feat[:, 6 * d + f, :] = -2.0 * row if own else row
        square = square + spots[d] * spots[d]
    if own:
        square = square + softening
    one = jnp.ones_like(square)
    for f, row in enumerate(split3(square)):
        feat[:, (18 if own else 21) + f, :] = row
        feat[:, (21 if own else 18) + f, :] = one
    for c, val in enumerate((charge, charge * spots[0], charge * spots[1], charge * spots[2])):
        for f, row in enumerate(split3(val)):
            vals[:, 4 * f + c, :] = row
    for f in range(12, 16):
        vals[:, f, :] = jnp.zeros_like(charge)


def tile_sums(own_ids, part_ids, own_feat, own_vals, part_feat, part_vals):
    left = jnp.concatenate([own_feat[o] for o in own_ids], axis=0).astype(BF16)
    blank = jnp.zeros((24, 128), F32)
    count = len(own_ids)
    right = jnp.concatenate(
        [
            jnp.concatenate([part_feat[r] if i == j else blank for i in range(count)], axis=0).astype(BF16)
            for j, r in enumerate(part_ids)
        ],
        axis=1,
    )
    dist = dot(left, right, ((0,), (0,)))
    sums = []
    for j in range(count):
        root = lax.rsqrt(dist[:, j * 128 : (j + 1) * 128])
        u = root * root * root
        high = u.astype(BF16)
        low = (u - high.astype(F32)).astype(BF16)
        mine = own_vals[own_ids[j]].astype(BF16)
        theirs = part_vals[part_ids[j]].astype(BF16)
        on_part = dot(jnp.concatenate([mine, mine], axis=1), jnp.concatenate([high, low], axis=0))
        on_own = dot(
            jnp.concatenate([theirs, theirs], axis=1),
            jnp.concatenate([high, low], axis=1),
            ((1,), (1,)),
        )
        sums.append((on_own, on_part))
    return sums


def pair_kernel(
    local_ref,
    dir_ref,
    slot_ref,
    data_ref,
    arrived_ref,
    own_ref,
    part_ref,
    own_feat,
    own_vals,
    part_feat,
    part_vals,
    own_acc,
    part_acc,
):
    features(data_ref, own_feat, own_vals, True)
    features(arrived_ref, part_feat, part_vals, False)
    own_acc[...] = jnp.zeros_like(own_acc)
    part_acc[...] = jnp.zeros_like(part_acc)
    slots = arrived_ref.shape[0] // len(OFFSETS)
    step = PAIRS_AT_ONCE * GROUPS

    @pl.loop(0, local_ref.shape[0] // step)
    def _(turn):
        done = []
        for group in range(GROUPS):
            base = turn * step + group * PAIRS_AT_ONCE
            own_ids = [local_ref[base + j] for j in range(PAIRS_AT_ONCE)]
            part_ids = [
                dir_ref[base + j] * slots + slot_ref[base + j] for j in range(PAIRS_AT_ONCE)
            ]
            done.append(
                (own_ids, part_ids, tile_sums(own_ids, part_ids, own_feat, own_vals, part_feat, part_vals))
            )
        for own_ids, part_ids, sums in done:
            for j, (on_own, on_part) in enumerate(sums):
                own_acc[own_ids[j]] += on_own
                part_acc[part_ids[j]] += on_part

    for acc, out in ((own_acc, own_ref), (part_acc, part_ref)):
        for c in range(4):
            out[:, c * 128 : (c + 1) * 128] = acc[:, c, :] + (acc[:, 4 + c, :] + acc[:, 8 + c, :])


def shards(
    groups,
    bricks,
    positions,
    charges,
    cluster_fill,
    cluster_cell,
    send_index,
    send_count,
    pair_local,
    pair_dir,
    pair_slot,
    ion_density,
    potential_prev,
    screening,
):
    clusters = cluster_fill.shape[0]
    psize = charges.shape[0] // clusters
    dirs, slots = send_index.shape
    nx, ny, nz = ion_density.shape
    placed = positions.reshape(3, clusters, psize).transpose(1, 0, 2)
    vmem = pl.BlockSpec(memory_space=pltpu.VMEM)
    smem = pl.BlockSpec(memory_space=pltpu.SMEM)
    hbm = pl.BlockSpec(memory_space=pltpu.HBM)
    shape = lambda *dims: jax.ShapeDtypeStruct(dims, F32)
    halo = lambda turns, fields, length: pltpu.VMEM((turns, 2, fields, length, nz), F32)
    block = shape(nx, ny, nz)
    rows = shape(dirs * slots, 4 * psize)
    padded = (nx + 2, ny + 2 * TOP, nz)
    cells = cluster_cell.reshape(clusters // 128, 128)
    late = SWEEPS + 1 - EARLY
    data, arrived, update, resid, total = pl.pallas_call(
        functools.partial(send_kernel, groups, bricks),
        out_shape=(shape(clusters, 4 * psize), rows, block, block, block),
        in_specs=[smem] + [hbm] * 8,
        out_specs=[vmem] * 5,
        scratch_shapes=[
            pltpu.VMEM((clusters, 3, psize), F32),
            pltpu.VMEM((clusters, psize), F32),
            pltpu.VMEM((clusters // 128, 128), I32),
            pltpu.VMEM((clusters // 128, 128), I32),
            pltpu.VMEM((dirs, slots), I32),
            pltpu.VMEM((nx, ny, nz), F32),
            pltpu.VMEM((dirs * slots, 4 * psize), F32),
            pltpu.VMEM((dirs * slots, 4 * psize), F32),
            halo(EARLY, 1, ny),
            halo(EARLY, 1, ny),
            halo(EARLY, 1, nx),
            halo(EARLY, 1, nx),
            pltpu.VMEM((2, *padded), F32),
            pltpu.SemaphoreType.DMA((8,)),
            pltpu.SemaphoreType.DMA((dirs - 1,)),
            pltpu.SemaphoreType.DMA((dirs - 1,)),
            pltpu.SemaphoreType.DMA((EARLY, 4)),
            pltpu.SemaphoreType.DMA((EARLY, 4)),
        ],
        compiler_params=pltpu.CompilerParams(
            collective_id=0, has_side_effects=True, vmem_limit_bytes=40 << 20
        ),
        name="send",
    )(
        send_count,
        placed,
        charges.reshape(clusters, psize),
        cluster_fill.reshape(clusters // 128, 128),
        cells,
        send_index,
        ion_density,
        potential_prev,
        screening,
    )
    own_sums, part_sums = pl.pallas_call(
        pair_kernel,
        out_shape=(shape(clusters, 4 * psize), rows),
        in_specs=[smem] * 3 + [vmem] * 2,
        out_specs=[vmem] * 2,
        scratch_shapes=[
            pltpu.VMEM((clusters, 24, psize), F32),
            pltpu.VMEM((clusters, 16, psize), F32),
            pltpu.VMEM((dirs * slots, 24, psize), F32),
            pltpu.VMEM((dirs * slots, 16, psize), F32),
            pltpu.VMEM((clusters, 16, psize), F32),
            pltpu.VMEM((dirs * slots, 16, psize), F32),
        ],
        compiler_params=pltpu.CompilerParams(vmem_limit_bytes=40 << 20),
        name="pairs",
    )(pair_local, pair_dir, pair_slot, data, arrived)
    forces, potential, ion_next = pl.pallas_call(
        functools.partial(return_kernel, groups, bricks),
        out_shape=(shape(clusters, 3, psize), block, block),
        in_specs=[smem] + [hbm] * 4 + [vmem] * 6,
        out_specs=[vmem] * 3,
        scratch_shapes=[
            pltpu.VMEM((clusters // 128, 128), I32),
            pltpu.VMEM((dirs, slots), I32),
            pltpu.VMEM((nx, ny, nz), F32),
            pltpu.VMEM((dirs * slots, 4 * psize), F32),
            pltpu.VMEM((nx, ny, nz), F32),
            halo(late, 2, ny),
            halo(late, 2, ny),
            halo(late, 2, nx),
            halo(late, 2, nx),
            pltpu.VMEM((2, *padded), F32),
            pltpu.VMEM(padded, F32),
            pltpu.VMEM((3, nx * ny, nz), F32),
            pltpu.SemaphoreType.DMA((4,)),
            pltpu.SemaphoreType.DMA((dirs - 1,)),
            pltpu.SemaphoreType.DMA((dirs - 1,)),
            pltpu.SemaphoreType.DMA((late, 4)),
            pltpu.SemaphoreType.DMA((late, 4)),
        ],
        compiler_params=pltpu.CompilerParams(
            collective_id=1, has_side_effects=True, vmem_limit_bytes=40 << 20
        ),
        name="back",
    )(
        send_count,
        cells,
        send_index,
        ion_density,
        screening,
        data,
        own_sums,
        part_sums,
        update,
        resid,
        total,
    )
    return (forces.transpose(1, 0, 2).reshape(3, -1), potential, ion_next)


def solution(mesh):
    in_specs = (
        P(None, ("grp", "brick")),
        P(("grp", "brick")),
        P(("grp", "brick")),
        P(("grp", "brick")),
        P(("grp", "brick"), None),
        P(("grp", "brick"), None),
        P(("grp", "brick")),
        P(("grp", "brick")),
        P(("grp", "brick")),
        P("grp", "brick", None),
        P("grp", "brick", None),
        P("grp", "brick", None),
    )
    out_specs = (P(None, ("grp", "brick")), P("grp", "brick", None), P("grp", "brick", None))
    body = functools.partial(shards, mesh.shape["grp"], mesh.shape["brick"])
    return jax.shard_map(body, mesh=mesh, in_specs=in_specs, out_specs=out_specs, check_vma=False)
```

time: 131 us -> 119 us (0.908)
  Pallas kernels: 121 us -> 110 us
    pallas_call x2, Pallas kernels: 107 us -> 86.5 us  [the longest x1 59.1 us: shards(): pl.pallas_call(pair_kernel, out_shape=(shape(clusters, 4 * psize), rows),...]
    pallas_call x1, Pallas kernels: 13.4 us -> 23.4 us  [shards(): pl.pallas_call(functools.partial(return_kernel, groups, bricks), out_shap...]
    unnamed x27 -> x31, local copies, waits for them, and re-layouts: 8.83 us -> 8.15 us
where the time goes in v2:
time: 119 us
  Pallas kernels  110 us (92%)
  local copies, waits for them, and re-layouts  8.15 us (7%)
    pallas_call x1, Pallas kernels, shards(): pl.pallas_call(pair_kernel, out_shape=(shape(clusters, 4 * psize), rows),...  59.1 us
    pallas_call x1, Pallas kernels, shards(): pl.pallas_call(functools.partial(send_kernel, groups, bricks), out_shape=...  27.4 us
    pallas_call x1, Pallas kernels, shards(): pl.pallas_call(functools.partial(return_kernel, groups, bricks), out_shap...  23.4 us
    unnamed x31, local copies, waits for them, and re-layouts  8.15 us

profile of v2, /device:TPU:1, one launch (start us, length us, event | category | flops | bytes accessed | tf_op | source)
XLA Modules:
  0.0 118.8 jit_solution(10396474756308694512)
XLA Ops:
  0.6 0.0 copy-start.7
  0.6 0.0 copy-start.13
  0.7 0.0 copy-start.11
  0.7 0.0 copy-start.12
  0.7 0.6 copy-done.7
  1.3 0.0 copy-done.13
  1.3 0.0 copy-done.11
  1.3 0.0 copy-done.12
  1.3 0.0 copy-start
  1.4 1.0 copy-done
  2.4 0.0 copy-start.2
  2.4 1.0 copy-done.2
  3.4 0.0 copy-start.4
  3.4 1.0 copy-done.4
  4.5 0.0 copy-start.5
  4.5 1.0 copy-done.5
  5.5 0.0 copy-start.6
  5.5 0.9 copy-done.6
  6.4 0.0 copy-start.8
  6.4 0.0 copy-start.9
  6.4 27.4 %send.1 = (f32[256,512]{1,0:T(8,128)S(1)}, f32[224,512]{1,0:T(8,128)S(1)}, f32[16,32,256]{2,1,0:T(8,128)S(1)}, f32[16,32,256]{2,1,0:T(8,128)S(1)}, f32[16,32,256]{2,1,0:T(8,128)S(1)}) custom-call(s32[1,7]{1,0:T(1,128)S(1)} %copy-done.12, f32[256,3,128]{2,1,0:T(4,128)S(1)} %bitcast.10, f32[256,128]{1,0:T(8,128)S(1)} %bitcast.11, s32[2,128]{1,0:T(2,128)S(1)} %bitcast.14, ...), custom_call_target="tpu_custom_call" | custom-call | tf_op jit(solution)/shard_map/send/pallas_call | solution.py:560
  33.8 0.0 copy-start.1
  33.9 0.0 copy-done.8
  33.9 0.0 copy-done.9
  33.9 0.0 copy-done.10
  33.9 59.1 %pairs.1 = (f32[256,512]{1,0:T(8,128)S(1)}, f32[224,512]{1,0:T(8,128)S(1)}) custom-call(s32[1024]{0:T(1024)S(1)} %copy-done.8, s32[1024]{0:T(1024)S(1)} %copy-done.9, s32[1024]{0:T(1024)S(1)} %copy-done.10, f32[256,512]{1,0:T(8,128)S(1)} %get-tuple-element.13.data_ref, f32[224,512]{1,0:T(8,128)S(1)} %get-tuple-element.14.arrived_ref), custom_call_target="tpu_custom_call" | custom-call | tf_op jit(solution)/shard_map/pairs/pallas_call | solution.py:600
  93.0 0.0 copy-done.3
  93.0 0.0 copy-done.1
  93.0 23.4 %back.1 = (f32[256,3,128]{2,1,0:T(4,128)S(1)}, f32[16,32,256]{2,1,0:T(8,128)S(1)}, f32[16,32,256]{2,1,0:T(8,128)S(1)}) custom-call(s32[1,7]{1,0:T(1,128)S(1)} %copy-done.12, s32[2,128]{1,0:T(2,128)S(1)} %bitcast.13, s32[7,32]{1,0:T(8,128)S(1)} %copy-done.7, f32[16,32,256]{2,1,0:T(8,128)S(1)} %copy-done.1, f32[16,32,256]{2,1,0:T(8,128)S(1)} %copy-done.3, ...), custom_call_target="tpu_custom_call" | custom-call | tf_op jit(solution)/shard_map/back/pallas_call | solution.py:616
  116.5 0.8 copy.18
  117.3 0.8 copy.19
  118.1 0.8 copy.20
  (2 shorter events, 0.0 us)
Async XLA Ops:
  0.6 0.7 copy-start.7
  0.6 0.7 copy-start.13
  0.7 0.7 copy-start.11
  0.7 0.7 copy-start.12
  1.3 1.0 copy-start
  2.4 1.0 copy-start.2
  3.4 1.0 copy-start.4
  4.5 1.0 copy-start.5
  5.5 0.9 copy-start.6
  6.4 27.4 %copy-start.8 = (s32[1024]{0:T(1024)S(1)}, s32[1024]{0:T(1024)}, u32[]{:S(2)}) copy-start(s32[1024]{0:T(1024)} %local_ref.1) | copy-start | bytes 12292
  6.4 27.4 %copy-start.9 = (s32[1024]{0:T(1024)S(1)}, s32[1024]{0:T(1024)}, u32[]{:S(2)}) copy-start(s32[1024]{0:T(1024)} %dir_ref.1) | copy-start | bytes 12292
  6.4 27.5 %copy-start.10 = (s32[1024]{0:T(1024)S(1)}, s32[1024]{0:T(1024)}, u32[]{:S(2)}) copy-start(s32[1024]{0:T(1024)} %slot_ref.1) | copy-start | bytes 12292
  6.4 86.6 %copy-start.3 = (f32[16,32,256]{2,1,0:T(8,128)S(1)}, f32[16,32,256]{2,1,0:T(8,128)}, u32[]{:S(2)}) copy-start(f32[16,32,256]{2,1,0:T(8,128)} %screen_hbm.3) | copy-start | bytes 1572868
  33.8 59.2 %copy-start.1 = (f32[16,32,256]{2,1,0:T(8,128)S(1)}, f32[16,32,256]{2,1,0:T(8,128)}, u32[]{:S(2)}) copy-start(f32[16,32,256]{2,1,0:T(8,128)} %ion_hbm.3) | copy-start | bytes 1572868

commit v3 on v2

--- a/solution.py
+++ b/solution.py
@@ -21,8 +21,9 @@
 time_step = 0.2
 OFFSETS = ((0, 0), (0, -1), (0, 1), (0, -2), (0, 2), (-1, 0), (1, 0))
 MESH = pl.DeviceIdType.MESH
-PAIRS_AT_ONCE = 8
-GROUPS = 4
+BATCH = 32
+STEP = 32
+ORDER = (4, 3, 2, 1)
 TOP = 8
 
 
@@ -316,7 +317,6 @@
 def return_kernel(
     groups,
     bricks,
-    count_ref,
     cell_hbm,
     index_hbm,
     ion_hbm,
@@ -377,14 +377,8 @@
     slots = index.shape[1]
     back[0:slots, :] = part_ref[0:slots, :]
     wanted = slot_row(index)
-    spot = lax.broadcasted_iota(I32, (1, slots), 1)
-    live = jnp.concatenate(
-        [jnp.where(spot < count_ref[0, k], 1.0, 0.0) for k in range(len(OFFSETS))], axis=1
-    )
     chooser = jnp.where(
-        lax.broadcasted_iota(I32, (clusters, wanted.shape[1]), 0) == wanted,
-        jnp.broadcast_to(live, (clusters, wanted.shape[1])),
-        0.0,
+        lax.broadcasted_iota(I32, (clusters, wanted.shape[1]), 0) == wanted, 1.0, 0.0
     ).astype(BF16)
     into, at_depth = cell_tables(cells, nx, ny, nz)
     for turn in range(EARLY, SWEEPS):
@@ -422,64 +416,145 @@
         push.append(field_scale * jnp.sum(seen * at_depth, axis=1, keepdims=True))
     for copy in sends:
         copy.wait()
-    sums = own_ref[...] + select_rows(chooser, back[...])
+    react = select_rows(chooser, back[...])
     charge = data_ref[:, 384:512]
     for d in range(3):
-        pull = data_ref[:, d * 128 : (d + 1) * 128] * sums[:, 0:128] - sums[:, (d + 1) * 128 : (d + 2) * 128]
-        force_ref[:, d, :] = charge * (coulomb_scale * pull + push[d])
-
-
-def features(data_ref, feat, vals, own):
-    spots = [data_ref[:, d * 128 : (d + 1) * 128] for d in range(3)]
-    charge = data_ref[:, 384:512]
+        near = slice(d * 128, (d + 1) * 128)
+        pull = data_ref[:, near] * own_ref[:, 0:128] - own_ref[:, (d + 1) * 128 : (d + 2) * 128]
+        force_ref[:, d, :] = charge * (coulomb_scale * pull + push[d]) + coulomb_scale * react[:, near]
+
+
+def features(data, base, row_feat, lane_feat, vals):
+    @pl.loop(0, data.shape[0] // 8, unroll=4)
+    def _(g):
+        at = pl.multiple_of(g * 8, 8)
+        feature_rows(data[pl.ds(at, 8), :], base + at, row_feat, lane_feat, vals)
+
+
+def feature_rows(data, base, row_feat, lane_feat, vals):
+    spots = [data[:, d * 128 : (d + 1) * 128] for d in range(3)]
+    charge = data[:, 384:512]
+    here = pl.ds(base, 8)
+    one = jnp.ones_like(charge)
     square = jnp.zeros_like(charge)
+    left, right, weighed = [], [], []
     for d in range(3):
         high, mid, low = split3(spots[d])
-        rows = (high, high, mid, mid, high, low) if own else (high, mid, high, mid, low, high)
-        for f, row in enumerate(rows):
-            feat[:, 6 * d + f, :] = -2.0 * row if own else row
+        left += [-2.0 * part for part in (high, high, mid, mid, high, low)]
+        right += [high, mid, high, mid, low, high]
         square = square + spots[d] * spots[d]
-    if own:
-        square = square + softening
-    one = jnp.ones_like(square)
-    for f, row in enumerate(split3(square)):
-        feat[:, (18 if own else 21) + f, :] = row
-        feat[:, (21 if own else 18) + f, :] = one
-    for c, val in enumerate((charge, charge * spots[0], charge * spots[1], charge * spots[2])):
-        for f, row in enumerate(split3(val)):
-            vals[:, 4 * f + c, :] = row
-    for f in range(12, 16):
-        vals[:, f, :] = jnp.zeros_like(charge)
-
-
-def tile_sums(own_ids, part_ids, own_feat, own_vals, part_feat, part_vals):
-    left = jnp.concatenate([own_feat[o] for o in own_ids], axis=0).astype(BF16)
+    left += list(split3(square + softening)) + [one] * 3
+    right += [one] * 3 + list(split3(square))
+    parts = [split3(v) for v in (charge, charge * spots[0], charge * spots[1], charge * spots[2])]
+    for f in range(3):
+        weighed += [part[f] for part in parts]
+    weighed += [jnp.zeros_like(charge)] * 4
+    for rows, table in ((left, row_feat), (right, lane_feat), (weighed, vals)):
+        for k in range(0, len(rows), 8):
+            table[here, k : k + 8, :] = jnp.transpose(jnp.stack(rows[k : k + 8]), (1, 0, 2))
+
+
+def extent(data):
+    charge = data[:, 384:512]
+    lane = lax.broadcasted_iota(I32, charge.shape, 1).astype(F32) + 1.0
+    return jnp.max(jnp.where(charge != 0.0, lane, 0.0), axis=1, keepdims=True)
+
+
+def sort_pairs(local_ref, part_ids, own_extent, part_extent, order_vmem):
+    rows = local_ref.shape[0]
+    clusters, partners = own_extent.shape[0], part_extent.shape[0]
+    own_lines, part_lines = [], []
+    for r in range(rows):
+        for lines, ids, ext in (
+            (own_lines, local_ref[r : r + 1, :], own_extent),
+            (part_lines, part_ids[r : r + 1, :], part_extent),
+        ):
+            spot = lax.broadcasted_iota(I32, (ext.shape[0], 128), 0)
+            lines.append(jnp.sum(jnp.where(spot == ids, ext, 0.0), axis=0, keepdims=True))
+    own_len = jnp.concatenate(own_lines, axis=0)
+    part_len = jnp.concatenate(part_lines, axis=0)
+    short = jnp.minimum(own_len, part_len)
+    blank = clusters + partners
+    own_code = blank - local_ref[...]
+    part_code = partners - part_ids
+    swap = part_len < own_len
+    row_code = jnp.where(swap, part_code, own_code)
+    lane_code = jnp.where(swap, own_code, part_code)
+    fields = [
+        v.astype(F32)
+        for v in (row_code & 255, row_code >> 8, lane_code & 255, lane_code >> 8)
+    ]
+    upto = jnp.where(
+        lax.broadcasted_iota(I32, (128, 128), 0) <= lax.broadcasted_iota(I32, (128, 128), 1), 1.0, 0.0
+    ).astype(BF16)
+    before = jnp.where(
+        lax.broadcasted_iota(I32, (rows, rows), 1) < lax.broadcasted_iota(I32, (rows, rows), 0), 1.0, 0.0
+    ).astype(BF16)
+    place = jnp.full((rows, 128), -1.0, F32)
+    base = jnp.int32(0)
+    spans = []
+    for blocks in ORDER:
+        member = jnp.where((short > float(STEP) * (blocks - 1)) & (short <= float(STEP) * blocks), 1.0, 0.0)
+        within = dot(member.astype(BF16), upto)
+        total = jnp.sum(member, axis=1, keepdims=True)
+        ahead = dot(before, jnp.broadcast_to(total, (rows, 128)).astype(BF16))
+        place = jnp.where(member > 0.0, base.astype(F32) + ahead + within - 1.0, place)
+        batches = (jnp.sum(member).astype(I32) + BATCH - 1) // BATCH
+        spans.append((base, batches))
+        base = base + batches * BATCH
+    place = place.astype(I32)
+    room = order_vmem.shape[1]
+    found = jnp.zeros((4 * room, 128), F32)
+    for r in range(rows):
+        at = place[r : r + 1, :]
+        here = jnp.where(lax.broadcasted_iota(I32, (128, 128), 0) == at & 127, 1.0, 0.0)
+        ours = lax.broadcasted_iota(I32, (room, 128), 0) == at >> 7
+        load = jnp.concatenate([jnp.where(ours, f[r : r + 1, :], 0.0) for f in fields], axis=0)
+        found = found + dot(load.astype(BF16), here.astype(BF16), ((1,), (1,)))
+    found = [found[i * room : (i + 1) * room, :] for i in range(4)]
+    order_vmem[0] = blank - (found[0] + 256.0 * found[1]).astype(I32)
+    order_vmem[1] = blank - (found[2] + 256.0 * found[3]).astype(I32)
+    return spans
+
+
+def distances(row_ids, lane_ids, rows, row_feat, lane_feat, dist):
     blank = jnp.zeros((24, 128), F32)
-    count = len(own_ids)
-    right = jnp.concatenate(
-        [
-            jnp.concatenate([part_feat[r] if i == j else blank for i in range(count)], axis=0).astype(BF16)
-            for j, r in enumerate(part_ids)
-        ],
-        axis=1,
-    )
-    dist = dot(left, right, ((0,), (0,)))
+    for k in range(0, len(row_ids), 2):
+        left = jnp.concatenate([row_feat[o] for o in row_ids[k : k + 2]], axis=0)
+        left = left[:, :rows].astype(BF16)
+        a, b = (lane_feat[r] for r in lane_ids[k : k + 2])
+        right = jnp.concatenate(
+            [
+                jnp.concatenate([a, blank], axis=0).astype(BF16),
+                jnp.concatenate([blank, b], axis=0).astype(BF16),
+            ],
+            axis=1,
+        )
+        dist[k // 2, 0:rows, :] = dot(left, right, ((0,), (0,)))
+
+
+def tile_sums(row_ids, lane_ids, rows, dist, vals, acc):
     sums = []
-    for j in range(count):
-        root = lax.rsqrt(dist[:, j * 128 : (j + 1) * 128])
+    for j in range(len(row_ids)):
+        root = lax.rsqrt(dist[j // 2, 0:rows, (j % 2) * 128 : (j % 2) * 128 + 128])
         u = root * root * root
         high = u.astype(BF16)
         low = (u - high.astype(F32)).astype(BF16)
-        mine = own_vals[own_ids[j]].astype(BF16)
-        theirs = part_vals[part_ids[j]].astype(BF16)
-        on_part = dot(jnp.concatenate([mine, mine], axis=1), jnp.concatenate([high, low], axis=0))
-        on_own = dot(
+        mine = vals[row_ids[j]][:, :rows].astype(BF16)
+        theirs = vals[lane_ids[j]].astype(BF16)
+        if rows == 128:
+            on_lane = dot(jnp.concatenate([mine, mine], axis=1), jnp.concatenate([high, low], axis=0))
+        else:
+            on_lane = dot(mine, high) + dot(mine, low)
+        on_row = dot(
             jnp.concatenate([theirs, theirs], axis=1),
             jnp.concatenate([high, low], axis=1),
             ((1,), (1,)),
         )
-        sums.append((on_own, on_part))
-    return sums
+        sums.append((on_row, on_lane))
+    for j, (on_row, on_lane) in enumerate(sums):
+        acc[row_ids[j], :, 0:rows] += on_row
+        acc[lane_ids[j]] += on_lane
 
 
 def pair_kernel(
@@ -490,40 +565,58 @@
     arrived_ref,
     own_ref,
     part_ref,
-    own_feat,
-    own_vals,
-    part_feat,
-    part_vals,
-    own_acc,
-    part_acc,
+    row_feat,
+    lane_feat,
+    vals,
+    acc,
+    dist,
+    order_vmem,
+    order,
+    sem,
 ):
-    features(data_ref, own_feat, own_vals, True)
-    features(arrived_ref, part_feat, part_vals, False)
-    own_acc[...] = jnp.zeros_like(own_acc)
-    part_acc[...] = jnp.zeros_like(part_acc)
-    slots = arrived_ref.shape[0] // len(OFFSETS)
-    step = PAIRS_AT_ONCE * GROUPS
-
-    @pl.loop(0, local_ref.shape[0] // step)
-    def _(turn):
-        done = []
-        for group in range(GROUPS):
-            base = turn * step + group * PAIRS_AT_ONCE
-            own_ids = [local_ref[base + j] for j in range(PAIRS_AT_ONCE)]
-            part_ids = [
-                dir_ref[base + j] * slots + slot_ref[base + j] for j in range(PAIRS_AT_ONCE)
-            ]
-            done.append(
-                (own_ids, part_ids, tile_sums(own_ids, part_ids, own_feat, own_vals, part_feat, part_vals))
-            )
-        for own_ids, part_ids, sums in done:
-            for j, (on_own, on_part) in enumerate(sums):
-                own_acc[own_ids[j]] += on_own
-                part_acc[part_ids[j]] += on_part
-
-    for acc, out in ((own_acc, own_ref), (part_acc, part_ref)):
-        for c in range(4):
-            out[:, c * 128 : (c + 1) * 128] = acc[:, c, :] + (acc[:, 4 + c, :] + acc[:, 8 + c, :])
+    clusters, partners = data_ref.shape[0], arrived_ref.shape[0]
+    slots = partners // len(OFFSETS)
+    part_ids = dir_ref[...] * slots + slot_ref[...]
+    spans = sort_pairs(
+        local_ref, part_ids, extent(data_ref[...]), extent(arrived_ref[...]), order_vmem
+    )
+    copy = pltpu.make_async_copy(order_vmem, order, sem)
+    copy.start()
+    features(data_ref, 0, row_feat, lane_feat, vals)
+    features(arrived_ref, clusters, row_feat, lane_feat, vals)
+    feature_rows(jnp.zeros((8, 512), F32), clusters + partners, row_feat, lane_feat, vals)
+    acc[...] = jnp.zeros_like(acc)
+    copy.wait()
+    for blocks, (base, batches) in zip(ORDER, spans):
+        rows = STEP * blocks
+
+        def ids(turn, base=base):
+            at = base + turn * BATCH
+            line, first = at >> 7, at & 127
+            return [[order[s, line, first + j] for j in range(BATCH)] for s in range(2)]
+
+        @pl.when(batches > 0)
+        def _(batches=batches, ids=ids, rows=rows):
+            distances(*ids(0), rows, row_feat, lane_feat, dist)
+
+            @pl.loop(0, batches)
+            def _(turn):
+                now = ids(turn)
+                ahead = ids(jnp.minimum(turn + 1, batches - 1))
+                tile_sums(*now, rows, dist, vals, acc)
+                distances(*ahead, rows, row_feat, lane_feat, dist)
+
+    def total(base, count, c):
+        here = pl.ds(base, count)
+        return acc[here, c, :] + (acc[here, 4 + c, :] + acc[here, 8 + c, :])
+
+    for c in range(4):
+        own_ref[:, c * 128 : (c + 1) * 128] = total(0, clusters, c)
+    charge = arrived_ref[:, 384:512]
+    whole = total(clusters, partners, 0)
+    for d in range(3):
+        near = slice(d * 128, (d + 1) * 128)
+        part_ref[:, near] = charge * (arrived_ref[:, near] * whole - total(clusters, partners, d + 1))
 
 
 def shards(
@@ -597,32 +690,38 @@
         potential_prev,
         screening,
     )
+    pairs = pair_local.shape[0]
+    table = (clusters + dirs * slots + 8,)
+    room = -(-(pairs + len(ORDER) * BATCH) // 1024) * 8
+    lines = lambda v: v.reshape(pairs // 128, 128)
     own_sums, part_sums = pl.pallas_call(
         pair_kernel,
-        out_shape=(shape(clusters, 4 * psize), rows),
-        in_specs=[smem] * 3 + [vmem] * 2,
+        out_shape=(shape(clusters, 4 * psize), shape(dirs * slots, 3 * psize)),
+        in_specs=[vmem] * 5,
         out_specs=[vmem] * 2,
         scratch_shapes=[
-            pltpu.VMEM((clusters, 24, psize), F32),
-            pltpu.VMEM((clusters, 16, psize), F32),
-            pltpu.VMEM((dirs * slots, 24, psize), F32),
-            pltpu.VMEM((dirs * slots, 16, psize), F32),
-            pltpu.VMEM((clusters, 16, psize), F32),
-            pltpu.VMEM((dirs * slots, 16, psize), F32),
+            pltpu.VMEM((*table, 24, psize), F32),
+            pltpu.VMEM((*table, 24, psize), F32),
+            pltpu.VMEM((*table, 16, psize), F32),
+            pltpu.VMEM((*table, 16, psize), F32),
+            pltpu.VMEM((BATCH // 2, psize, 2 * psize), F32),
+            pltpu.VMEM((2, room, 128), I32),
+            pltpu.SMEM((2, room, 128), I32),
+            pltpu.SemaphoreType.DMA(()),
         ],
-        compiler_params=pltpu.CompilerParams(vmem_limit_bytes=40 << 20),
+        compiler_params=pltpu.CompilerParams(vmem_limit_bytes=48 << 20),
         name="pairs",
-    )(pair_local, pair_dir, pair_slot, data, arrived)
+    )(lines(pair_local), lines(pair_dir), lines(pair_slot), data, arrived)
     forces, potential, ion_next = pl.pallas_call(
         functools.partial(return_kernel, groups, bricks),
         out_shape=(shape(clusters, 3, psize), block, block),
-        in_specs=[smem] + [hbm] * 4 + [vmem] * 6,
+        in_specs=[hbm] * 4 + [vmem] * 6,
         out_specs=[vmem] * 3,
         scratch_shapes=[
             pltpu.VMEM((clusters // 128, 128), I32),
             pltpu.VMEM((dirs, slots), I32),
             pltpu.VMEM((nx, ny, nz), F32),
-            pltpu.VMEM((dirs * slots, 4 * psize), F32),
+            pltpu.VMEM((dirs * slots, 3 * psize), F32),
             pltpu.VMEM((nx, ny, nz), F32),
             halo(late, 2, ny),
             halo(late, 2, ny),
@@ -642,7 +741,6 @@
         ),
         name="back",
     )(
-        send_count,
         cells,
         send_index,
         ion_density,

time: 119 us -> 87.2 us (0.73)
  Pallas kernels: 110 us -> 77.2 us
    pallas_call x1, Pallas kernels: 59.1 us -> 25.2 us  [shards(): pl.pallas_call(pair_kernel, out_shape=(shape(clusters, 4 * psize), shape(...]
where the time goes in v3:
time: 87.2 us; the launch traced here: 86.1 us
  Pallas kernels  77.2 us (89%)
  local copies, waits for them, and re-layouts  8.15 us (9%)
    pallas_call x1, Pallas kernels, shards(): pl.pallas_call(functools.partial(send_kernel, groups, bricks), out_shape=...  27.4 us
    pallas_call x1, Pallas kernels, shards(): pl.pallas_call(pair_kernel, out_shape=(shape(clusters, 4 * psize), shape(...  25.2 us
    pallas_call x1, Pallas kernels, shards(): pl.pallas_call(functools.partial(return_kernel, groups, bricks), out_shap...  24.6 us
    unnamed x31, local copies, waits for them, and re-layouts  8.15 us

profile of v3, /device:TPU:1, one launch (start us, length us, event | category | flops | bytes accessed | tf_op | source)
XLA Modules:
  0.0 86.1 jit_solution(15159529234418244098)
XLA Ops:
  0.6 0.0 copy-start.7
  0.6 0.0 copy-start.12
  0.7 0.0 copy-start.11
  0.7 0.0 copy-start.13
  0.7 0.6 copy-done.7
  1.3 0.0 copy-done.12
  1.3 0.0 copy-done.11
  1.3 0.0 copy-done.13
  1.3 0.0 copy-start
  1.4 1.0 %copy-done = f32[16,32,256]{2,1,0:T(8,128)S(1)} copy-done((f32[16,32,256]{2,1,0:T(8,128)S(1)}, f32[16,32,256]{2,1,0:T(8,128)}, u32[]{:S(2)}) %copy-start) | copy-done | bytes 524312
  2.4 0.0 copy-start.2
  2.4 1.0 %copy-done.2 = f32[16,32,256]{2,1,0:T(8,128)S(1)} copy-done((f32[16,32,256]{2,1,0:T(8,128)S(1)}, f32[16,32,256]{2,1,0:T(8,128)}, u32[]{:S(2)}) %copy-start.2) | copy-done | bytes 524312
  3.4 0.0 copy-start.4
  3.4 1.0 %copy-done.4 = f32[3,32768]{1,0:T(4,128)S(1)} copy-done((f32[3,32768]{1,0:T(4,128)S(1)}, f32[3,32768]{1,0:T(4,128)}, u32[]{:S(2)}) %copy-start.4) | copy-done | bytes 393240
  4.5 0.0 copy-start.5
  4.5 1.0 %copy-done.5 = f32[16,32,256]{2,1,0:T(8,128)S(1)} copy-done((f32[16,32,256]{2,1,0:T(8,128)S(1)}, f32[16,32,256]{2,1,0:T(8,128)}, u32[]{:S(2)}) %copy-start.5) | copy-done | bytes 524312
  5.5 0.0 copy-start.6
  5.5 0.9 %copy-done.6 = f32[32768]{0:T(1024)S(1)} copy-done((f32[32768]{0:T(1024)S(1)}, f32[32768]{0:T(1024)}, u32[]{:S(2)}) %copy-start.6) | copy-done | bytes 131096
  6.4 0.0 copy-start.8
  6.4 0.0 copy-start.9
  6.4 27.4 %send.1 = (f32[256,512]{1,0:T(8,128)S(1)}, f32[224,512]{1,0:T(8,128)S(1)}, f32[16,32,256]{2,1,0:T(8,128)S(1)}, f32[16,32,256]{2,1,0:T(8,128)S(1)}, f32[16,32,256]{2,1,0:T(8,128)S(1)}) custom-call(s32[1,7]{1,0:T(1,128)S(1)} %copy-done.13, f32[256,3,128]{2,1,0:T(4,128)S(1)} %bitcast.13, f32[256,128]{1,0:T(8,128)S(1)} %bitcast.14, s32[2,128]{1,0:T(2,128)S(1)} %bitcast.20, ...), custom_call_target="tpu_custom_call" | custom-call | tf_op jit(solution)/shard_map/send/pallas_call | solution.py:653
  33.9 0.0 copy-start.1
  33.9 0.0 copy-done.8
  33.9 0.0 copy-done.9
  33.9 0.0 copy-done.10
  33.9 25.2 %pairs.1 = (f32[256,512]{1,0:T(8,128)S(1)}, f32[224,384]{1,0:T(8,128)S(1)}) custom-call(s32[8,128]{1,0:T(8,128)S(1)} %bitcast.15, s32[8,128]{1,0:T(8,128)S(1)} %bitcast.16, s32[8,128]{1,0:T(8,128)S(1)} %bitcast.17, f32[256,512]{1,0:T(8,128)S(1)} %get-tuple-element.13.data_ref, f32[224,512]{1,0:T(8,128)S(1)} %get-tuple-element.14.arrived_ref), custom_call_target="tpu_custom_call" | custom-call | tf_op jit(solution)/shard_map/pairs/pallas_call | solution.py:697
  59.2 0.0 copy-done.3
  59.2 0.0 copy-done.1
  59.2 24.6 %back.1 = (f32[256,3,128]{2,1,0:T(4,128)S(1)}, f32[16,32,256]{2,1,0:T(8,128)S(1)}, f32[16,32,256]{2,1,0:T(8,128)S(1)}) custom-call(s32[2,128]{1,0:T(2,128)S(1)} %bitcast.19, s32[7,32]{1,0:T(8,128)S(1)} %copy-done.7, f32[16,32,256]{2,1,0:T(8,128)S(1)} %copy-done.1, f32[16,32,256]{2,1,0:T(8,128)S(1)} %copy-done.3, f32[256,512]{1,0:T(8,128)S(1)} %get-tuple-element.13.data_ref, ...), custom_call_target="tpu_custom_call" | custom-call | tf_op jit(solution)/shard_map/back/pallas_call | solution.py:715
  83.7 0.8 copy.18
  84.5 0.8 copy.19
  85.3 0.8 copy.20
  (2 shorter events, 0.0 us)
Async XLA Ops:
  0.6 0.7 copy-start.7
  0.6 0.7 copy-start.12
  0.7 0.7 copy-start.11
  0.7 0.7 copy-start.13
  1.3 1.0 %copy-start = (f32[16,32,256]{2,1,0:T(8,128)S(1)}, f32[16,32,256]{2,1,0:T(8,128)}, u32[]{:S(2)}) copy-start(f32[16,32,256]{2,1,0:T(8,128)} %ion_hbm.3) | copy-start | bytes 1572868
  2.4 1.0 %copy-start.2 = (f32[16,32,256]{2,1,0:T(8,128)S(1)}, f32[16,32,256]{2,1,0:T(8,128)}, u32[]{:S(2)}) copy-start(f32[16,32,256]{2,1,0:T(8,128)} %screen_hbm.3) | copy-start | bytes 1572868
  3.4 1.0 %copy-start.4 = (f32[3,32768]{1,0:T(4,128)S(1)}, f32[3,32768]{1,0:T(4,128)}, u32[]{:S(2)}) copy-start(f32[3,32768]{1,0:T(4,128)} %param.12) | copy-start | bytes 1179652
  4.5 1.0 %copy-start.5 = (f32[16,32,256]{2,1,0:T(8,128)S(1)}, f32[16,32,256]{2,1,0:T(8,128)}, u32[]{:S(2)}) copy-start(f32[16,32,256]{2,1,0:T(8,128)} %prev_hbm.1) | copy-start | bytes 1572868
  5.5 0.9 %copy-start.6 = (f32[32768]{0:T(1024)S(1)}, f32[32768]{0:T(1024)}, u32[]{:S(2)}) copy-start(f32[32768]{0:T(1024)} %param.13) | copy-start | bytes 393220
  6.4 27.4 %copy-start.8 = (s32[1024]{0:T(1024)S(1)}, s32[1024]{0:T(1024)}, u32[]{:S(2)}) copy-start(s32[1024]{0:T(1024)} %param.18) | copy-start | bytes 12292
  6.4 27.5 %copy-start.9 = (s32[1024]{0:T(1024)S(1)}, s32[1024]{0:T(1024)}, u32[]{:S(2)}) copy-start(s32[1024]{0:T(1024)} %param.19) | copy-start | bytes 12292
  6.4 27.5 %copy-start.10 = (s32[1024]{0:T(1024)S(1)}, s32[1024]{0:T(1024)}, u32[]{:S(2)}) copy-start(s32[1024]{0:T(1024)} %param.20) | copy-start | bytes 12292
  6.4 52.7 %copy-start.3 = (f32[16,32,256]{2,1,0:T(8,128)S(1)}, f32[16,32,256]{2,1,0:T(8,128)}, u32[]{:S(2)}) copy-start(f32[16,32,256]{2,1,0:T(8,128)} %screen_hbm.3) | copy-start | bytes 1572868
  33.9 25.3 %copy-start.1 = (f32[16,32,256]{2,1,0:T(8,128)S(1)}, f32[16,32,256]{2,1,0:T(8,128)}, u32[]{:S(2)}) copy-start(f32[16,32,256]{2,1,0:T(8,128)} %ion_hbm.3) | copy-start | bytes 1572868

commit v4 on v3

--- a/solution.py
+++ b/solution.py
@@ -111,28 +111,29 @@
     )
 
 
-def start_halos(fields, turn, x_out, x_in, y_out, y_in, send, recv, groups, bricks):
+def start_halos(axis, fields, turn, x_out, x_in, y_out, y_in, send, recv, groups, bricks):
     nx, ny = fields[0].shape[0] - 2, fields[0].shape[1] - 2 * TOP
+    out, into = (y_out, y_in) if axis else (x_out, x_in)
     for f, field in enumerate(fields):
-        y_out[turn, 0, f] = field[1 : nx + 1, TOP, :]
-        y_out[turn, 1, f] = field[1 : nx + 1, TOP + ny - 1, :]
-        x_out[turn, 0, f] = field[1, TOP : TOP + ny, :]
-        x_out[turn, 1, f] = field[nx, TOP : TOP + ny, :]
-    count = len(fields)
+        if axis:
+            out[turn, 0, f] = field[1 : nx + 1, TOP, :]
+            out[turn, 1, f] = field[1 : nx + 1, TOP + ny - 1, :]
+        else:
+            out[turn, 0, f] = field[1, TOP : TOP + ny, :]
+            out[turn, 1, f] = field[nx, TOP : TOP + ny, :]
     copies = []
     for side in range(2):
         step = 2 * side - 1
-        for axis, (out, into) in enumerate(((x_out, x_in), (y_out, y_in))):
-            copy = pltpu.make_async_remote_copy(
-                src_ref=out.at[turn, side, pl.ds(0, count)],
-                dst_ref=into.at[turn, 1 - side, pl.ds(0, count)],
-                send_sem=send.at[turn, 2 * axis + side],
-                recv_sem=recv.at[turn, 2 * axis + 1 - side],
-                device_id=neighbour(step * (1 - axis), step * axis, groups, bricks),
-                device_id_type=MESH,
-            )
-            copy.start()
-            copies.append(copy)
+        copy = pltpu.make_async_remote_copy(
+            src_ref=out.at[turn, side, pl.ds(0, len(fields))],
+            dst_ref=into.at[turn, 1 - side, pl.ds(0, len(fields))],
+            send_sem=send.at[turn, 2 * axis + side],
+            recv_sem=recv.at[turn, 2 * axis + 1 - side],
+            device_id=neighbour(step * (1 - axis), step * axis, groups, bricks),
+            device_id_type=MESH,
+        )
+        copy.start()
+        copies.append(copy)
     return copies
 
 
@@ -178,7 +179,7 @@
     return table
 
 
-def sweep(turn, held, other, resid, screen, total):
+def sweep(turn, held, other, resid, screen, total, between, whole=False):
     keep, gain = weights()[turn]
     nx, ny, nz = resid.shape
 
@@ -190,13 +191,18 @@
         update = gain * (rest / diag)
         if turn:
             update = keep * centre + update
-            total[i] = total[i] + update
+            done = total[i] + update
         else:
-            total[i] = centre + update
-        other[i + 1, TOP : TOP + ny, :] = update
+            done = centre + update
+        total[i] = done
+        other[i + 1, TOP : TOP + ny, :] = done if whole else update
         return carry
 
-    lax.fori_loop(0, nx, plane, 0, unroll=2)
+    plane(0, 0)
+    plane(nx - 1, 0)
+    result = between()
+    lax.fori_loop(1, nx - 1, plane, 0, unroll=2)
+    return result
 
 
 def cell_tables(cell_ref, nx, ny, nz):
@@ -224,6 +230,9 @@
     fill_hbm,
     cell_hbm,
     index_hbm,
+    local_hbm,
+    dir_hbm,
+    slot_hbm,
     ion_hbm,
     prev_hbm,
     screen_hbm,
@@ -232,11 +241,17 @@
     update_ref,
     resid_ref,
     total_ref,
+    into_ref,
+    depth_ref,
+    order_ref,
     pos,
     charges,
     fill,
     cells,
     index,
+    pair_local,
+    pair_dir,
+    pair_slot,
     screen,
     out_rows,
     in_rows,
@@ -264,6 +279,9 @@
                 (charge_hbm, charges),
                 (ion_hbm, resid_ref),
                 (screen_hbm, screen),
+                (local_hbm, pair_local),
+                (dir_hbm, pair_dir),
+                (slot_hbm, pair_slot),
             )
         )
     ]
@@ -289,7 +307,7 @@
         data_ref[:, d * 128 : (d + 1) * 128] = pos[:, d, :]
     data_ref[:, 384:512] = charge
     pl.semaphore_wait(barrier, len(OFFSETS) - 1)
-    halos = start_halos([pad.at[0]], 0, *exchange)
+    halos = start_halos(0, [pad.at[0]], 0, *exchange) + start_halos(1, [pad.at[0]], 0, *exchange)
     out_rows[...] = select_rows(chooser, data_ref[...], ((0,), (0,)))
     slot_id = lax.broadcasted_iota(I32, (slots, 128), 0)
     for k in range(len(OFFSETS)):
@@ -299,49 +317,62 @@
         )
     sends = send_rows(out_rows, in_rows, -1, row_send, row_recv, groups, bricks)
     into, at_depth = cell_tables(cells, nx, ny, nz)
+    into_ref[...] = into
+    depth_ref[...] = at_depth
     deposit = select_rows(into, at_depth * jnp.sum(charge, axis=1, keepdims=True))
     resid_ref[...] = resid_ref[...] + deposit_scale * deposit.reshape(nx, ny, nz)
     for turn in range(EARLY):
         held, other = pad.at[turn % 2], pad.at[1 - turn % 2]
-        if turn:
-            halos = start_halos([held], turn, *exchange)
+        if turn == EARLY - 1:
+            for copy in sends:
+                copy.wait()
+            arrived_ref[0:slots, :] = out_rows[0:slots, :]
+            arrived_ref[slots:, :] = in_rows[slots:, :]
+            sort_pairs(
+                pair_local,
+                pair_dir[...] * slots + pair_slot[...],
+                extent(data_ref),
+                extent(arrived_ref),
+                order_ref,
+            )
         finish_halos(halos, [held], turn, x_in, y_in, inside)
-        sweep(turn, held, other, resid_ref, screen, total_ref)
+        if turn + 1 < EARLY:
+            halos = sweep(
+                turn,
+                held,
+                other,
+                resid_ref,
+                screen,
+                total_ref,
+                lambda turn=turn, other=other: start_halos(0, [other], turn + 1, *exchange),
+            )
+            halos = halos + start_halos(1, [other], turn + 1, *exchange)
+        else:
+            sweep(turn, held, other, resid_ref, screen, total_ref, lambda: None)
     update_ref[...] = pad[EARLY % 2, 1 : nx + 1, TOP : TOP + ny, :]
-    for copy in sends:
-        copy.wait()
-    arrived_ref[0:slots, :] = out_rows[0:slots, :]
-    arrived_ref[slots:, :] = in_rows[slots:, :]
-
-
-def return_kernel(
+
+
+def back_kernel(
     groups,
     bricks,
-    cell_hbm,
-    index_hbm,
     ion_hbm,
     screen_hbm,
-    data_ref,
-    own_ref,
     part_ref,
     update_ref,
     resid_ref,
     total_ref,
-    force_ref,
+    back_ref,
     pot_ref,
-    next_ref,
-    cells,
-    index,
+    ion_ref,
     screen,
     back,
     resid,
+    total,
     x_out,
     x_in,
     y_out,
     y_in,
     pad,
-    ion,
-    efield,
     load,
     row_send,
     row_recv,
@@ -350,48 +381,78 @@
 ):
     nx, ny, nz = ion_hbm.shape
     loads = [
-        pltpu.make_async_copy(src, dst, load.at[i])
-        for i, (src, dst) in enumerate(
-            (
-                (ion_hbm, ion.at[pl.ds(1, nx), pl.ds(TOP, ny), :]),
-                (screen_hbm, screen),
-                (index_hbm, index),
-                (cell_hbm, cells),
-            )
-        )
+        pltpu.make_async_copy(
+            ion_hbm, ion_ref.at[pl.ds(1, nx), pl.ds(TOP, ny), :], load.at[0]
+        ),
+        pltpu.make_async_copy(screen_hbm, screen, load.at[1]),
     ]
     for copy in loads:
         copy.start()
     barrier = greet(groups, bricks)
     inside = inside_flags(groups, bricks)
-    pad[EARLY % 2, 1 : nx + 1, TOP : TOP + ny, :] = update_ref[...]
-    resid[...] = resid_ref[...]
-    pot_ref[...] = total_ref[...]
+    first = pad.at[EARLY % 2]
+    first[1 : nx + 1, TOP : TOP + ny, :] = update_ref[...]
     for copy in loads:
         copy.wait()
     exchange = (x_out, x_in, y_out, y_in, halo_send, halo_recv, groups, bricks)
     pl.semaphore_wait(barrier, len(OFFSETS) - 1)
-    halos = start_halos([pad.at[EARLY % 2], ion], 0, *exchange)
+    halos = start_halos(0, [first, ion_ref], 0, *exchange)
+    halos = halos + start_halos(1, [first, ion_ref], 0, *exchange)
     sends = send_rows(part_ref, back, 1, row_send, row_recv, groups, bricks)
-    clusters = data_ref.shape[0]
-    slots = index.shape[1]
-    back[0:slots, :] = part_ref[0:slots, :]
-    wanted = slot_row(index)
-    chooser = jnp.where(
-        lax.broadcasted_iota(I32, (clusters, wanted.shape[1]), 0) == wanted, 1.0, 0.0
-    ).astype(BF16)
-    into, at_depth = cell_tables(cells, nx, ny, nz)
+    resid[...] = resid_ref[...]
+    total[...] = total_ref[...]
+    slots = part_ref.shape[0] // len(OFFSETS)
+    back_ref[0:slots, :] = part_ref[0:slots, :]
     for turn in range(EARLY, SWEEPS):
         held, other = pad.at[turn % 2], pad.at[1 - turn % 2]
-        fields = [held, ion] if turn == EARLY else [held]
-        if turn > EARLY:
-            halos = start_halos(fields, turn - EARLY, *exchange)
+        fields = [held, ion_ref] if turn == EARLY else [held]
+        last = turn == SWEEPS - 1
+        other = pot_ref if last else other
         finish_halos(halos, fields, turn - EARLY, x_in, y_in, inside)
-        sweep(turn, held, other, resid, screen, pot_ref)
-    pot = pad.at[SWEEPS % 2]
-    pot[1 : nx + 1, TOP : TOP + ny, :] = pot_ref[...]
-    halos = start_halos([pot], SWEEPS - EARLY, *exchange)
-    finish_halos(halos, [pot], SWEEPS - EARLY, x_in, y_in, inside)
+        halos = sweep(
+            turn,
+            held,
+            other,
+            resid,
+            screen,
+            total,
+            lambda turn=turn, other=other: start_halos(0, [other], turn + 1 - EARLY, *exchange),
+            last,
+        )
+        halos = halos + start_halos(1, [other], turn + 1 - EARLY, *exchange)
+    for copy in sends:
+        copy.wait()
+    back_ref[slots:, :] = back[slots:, :]
+    finish_halos(halos, [pot_ref], SWEEPS - EARLY, x_in, y_in, inside)
+
+
+def final_kernel(
+    index_hbm,
+    data_ref,
+    own_ref,
+    back_ref,
+    pot,
+    ion,
+    into_ref,
+    depth_ref,
+    force_hbm,
+    pot_hbm,
+    next_hbm,
+    force,
+    after,
+    efield,
+    index,
+    store,
+):
+    nx, ny, nz = pot_hbm.shape
+    out = [
+        pltpu.make_async_copy(pot.at[pl.ds(1, nx), pl.ds(TOP, ny), :], pot_hbm, store.at[0]),
+        pltpu.make_async_copy(after, next_hbm, store.at[1]),
+        pltpu.make_async_copy(force, force_hbm, store.at[2]),
+    ]
+    fetch = pltpu.make_async_copy(index_hbm, index, store.at[3])
+    fetch.start()
+    out[0].start()
 
     def finish(i, carry):
         lo, hi = TOP, TOP + ny
@@ -402,26 +463,32 @@
         iy = (ion[i + 1, lo - 1 : hi - 1, :], ion[i + 1, lo + 1 : hi + 1, :])
         pz = z_shifts(p)[::-1]
         iz = z_shifts(n)[::-1]
-        out = jnp.zeros_like(p)
+        change = jnp.zeros_like(p)
         for d, (ps, ns) in enumerate(((px, ix), (py, iy), (pz, iz))):
-            out = out + (face_flux(p, ps[1], n, ns[1]) - face_flux(ps[0], p, ns[0], n))
+            change = change + (face_flux(p, ps[1], n, ns[1]) - face_flux(ps[0], p, ns[0], n))
             efield[d, pl.ds(pl.multiple_of(i * ny, ny), ny), :] = -(ps[1] - ps[0]) * 0.5
-        next_ref[i] = n - time_step * out
+        after[i] = n - time_step * change
         return carry
 
     lax.fori_loop(0, nx, finish, 0)
-    push = []
-    for d in range(3):
-        seen = select_rows(into, efield[d], ((0,), (0,)))
-        push.append(field_scale * jnp.sum(seen * at_depth, axis=1, keepdims=True))
-    for copy in sends:
-        copy.wait()
-    react = select_rows(chooser, back[...])
+    out[1].start()
+    fetch.wait()
+    wanted = slot_row(index)
+    clusters = data_ref.shape[0]
+    chooser = jnp.where(
+        lax.broadcasted_iota(I32, (clusters, wanted.shape[1]), 0) == wanted, 1.0, 0.0
+    ).astype(BF16)
+    react = select_rows(chooser, back_ref[...])
     charge = data_ref[:, 384:512]
     for d in range(3):
+        seen = select_rows(into_ref[...], efield[d], ((0,), (0,)))
+        push = field_scale * jnp.sum(seen * depth_ref[...], axis=1, keepdims=True)
         near = slice(d * 128, (d + 1) * 128)
         pull = data_ref[:, near] * own_ref[:, 0:128] - own_ref[:, (d + 1) * 128 : (d + 2) * 128]
-        force_ref[:, d, :] = charge * (coulomb_scale * pull + push[d]) + coulomb_scale * react[:, near]
+        force[:, d, :] = charge * (coulomb_scale * pull + push) + coulomb_scale * react[:, near]
+    out[2].start()
+    for copy in out:
+        copy.wait()
 
 
 def features(data, base, row_feat, lane_feat, vals):
@@ -460,7 +527,7 @@
     return jnp.max(jnp.where(charge != 0.0, lane, 0.0), axis=1, keepdims=True)
 
 
-def sort_pairs(local_ref, part_ids, own_extent, part_extent, order_vmem):
+def sort_pairs(local_ref, part_ids, own_extent, part_extent, order_ref):
     rows = local_ref.shape[0]
     clusters, partners = own_extent.shape[0], part_extent.shape[0]
     own_lines, part_lines = [], []
@@ -491,19 +558,20 @@
         lax.broadcasted_iota(I32, (rows, rows), 1) < lax.broadcasted_iota(I32, (rows, rows), 0), 1.0, 0.0
     ).astype(BF16)
     place = jnp.full((rows, 128), -1.0, F32)
-    base = jnp.int32(0)
-    spans = []
+    base = jnp.zeros((1, 1), F32)
+    lane = lax.broadcasted_iota(I32, (1, 128), 1)
+    spans = jnp.zeros((1, 128), F32)
     for blocks in ORDER:
         member = jnp.where((short > float(STEP) * (blocks - 1)) & (short <= float(STEP) * blocks), 1.0, 0.0)
         within = dot(member.astype(BF16), upto)
         total = jnp.sum(member, axis=1, keepdims=True)
         ahead = dot(before, jnp.broadcast_to(total, (rows, 128)).astype(BF16))
-        place = jnp.where(member > 0.0, base.astype(F32) + ahead + within - 1.0, place)
-        batches = (jnp.sum(member).astype(I32) + BATCH - 1) // BATCH
-        spans.append((base, batches))
+        place = jnp.where(member > 0.0, base + ahead + within - 1.0, place)
+        batches = jnp.floor((jnp.sum(total, axis=0, keepdims=True) + (BATCH - 1.0)) / BATCH)
+        spans = jnp.where(lane == len(ORDER) - blocks, batches, spans)
         base = base + batches * BATCH
     place = place.astype(I32)
-    room = order_vmem.shape[1]
+    room = order_ref.shape[1] - 1
     found = jnp.zeros((4 * room, 128), F32)
     for r in range(rows):
         at = place[r : r + 1, :]
@@ -512,9 +580,10 @@
         load = jnp.concatenate([jnp.where(ours, f[r : r + 1, :], 0.0) for f in fields], axis=0)
         found = found + dot(load.astype(BF16), here.astype(BF16), ((1,), (1,)))
     found = [found[i * room : (i + 1) * room, :] for i in range(4)]
-    order_vmem[0] = blank - (found[0] + 256.0 * found[1]).astype(I32)
-    order_vmem[1] = blank - (found[2] + 256.0 * found[3]).astype(I32)
-    return spans
+    order_ref[0, 0:room, :] = blank - (found[0] + 256.0 * found[1]).astype(I32)
+    order_ref[1, 0:room, :] = blank - (found[2] + 256.0 * found[3]).astype(I32)
+    order_ref[0, room : room + 1, :] = spans.astype(I32)
+    order_ref[1, room : room + 1, :] = spans.astype(I32)
 
 
 def distances(row_ids, lane_ids, rows, row_feat, lane_feat, dist):
@@ -558,9 +627,7 @@
 
 
 def pair_kernel(
-    local_ref,
-    dir_ref,
-    slot_ref,
+    order,
     data_ref,
     arrived_ref,
     own_ref,
@@ -570,23 +637,19 @@
     vals,
     acc,
     dist,
-    order_vmem,
-    order,
-    sem,
 ):
     clusters, partners = data_ref.shape[0], arrived_ref.shape[0]
-    slots = partners // len(OFFSETS)
-    part_ids = dir_ref[...] * slots + slot_ref[...]
-    spans = sort_pairs(
-        local_ref, part_ids, extent(data_ref[...]), extent(arrived_ref[...]), order_vmem
-    )
-    copy = pltpu.make_async_copy(order_vmem, order, sem)
-    copy.start()
     features(data_ref, 0, row_feat, lane_feat, vals)
     features(arrived_ref, clusters, row_feat, lane_feat, vals)
     feature_rows(jnp.zeros((8, 512), F32), clusters + partners, row_feat, lane_feat, vals)
     acc[...] = jnp.zeros_like(acc)
-    copy.wait()
+    room = order.shape[1] - 1
+    spans = []
+    base = 0
+    for at in range(len(ORDER)):
+        batches = order[0, room, at]
+        spans.append((base, batches))
+        base = base + batches * BATCH
     for blocks, (base, batches) in zip(ORDER, spans):
         rows = STEP * blocks
 
@@ -650,17 +713,34 @@
     padded = (nx + 2, ny + 2 * TOP, nz)
     cells = cluster_cell.reshape(clusters // 128, 128)
     late = SWEEPS + 1 - EARLY
-    data, arrived, update, resid, total = pl.pallas_call(
+    pairs = pair_local.shape[0]
+    lines = lambda v: v.reshape(pairs // 128, 128)
+    room = -(-(pairs + len(ORDER) * BATCH) // 1024) * 8
+    still = lambda v: pltpu.with_memory_space_constraint(v, pltpu.HBM)
+    ion_density, potential_prev, screening = map(still, (ion_density, potential_prev, screening))
+    data, arrived, update, resid, total, into, at_depth, order = pl.pallas_call(
         functools.partial(send_kernel, groups, bricks),
-        out_shape=(shape(clusters, 4 * psize), rows, block, block, block),
-        in_specs=[smem] + [hbm] * 8,
-        out_specs=[vmem] * 5,
+        out_shape=(
+            shape(clusters, 4 * psize),
+            rows,
+            block,
+            block,
+            block,
+            jax.ShapeDtypeStruct((nx * ny, clusters), BF16),
+            shape(clusters, nz),
+            jax.ShapeDtypeStruct((2, room + 1, 128), I32),
+        ),
+        in_specs=[smem] + [hbm] * 11,
+        out_specs=[vmem] * 8,
         scratch_shapes=[
             pltpu.VMEM((clusters, 3, psize), F32),
             pltpu.VMEM((clusters, psize), F32),
             pltpu.VMEM((clusters // 128, 128), I32),
             pltpu.VMEM((clusters // 128, 128), I32),
             pltpu.VMEM((dirs, slots), I32),
+            pltpu.VMEM((pairs // 128, 128), I32),
+            pltpu.VMEM((pairs // 128, 128), I32),
+            pltpu.VMEM((pairs // 128, 128), I32),
             pltpu.VMEM((nx, ny, nz), F32),
             pltpu.VMEM((dirs * slots, 4 * psize), F32),
             pltpu.VMEM((dirs * slots, 4 * psize), F32),
@@ -669,7 +749,7 @@
             halo(EARLY, 1, nx),
             halo(EARLY, 1, nx),
             pltpu.VMEM((2, *padded), F32),
-            pltpu.SemaphoreType.DMA((8,)),
+            pltpu.SemaphoreType.DMA((11,)),
             pltpu.SemaphoreType.DMA((dirs - 1,)),
             pltpu.SemaphoreType.DMA((dirs - 1,)),
             pltpu.SemaphoreType.DMA((EARLY, 4)),
@@ -680,24 +760,24 @@
         ),
         name="send",
     )(
-        send_count,
-        placed,
-        charges.reshape(clusters, psize),
-        cluster_fill.reshape(clusters // 128, 128),
-        cells,
-        send_index,
+        still(send_count),
+        still(placed),
+        still(charges.reshape(clusters, psize)),
+        still(cluster_fill.reshape(clusters // 128, 128)),
+        still(cells),
+        still(send_index),
+        still(lines(pair_local)),
+        still(lines(pair_dir)),
+        still(lines(pair_slot)),
         ion_density,
         potential_prev,
         screening,
     )
-    pairs = pair_local.shape[0]
     table = (clusters + dirs * slots + 8,)
-    room = -(-(pairs + len(ORDER) * BATCH) // 1024) * 8
-    lines = lambda v: v.reshape(pairs // 128, 128)
     own_sums, part_sums = pl.pallas_call(
         pair_kernel,
         out_shape=(shape(clusters, 4 * psize), shape(dirs * slots, 3 * psize)),
-        in_specs=[vmem] * 5,
+        in_specs=[smem] + [vmem] * 2,
         out_specs=[vmem] * 2,
         scratch_shapes=[
             pltpu.VMEM((*table, 24, psize), F32),
@@ -705,32 +785,27 @@
             pltpu.VMEM((*table, 16, psize), F32),
             pltpu.VMEM((*table, 16, psize), F32),
             pltpu.VMEM((BATCH // 2, psize, 2 * psize), F32),
-            pltpu.VMEM((2, room, 128), I32),
-            pltpu.SMEM((2, room, 128), I32),
-            pltpu.SemaphoreType.DMA(()),
         ],
-        compiler_params=pltpu.CompilerParams(vmem_limit_bytes=48 << 20),
+        compiler_params=pltpu.CompilerParams(vmem_limit_bytes=40 << 20),
         name="pairs",
-    )(lines(pair_local), lines(pair_dir), lines(pair_slot), data, arrived)
-    forces, potential, ion_next = pl.pallas_call(
-        functools.partial(return_kernel, groups, bricks),
-        out_shape=(shape(clusters, 3, psize), block, block),
-        in_specs=[hbm] * 4 + [vmem] * 6,
+    )(order, data, arrived)
+    padding = shape(*padded)
+    back, pot, ion = pl.pallas_call(
+        functools.partial(back_kernel, groups, bricks),
+        out_shape=(shape(dirs * slots, 3 * psize), padding, padding),
+        in_specs=[hbm] * 2 + [vmem] * 4,
         out_specs=[vmem] * 3,
         scratch_shapes=[
-            pltpu.VMEM((clusters // 128, 128), I32),
-            pltpu.VMEM((dirs, slots), I32),
             pltpu.VMEM((nx, ny, nz), F32),
             pltpu.VMEM((dirs * slots, 3 * psize), F32),
+            pltpu.VMEM((nx, ny, nz), F32),
             pltpu.VMEM((nx, ny, nz), F32),
             halo(late, 2, ny),
             halo(late, 2, ny),
             halo(late, 2, nx),
             halo(late, 2, nx),
             pltpu.VMEM((2, *padded), F32),
-            pltpu.VMEM(padded, F32),
-            pltpu.VMEM((3, nx * ny, nz), F32),
-            pltpu.SemaphoreType.DMA((4,)),
+            pltpu.SemaphoreType.DMA((2,)),
             pltpu.SemaphoreType.DMA((dirs - 1,)),
             pltpu.SemaphoreType.DMA((dirs - 1,)),
             pltpu.SemaphoreType.DMA((late, 4)),
@@ -740,18 +815,22 @@
             collective_id=1, has_side_effects=True, vmem_limit_bytes=40 << 20
         ),
         name="back",
-    )(
-        cells,
-        send_index,
-        ion_density,
-        screening,
-        data,
-        own_sums,
-        part_sums,
-        update,
-        resid,
-        total,
-    )
+    )(ion_density, screening, part_sums, update, resid, total)
+    forces, potential, ion_next = pl.pallas_call(
+        final_kernel,
+        out_shape=(shape(clusters, 3, psize), block, block),
+        in_specs=[hbm] + [vmem] * 7,
+        out_specs=[hbm] * 3,
+        scratch_shapes=[
+            pltpu.VMEM((clusters, 3, psize), F32),
+            pltpu.VMEM((nx, ny, nz), F32),
+            pltpu.VMEM((3, nx * ny, nz), F32),
+            pltpu.VMEM((dirs, slots), I32),
+            pltpu.SemaphoreType.DMA((4,)),
+        ],
+        compiler_params=pltpu.CompilerParams(vmem_limit_bytes=40 << 20),
+        name="final",
+    )(still(send_index), data, own_sums, back, pot, ion, into, at_depth)
     return (forces.transpose(1, 0, 2).reshape(3, -1), potential, ion_next)
 
 

time: 87.2 us -> 77.6 us (0.89); the launches traced: 86.1 us -> 77.5 us
  local copies, waits for them, and re-layouts: 8.15 us -> 0 us
    unnamed x31 -> x0, local copies, waits for them, and re-layouts: 8.15 us -> none
    pallas_call x1, Pallas kernels: 27.4 us -> 26.3 us  [shards(): pl.pallas_call(functools.partial(send_kernel, groups, bricks), out_shape=...]
    pallas_call x1, Pallas kernels: 25.2 us -> 26.2 us  [shards(): pl.pallas_call(pair_kernel, out_shape=(shape(clusters, 4 * psize), shape(...]
    pallas_call x1 -> x2, Pallas kernels: 24.6 us -> 24.2 us  [the longest x1 19.8 us: shards(): pl.pallas_call(functools.partial(back_kernel, groups, bricks), out_shape=...]
where the time goes in v4:
time: 77.6 us; the launch traced here: 77.5 us
  Pallas kernels  76.7 us (99%)
  between operations  0.82 us (1%)
    pallas_call x1, Pallas kernels, shards(): pl.pallas_call(functools.partial(send_kernel, groups, bricks), out_shape=...  26.3 us
    pallas_call x1, Pallas kernels, shards(): pl.pallas_call(pair_kernel, out_shape=(shape(clusters, 4 * psize), shape(...  26.2 us
    pallas_call x1, Pallas kernels, shards(): pl.pallas_call(functools.partial(back_kernel, groups, bricks), out_shape=...  19.8 us
    pallas_call x1, Pallas kernels, shards(): pl.pallas_call(final_kernel, out_shape=(shape(clusters, 3, psize), block,...  4.33 us

profile of v4, /device:TPU:1, one launch (start us, length us, event | category | flops | bytes accessed | tf_op | source)
XLA Modules:
  0.0 77.5 jit_solution(4707763511513209802)
XLA Ops:
  0.6 26.3 %send.1 = (f32[256,512]{1,0:T(8,128)S(1)}, f32[224,512]{1,0:T(8,128)S(1)}, f32[16,32,256]{2,1,0:T(8,128)S(1)}, f32[16,32,256]{2,1,0:T(8,128)S(1)}, f32[16,32,256...) custom-call(s32[1,7]{1,0:T(1,128)} %count_ref.1, ...), custom_call_target="tpu_custom_call" | custom-call | tf_op jit(solution)/shard_map/send/pallas_call | solution.py:721
  27.0 26.2 %pairs.1 = (f32[256,512]{1,0:T(8,128)S(1)}, f32[224,384]{1,0:T(8,128)S(1)}) custom-call(s32[2,17,128]{2,1,0:T(8,128)S(1)} %get-tuple-element.20.order, f32[256,512]{1,0:T(8,128)S(1)} %get-tuple-element.19.data_ref, f32[224,512]{1,0:T(8,128)S(1)} %get-tuple-element.21.arrived_ref), custom_call_target="tpu_custom_call" | custom-call | tf_op jit(solution)/shard_map/pairs/pallas_call | solution.py:777
  53.2 19.8 %back.1 = (f32[224,384]{1,0:T(8,128)S(1)}, f32[18,48,256]{2,1,0:T(8,128)S(1)}, f32[18,48,256]{2,1,0:T(8,128)S(1)}) custom-call(f32[16,32,256]{2,1,0:T(8,128)} %ion_hbm.3, f32[16,32,256]{2,1,0:T(8,128)} %screen_hbm.3, f32[224,384]{1,0:T(8,128)S(1)} %get-tuple-element.23.part_ref, f32[16,32,256]{2,1,0:T(8,128)S(1)} %get-tuple-element.24.update_ref, ...), custom_call_target="tpu_custom_call" | custom-call | tf_op jit(solution)/shard_map/back/pallas_call | solution.py:793
  73.0 4.3 %final.1 = (f32[256,3,128]{2,1,0:T(4,128)}, f32[16,32,256]{2,1,0:T(8,128)}, f32[16,32,256]{2,1,0:T(8,128)}) custom-call(s32[7,32]{1,0:T(8,128)} %index_hbm.3, f32[256,512]{1,0:T(8,128)S(1)} %get-tuple-element.19.data_ref, f32[256,512]{1,0:T(8,128)S(1)} %get-tuple-element.22.own_ref, f32[224,384]{1,0:T(8,128)S(1)} %get-tuple-element.27.back_ref, ...), custom_call_target="tpu_custom_call" | custom-call | tf_op jit(solution)/shard_map/final/pallas_call | solution.py:819

commit v5 on v4

--- a/solution.py
+++ b/solution.py
@@ -137,15 +137,22 @@
     return copies
 
 
-def finish_halos(copies, fields, turn, x_in, y_in, inside):
-    for copy in copies:
-        copy.wait()
-    nx, ny = fields[0].shape[0] - 2, fields[0].shape[1] - 2 * TOP
-    for f, field in enumerate(fields):
-        field[0, TOP : TOP + ny, :] = x_in[turn, 0, f] * inside[0]
-        field[nx + 1, TOP : TOP + ny, :] = x_in[turn, 1, f] * inside[1]
-        field[1 : nx + 1, TOP - 1, :] = y_in[turn, 0, f] * inside[2]
-        field[1 : nx + 1, TOP + ny, :] = y_in[turn, 1, f] * inside[3]
+def place_halos(field, at, x_in, y_in, inside):
+    nx, ny = field.shape[0] - 2, field.shape[1] - 2 * TOP
+    field[0, TOP : TOP + ny, :] = x_in[at[0], 0, at[1]] * inside[0]
+    field[nx + 1, TOP : TOP + ny, :] = x_in[at[0], 1, at[1]] * inside[1]
+    field[1 : nx + 1, TOP - 1, :] = y_in[at[0], 0, at[1]] * inside[2]
+    field[1 : nx + 1, TOP + ny, :] = y_in[at[0], 1, at[1]] * inside[3]
+
+
+def clear_halos(field):
+    nx, ny = field.shape[0] - 2, field.shape[1] - 2 * TOP
+    edge = jnp.zeros(field.shape[1:], F32)
+    field[0] = edge
+    field[nx + 1] = edge
+    for i in range(1, nx + 1):
+        field[i, 0:TOP, :] = edge[:TOP]
+        field[i, TOP + ny :, :] = edge[:TOP]
 
 
 def send_rows(source, target, towards, send, recv, groups, bricks):
@@ -179,7 +186,7 @@
     return table
 
 
-def sweep(turn, held, other, resid, screen, total, between, whole=False):
+def sweep(turn, held, other, resid, screen, total, whole=False):
     keep, gain = weights()[turn]
     nx, ny, nz = resid.shape
 
@@ -198,11 +205,26 @@
         other[i + 1, TOP : TOP + ny, :] = done if whole else update
         return carry
 
-    plane(0, 0)
-    plane(nx - 1, 0)
-    result = between()
-    lax.fori_loop(1, nx - 1, plane, 0, unroll=2)
-    return result
+    lax.fori_loop(0, nx, plane, 0, unroll=2)
+
+
+def add_halos(turn, at, other, resid, screen, total, x_in, y_in, inside):
+    gain = weights()[turn][1]
+    nx, ny, nz = resid.shape
+    for side in range(2):
+        i = side * (nx - 1)
+        halo = x_in[at, side, 0] * inside[side]
+        step = gain * (halo / (6.0 + screen[i]))
+        resid[i] = resid[i] + halo
+        total[i] = total[i] + step
+        other[i + 1, TOP : TOP + ny, :] = other[i + 1, TOP : TOP + ny, :] + step
+    for side in range(2):
+        j = side * (ny - 1)
+        halo = y_in[at, side, 0] * inside[2 + side]
+        step = gain * (halo / (6.0 + screen[:, j, :]))
+        resid[:, j, :] = resid[:, j, :] + halo
+        total[:, j, :] = total[:, j, :] + step
+        other[1 : nx + 1, TOP + j, :] = other[1 : nx + 1, TOP + j, :] + step
 
 
 def cell_tables(cell_ref, nx, ny, nz):
@@ -244,6 +266,9 @@
     into_ref,
     depth_ref,
     order_ref,
+    row_feat,
+    lane_feat,
+    vals,
     pos,
     charges,
     fill,
@@ -289,6 +314,8 @@
         copy.start()
     barrier = greet(groups, bricks)
     inside = inside_flags(groups, bricks)
+    clear_halos(pad.at[0])
+    clear_halos(pad.at[1])
     for copy in loads[:4]:
         copy.wait()
     exchange = (x_out, x_in, y_out, y_in, halo_send, halo_recv, groups, bricks)
@@ -323,6 +350,8 @@
     resid_ref[...] = resid_ref[...] + deposit_scale * deposit.reshape(nx, ny, nz)
     for turn in range(EARLY):
         held, other = pad.at[turn % 2], pad.at[1 - turn % 2]
+        if turn == EARLY - 2:
+            features(data_ref, 0, row_feat, lane_feat, vals)
         if turn == EARLY - 1:
             for copy in sends:
                 copy.wait()
@@ -335,35 +364,35 @@
                 extent(arrived_ref),
                 order_ref,
             )
-        finish_halos(halos, [held], turn, x_in, y_in, inside)
+            partners = arrived_ref.shape[0]
+            features(arrived_ref, clusters, row_feat, lane_feat, vals)
+            feature_rows(jnp.zeros((8, 512), F32), clusters + partners, row_feat, lane_feat, vals)
+        sweep(turn, held, other, resid_ref, screen, total_ref)
+        for copy in halos:
+            copy.wait()
+        add_halos(turn, turn, other, resid_ref, screen, total_ref, x_in, y_in, inside)
         if turn + 1 < EARLY:
-            halos = sweep(
-                turn,
-                held,
-                other,
-                resid_ref,
-                screen,
-                total_ref,
-                lambda turn=turn, other=other: start_halos(0, [other], turn + 1, *exchange),
-            )
+            halos = start_halos(0, [other], turn + 1, *exchange)
             halos = halos + start_halos(1, [other], turn + 1, *exchange)
-        else:
-            sweep(turn, held, other, resid_ref, screen, total_ref, lambda: None)
     update_ref[...] = pad[EARLY % 2, 1 : nx + 1, TOP : TOP + ny, :]
 
 
 def back_kernel(
     groups,
     bricks,
+    index_hbm,
     ion_hbm,
     screen_hbm,
+    data_ref,
+    own_ref,
     part_ref,
     update_ref,
     resid_ref,
     total_ref,
-    back_ref,
+    pull_ref,
     pot_ref,
     ion_ref,
+    index,
     screen,
     back,
     resid,
@@ -385,12 +414,15 @@
             ion_hbm, ion_ref.at[pl.ds(1, nx), pl.ds(TOP, ny), :], load.at[0]
         ),
         pltpu.make_async_copy(screen_hbm, screen, load.at[1]),
+        pltpu.make_async_copy(index_hbm, index, load.at[2]),
     ]
     for copy in loads:
         copy.start()
     barrier = greet(groups, bricks)
     inside = inside_flags(groups, bricks)
     first = pad.at[EARLY % 2]
+    clear_halos(pad.at[0])
+    clear_halos(pad.at[1])
     first[1 : nx + 1, TOP : TOP + ny, :] = update_ref[...]
     for copy in loads:
         copy.wait()
@@ -402,35 +434,39 @@
     resid[...] = resid_ref[...]
     total[...] = total_ref[...]
     slots = part_ref.shape[0] // len(OFFSETS)
-    back_ref[0:slots, :] = part_ref[0:slots, :]
+    back[0:slots, :] = part_ref[0:slots, :]
+    wanted = slot_row(index)
+    clusters = data_ref.shape[0]
+    chooser = jnp.where(
+        lax.broadcasted_iota(I32, (clusters, wanted.shape[1]), 0) == wanted, 1.0, 0.0
+    ).astype(BF16)
+    for d in range(3):
+        near = slice(d * 128, (d + 1) * 128)
+        pull = data_ref[:, near] * own_ref[:, 0:128] - own_ref[:, (d + 1) * 128 : (d + 2) * 128]
+        pull_ref[:, near] = coulomb_scale * data_ref[:, 384:512] * pull
     for turn in range(EARLY, SWEEPS):
         held, other = pad.at[turn % 2], pad.at[1 - turn % 2]
-        fields = [held, ion_ref] if turn == EARLY else [held]
         last = turn == SWEEPS - 1
         other = pot_ref if last else other
-        finish_halos(halos, fields, turn - EARLY, x_in, y_in, inside)
-        halos = sweep(
-            turn,
-            held,
-            other,
-            resid,
-            screen,
-            total,
-            lambda turn=turn, other=other: start_halos(0, [other], turn + 1 - EARLY, *exchange),
-            last,
-        )
+        sweep(turn, held, other, resid, screen, total, last)
+        for copy in halos:
+            copy.wait()
+        add_halos(turn, turn - EARLY, other, resid, screen, total, x_in, y_in, inside)
+        halos = start_halos(0, [other], turn + 1 - EARLY, *exchange)
         halos = halos + start_halos(1, [other], turn + 1 - EARLY, *exchange)
+        if turn == EARLY:
+            place_halos(ion_ref, (0, 1), x_in, y_in, inside)
     for copy in sends:
         copy.wait()
-    back_ref[slots:, :] = back[slots:, :]
-    finish_halos(halos, [pot_ref], SWEEPS - EARLY, x_in, y_in, inside)
+    pull_ref[...] = pull_ref[...] + coulomb_scale * select_rows(chooser, back[...])
+    for copy in halos:
+        copy.wait()
+    place_halos(pot_ref, (SWEEPS - EARLY, 0), x_in, y_in, inside)
 
 
 def final_kernel(
-    index_hbm,
     data_ref,
-    own_ref,
-    back_ref,
+    pull_ref,
     pot,
     ion,
     into_ref,
@@ -441,7 +477,6 @@
     force,
     after,
     efield,
-    index,
     store,
 ):
     nx, ny, nz = pot_hbm.shape
@@ -450,8 +485,6 @@
         pltpu.make_async_copy(after, next_hbm, store.at[1]),
         pltpu.make_async_copy(force, force_hbm, store.at[2]),
     ]
-    fetch = pltpu.make_async_copy(index_hbm, index, store.at[3])
-    fetch.start()
     out[0].start()
 
     def finish(i, carry):
@@ -472,20 +505,11 @@
 
     lax.fori_loop(0, nx, finish, 0)
     out[1].start()
-    fetch.wait()
-    wanted = slot_row(index)
-    clusters = data_ref.shape[0]
-    chooser = jnp.where(
-        lax.broadcasted_iota(I32, (clusters, wanted.shape[1]), 0) == wanted, 1.0, 0.0
-    ).astype(BF16)
-    react = select_rows(chooser, back_ref[...])
-    charge = data_ref[:, 384:512]
+    charge = field_scale * data_ref[:, 384:512]
     for d in range(3):
-        seen = select_rows(into_ref[...], efield[d], ((0,), (0,)))
-        push = field_scale * jnp.sum(seen * depth_ref[...], axis=1, keepdims=True)
-        near = slice(d * 128, (d + 1) * 128)
-        pull = data_ref[:, near] * own_ref[:, 0:128] - own_ref[:, (d + 1) * 128 : (d + 2) * 128]
-        force[:, d, :] = charge * (coulomb_scale * pull + push) + coulomb_scale * react[:, near]
+        seen = select_rows(into_ref[...], efield[d], ((0,), (0,)), 2)
+        push = jnp.sum(seen * depth_ref[...], axis=1, keepdims=True)
+        force[:, d, :] = charge * push + pull_ref[:, d * 128 : (d + 1) * 128]
     out[2].start()
     for copy in out:
         copy.wait()
@@ -628,20 +652,16 @@
 
 def pair_kernel(
     order,
-    data_ref,
     arrived_ref,
-    own_ref,
-    part_ref,
     row_feat,
     lane_feat,
     vals,
+    own_ref,
+    part_ref,
     acc,
     dist,
 ):
-    clusters, partners = data_ref.shape[0], arrived_ref.shape[0]
-    features(data_ref, 0, row_feat, lane_feat, vals)
-    features(arrived_ref, clusters, row_feat, lane_feat, vals)
-    feature_rows(jnp.zeros((8, 512), F32), clusters + partners, row_feat, lane_feat, vals)
+    clusters, partners = own_ref.shape[0], arrived_ref.shape[0]
     acc[...] = jnp.zeros_like(acc)
     room = order.shape[1] - 1
     spans = []
@@ -713,12 +733,13 @@
     padded = (nx + 2, ny + 2 * TOP, nz)
     cells = cluster_cell.reshape(clusters // 128, 128)
     late = SWEEPS + 1 - EARLY
+    table = (clusters + dirs * slots + 8,)
     pairs = pair_local.shape[0]
     lines = lambda v: v.reshape(pairs // 128, 128)
     room = -(-(pairs + len(ORDER) * BATCH) // 1024) * 8
     still = lambda v: pltpu.with_memory_space_constraint(v, pltpu.HBM)
     ion_density, potential_prev, screening = map(still, (ion_density, potential_prev, screening))
-    data, arrived, update, resid, total, into, at_depth, order = pl.pallas_call(
+    data, arrived, update, resid, total, into, at_depth, order, *tables = pl.pallas_call(
         functools.partial(send_kernel, groups, bricks),
         out_shape=(
             shape(clusters, 4 * psize),
@@ -729,9 +750,12 @@
             jax.ShapeDtypeStruct((nx * ny, clusters), BF16),
             shape(clusters, nz),
             jax.ShapeDtypeStruct((2, room + 1, 128), I32),
+            shape(*table, 24, psize),
+            shape(*table, 24, psize),
+            shape(*table, 16, psize),
         ),
         in_specs=[smem] + [hbm] * 11,
-        out_specs=[vmem] * 8,
+        out_specs=[vmem] * 11,
         scratch_shapes=[
             pltpu.VMEM((clusters, 3, psize), F32),
             pltpu.VMEM((clusters, psize), F32),
@@ -756,7 +780,7 @@
             pltpu.SemaphoreType.DMA((EARLY, 4)),
         ],
         compiler_params=pltpu.CompilerParams(
-            collective_id=0, has_side_effects=True, vmem_limit_bytes=40 << 20
+            collective_id=0, has_side_effects=True, vmem_limit_bytes=32 << 20
         ),
         name="send",
     )(
@@ -773,29 +797,26 @@
         potential_prev,
         screening,
     )
-    table = (clusters + dirs * slots + 8,)
     own_sums, part_sums = pl.pallas_call(
         pair_kernel,
         out_shape=(shape(clusters, 4 * psize), shape(dirs * slots, 3 * psize)),
-        in_specs=[smem] + [vmem] * 2,
+        in_specs=[smem] + [vmem] * 4,
         out_specs=[vmem] * 2,
         scratch_shapes=[
-            pltpu.VMEM((*table, 24, psize), F32),
-            pltpu.VMEM((*table, 24, psize), F32),
-            pltpu.VMEM((*table, 16, psize), F32),
             pltpu.VMEM((*table, 16, psize), F32),
             pltpu.VMEM((BATCH // 2, psize, 2 * psize), F32),
         ],
-        compiler_params=pltpu.CompilerParams(vmem_limit_bytes=40 << 20),
+        compiler_params=pltpu.CompilerParams(vmem_limit_bytes=28 << 20),
         name="pairs",
-    )(order, data, arrived)
+    )(order, arrived, *tables)
     padding = shape(*padded)
-    back, pot, ion = pl.pallas_call(
+    pull, pot, ion = pl.pallas_call(
         functools.partial(back_kernel, groups, bricks),
-        out_shape=(shape(dirs * slots, 3 * psize), padding, padding),
-        in_specs=[hbm] * 2 + [vmem] * 4,
+        out_shape=(shape(clusters, 3 * psize), padding, padding),
+        in_specs=[hbm] * 3 + [vmem] * 6,
         out_specs=[vmem] * 3,
         scratch_shapes=[
+            pltpu.VMEM((dirs, slots), I32),
             pltpu.VMEM((nx, ny, nz), F32),
             pltpu.VMEM((dirs * slots, 3 * psize), F32),
             pltpu.VMEM((nx, ny, nz), F32),
@@ -805,32 +826,31 @@
             halo(late, 2, nx),
             halo(late, 2, nx),
             pltpu.VMEM((2, *padded), F32),
-            pltpu.SemaphoreType.DMA((2,)),
+            pltpu.SemaphoreType.DMA((3,)),
             pltpu.SemaphoreType.DMA((dirs - 1,)),
             pltpu.SemaphoreType.DMA((dirs - 1,)),
             pltpu.SemaphoreType.DMA((late, 4)),
             pltpu.SemaphoreType.DMA((late, 4)),
         ],
         compiler_params=pltpu.CompilerParams(
-            collective_id=1, has_side_effects=True, vmem_limit_bytes=40 << 20
+            collective_id=1, has_side_effects=True, vmem_limit_bytes=28 << 20
         ),
         name="back",
-    )(ion_density, screening, part_sums, update, resid, total)
+    )(still(send_index), ion_density, screening, data, own_sums, part_sums, update, resid, total)
     forces, potential, ion_next = pl.pallas_call(
         final_kernel,
         out_shape=(shape(clusters, 3, psize), block, block),
-        in_specs=[hbm] + [vmem] * 7,
+        in_specs=[vmem] * 6,
         out_specs=[hbm] * 3,
         scratch_shapes=[
             pltpu.VMEM((clusters, 3, psize), F32),
             pltpu.VMEM((nx, ny, nz), F32),
             pltpu.VMEM((3, nx * ny, nz), F32),
-            pltpu.VMEM((dirs, slots), I32),
-            pltpu.SemaphoreType.DMA((4,)),
+            pltpu.SemaphoreType.DMA((3,)),
         ],
-        compiler_params=pltpu.CompilerParams(vmem_limit_bytes=40 << 20),
+        compiler_params=pltpu.CompilerParams(vmem_limit_bytes=28 << 20),
         name="final",
-    )(still(send_index), data, own_sums, back, pot, ion, into, at_depth)
+    )(data, pull, pot, ion, into, at_depth)
     return (forces.transpose(1, 0, 2).reshape(3, -1), potential, ion_next)
 
 

time: 77.6 us -> 74.6 us (0.961)
  Pallas kernels: 76.7 us -> 73.6 us
    pallas_call x1, Pallas kernels: 26.2 us -> 20.4 us  [shards(): pl.pallas_call(pair_kernel, out_shape=(shape(clusters, 4 * psize), shape(...]
    pallas_call x1, Pallas kernels: 19.8 us -> 23.6 us  [shards(): pl.pallas_call(functools.partial(back_kernel, groups, bricks), out_shape=...]
where the time goes in v5:
time: 74.6 us; the launch traced here: 74.4 us
  Pallas kernels  73.6 us (99%)
  between operations  0.81 us (1%)
    pallas_call x1, Pallas kernels, shards(): pl.pallas_call(functools.partial(send_kernel, groups, bricks), out_shape=...  25.8 us
    pallas_call x1, Pallas kernels, shards(): pl.pallas_call(functools.partial(back_kernel, groups, bricks), out_shape=...  23.6 us
    pallas_call x1, Pallas kernels, shards(): pl.pallas_call(pair_kernel, out_shape=(shape(clusters, 4 * psize), shape(...  20.4 us
    pallas_call x1, Pallas kernels, shards(): pl.pallas_call(final_kernel, out_shape=(shape(clusters, 3, psize), block,...  3.77 us

profile of v5, /device:TPU:1, one launch (start us, length us, event | category | flops | bytes accessed | tf_op | source)
XLA Modules:
  0.0 74.4 jit_solution(11891142792537533741)
XLA Ops:
  0.6 25.8 %send.1 = (f32[256,512]{1,0:T(8,128)S(1)}, f32[224,512]{1,0:T(8,128)S(1)}, f32[16,32,256]{2,1,0:T(8,128)S(1)}, f32[16,32,256]{2,1,0:T(8,128)S(1)}, f32[16,32,256...) custom-call(s32[1,7]{1,0:T(1,128)} %count_ref.1, ...), custom_call_target="tpu_custom_call" | custom-call | tf_op jit(solution)/shard_map/send/pallas_call | solution.py:742
  26.5 20.4 %pairs.1 = (f32[256,512]{1,0:T(8,128)S(1)}, f32[224,384]{1,0:T(8,128)S(1)}) custom-call(s32[2,17,128]{2,1,0:T(8,128)S(1)} %get-tuple-element.23.order, f32[224,512]{1,0:T(8,128)S(1)} %get-tuple-element.24.arrived_ref, f32[488,24,128]{2,1,0:T(8,128)S(1)} %get-tuple-element.25.row_feat, f32[488,24,128]{2,1,0:T(8,128)S(1)} %get-tuple-element.26.lane_feat, ...), custom_call_target="tpu_custom_call" | custom-call | tf_op jit(solution)/shard_map/pairs/pallas_call | solution.py:800
  46.9 23.6 %back.1 = (f32[256,384]{1,0:T(8,128)S(1)}, f32[18,48,256]{2,1,0:T(8,128)S(1)}, f32[18,48,256]{2,1,0:T(8,128)S(1)}) custom-call(s32[7,32]{1,0:T(8,128)} %index_hbm.3, f32[16,32,256]{2,1,0:T(8,128)} %ion_hbm.3, f32[16,32,256]{2,1,0:T(8,128)} %screen_hbm.3, f32[256,512]{1,0:T(8,128)S(1)} %get-tuple-element.22.data_ref, ...), custom_call_target="tpu_custom_call" | custom-call | tf_op jit(solution)/shard_map/back/pallas_call | solution.py:813
  70.5 3.8 %final.1 = (f32[256,3,128]{2,1,0:T(4,128)}, f32[16,32,256]{2,1,0:T(8,128)}, f32[16,32,256]{2,1,0:T(8,128)}) custom-call(f32[256,512]{1,0:T(8,128)S(1)} %get-tuple-element.22.data_ref, f32[256,384]{1,0:T(8,128)S(1)} %get-tuple-element.33.pull_ref, f32[18,48,256]{2,1,0:T(8,128)S(1)} %get-tuple-element.34.pot, f32[18,48,256]{2,1,0:T(8,128)S(1)} %get-tuple-element.35.ion, ...), custom_call_target="tpu_custom_call" | custom-call | tf_op jit(solution)/shard_map/final/pallas_call | solution.py:840

commit v6 on v5

--- a/solution.py
+++ b/solution.py
@@ -240,7 +240,13 @@
     at_depth = jnp.where(
         lax.broadcasted_iota(I32, (clusters, nz), 1).astype(F32) == k_col, 1.0, 0.0
     )
-    return into, at_depth
+    i_line = row_line // ny
+    j_line = row_line - i_line * ny
+    edge_line = jnp.where(j_line == 0, i_line, jnp.where(j_line == ny - 1, nx + i_line, -1))
+    edge = jnp.where(
+        lax.broadcasted_iota(I32, (2 * nx, clusters), 0) == edge_line, 1.0, 0.0
+    ).astype(BF16)
+    return into, at_depth, edge
 
 
 def send_kernel(
@@ -265,6 +271,7 @@
     total_ref,
     into_ref,
     depth_ref,
+    edge_ref,
     order_ref,
     row_feat,
     lane_feat,
@@ -343,8 +350,9 @@
             out_rows[k * slots : (k + 1) * slots, 384:512] * live
         )
     sends = send_rows(out_rows, in_rows, -1, row_send, row_recv, groups, bricks)
-    into, at_depth = cell_tables(cells, nx, ny, nz)
+    into, at_depth, edge = cell_tables(cells, nx, ny, nz)
     into_ref[...] = into
+    edge_ref[...] = edge
     depth_ref[...] = at_depth
     deposit = select_rows(into, at_depth * jnp.sum(charge, axis=1, keepdims=True))
     resid_ref[...] = resid_ref[...] + deposit_scale * deposit.reshape(nx, ny, nz)
@@ -384,6 +392,8 @@
     ion_hbm,
     screen_hbm,
     data_ref,
+    into_ref,
+    depth_ref,
     own_ref,
     part_ref,
     update_ref,
@@ -397,6 +407,7 @@
     back,
     resid,
     total,
+    efield,
     x_out,
     x_in,
     y_out,
@@ -423,6 +434,7 @@
     first = pad.at[EARLY % 2]
     clear_halos(pad.at[0])
     clear_halos(pad.at[1])
+    clear_halos(pot_ref)
     first[1 : nx + 1, TOP : TOP + ny, :] = update_ref[...]
     for copy in loads:
         copy.wait()
@@ -456,6 +468,22 @@
         halos = halos + start_halos(1, [other], turn + 1 - EARLY, *exchange)
         if turn == EARLY:
             place_halos(ion_ref, (0, 1), x_in, y_in, inside)
+
+    def field(i, carry):
+        lo, hi = TOP, TOP + ny
+        above, below = z_shifts(pot_ref[i + 1, lo:hi, :])
+        spot = pl.ds(pl.multiple_of(i * ny, ny), ny)
+        efield[0, spot, :] = -(pot_ref[i + 2, lo:hi, :] - pot_ref[i, lo:hi, :]) * 0.5
+        efield[1, spot, :] = -(pot_ref[i + 1, lo + 1 : hi + 1, :] - pot_ref[i + 1, lo - 1 : hi - 1, :]) * 0.5
+        efield[2, spot, :] = -(above - below) * 0.5
+        return carry
+
+    lax.fori_loop(0, nx, field, 0, unroll=2)
+    for d in range(3):
+        seen = select_rows(into_ref[...], efield[d], ((0,), (0,)), 2)
+        push = field_scale * jnp.sum(seen * depth_ref[...], axis=1, keepdims=True)
+        near = slice(d * 128, (d + 1) * 128)
+        pull_ref[:, near] = pull_ref[:, near] + data_ref[:, 384:512] * push
     for copy in sends:
         copy.wait()
     pull_ref[...] = pull_ref[...] + coulomb_scale * select_rows(chooser, back[...])
@@ -470,22 +498,38 @@
     pot,
     ion,
     into_ref,
+    edge_ref,
     depth_ref,
     force_hbm,
     pot_hbm,
     next_hbm,
     force,
     after,
-    efield,
     store,
 ):
     nx, ny, nz = pot_hbm.shape
     out = [
         pltpu.make_async_copy(pot.at[pl.ds(1, nx), pl.ds(TOP, ny), :], pot_hbm, store.at[0]),
-        pltpu.make_async_copy(after, next_hbm, store.at[1]),
         pltpu.make_async_copy(force, force_hbm, store.at[2]),
     ]
+    half = nx // 2
+    for k in range(2):
+        span = pl.ds(k * half, half)
+        out.append(pltpu.make_async_copy(after.at[span], next_hbm.at[span], store.at[2 * k + 1]))
     out[0].start()
+
+    charge = field_scale * data_ref[:, 384:512]
+    beside = 0.5 * jnp.concatenate([pot[0, TOP : TOP + ny, :], -pot[nx + 1, TOP : TOP + ny, :]], axis=0)
+    across = 0.5 * jnp.concatenate(
+        [pot[1 : nx + 1, TOP - 1, :], -pot[1 : nx + 1, TOP + ny, :]], axis=0
+    )
+    ends = jnp.concatenate([into_ref[0:ny, :], into_ref[(nx - 1) * ny :, :]], axis=0)
+    for d, (chooser, halo) in enumerate(((ends, beside), (edge_ref[...], across))):
+        seen = select_rows(chooser, halo, ((0,), (0,)), 2)
+        push = jnp.sum(seen * depth_ref[...], axis=1, keepdims=True)
+        force[:, d, :] = charge * push + pull_ref[:, d * 128 : (d + 1) * 128]
+    force[:, 2, :] = pull_ref[:, 256:384]
+    out[1].start()
 
     def finish(i, carry):
         lo, hi = TOP, TOP + ny
@@ -497,20 +541,14 @@
         pz = z_shifts(p)[::-1]
         iz = z_shifts(n)[::-1]
         change = jnp.zeros_like(p)
-        for d, (ps, ns) in enumerate(((px, ix), (py, iy), (pz, iz))):
+        for ps, ns in ((px, ix), (py, iy), (pz, iz)):
             change = change + (face_flux(p, ps[1], n, ns[1]) - face_flux(ps[0], p, ns[0], n))
-            efield[d, pl.ds(pl.multiple_of(i * ny, ny), ny), :] = -(ps[1] - ps[0]) * 0.5
         after[i] = n - time_step * change
         return carry
 
-    lax.fori_loop(0, nx, finish, 0)
-    out[1].start()
-    charge = field_scale * data_ref[:, 384:512]
-    for d in range(3):
-        seen = select_rows(into_ref[...], efield[d], ((0,), (0,)), 2)
-        push = jnp.sum(seen * depth_ref[...], axis=1, keepdims=True)
-        force[:, d, :] = charge * push + pull_ref[:, d * 128 : (d + 1) * 128]
-    out[2].start()
+    for k in range(2):
+        lax.fori_loop(k * half, (k + 1) * half, finish, 0, unroll=2)
+        out[2 + k].start()
     for copy in out:
         copy.wait()
 
@@ -540,9 +578,11 @@
     for f in range(3):
         weighed += [part[f] for part in parts]
     weighed += [jnp.zeros_like(charge)] * 4
-    for rows, table in ((left, row_feat), (right, lane_feat), (weighed, vals)):
+    for rows, table in ((left, row_feat), (right, lane_feat)):
         for k in range(0, len(rows), 8):
             table[here, k : k + 8, :] = jnp.transpose(jnp.stack(rows[k : k + 8]), (1, 0, 2))
+    halves = [jnp.transpose(jnp.stack(weighed[k : k + 8]), (1, 0, 2)) for k in (0, 8)]
+    vals[here] = jnp.concatenate(halves, axis=1).astype(BF16)
 
 
 def extent(data):
@@ -633,8 +673,8 @@
         u = root * root * root
         high = u.astype(BF16)
         low = (u - high.astype(F32)).astype(BF16)
-        mine = vals[row_ids[j]][:, :rows].astype(BF16)
-        theirs = vals[lane_ids[j]].astype(BF16)
+        mine = vals[row_ids[j]][:, :rows]
+        theirs = vals[lane_ids[j]]
         if rows == 128:
             on_lane = dot(jnp.concatenate([mine, mine], axis=1), jnp.concatenate([high, low], axis=0))
         else:
@@ -689,17 +729,26 @@
                 tile_sums(*now, rows, dist, vals, acc)
                 distances(*ahead, rows, row_feat, lane_feat, dist)
 
-    def total(base, count, c):
-        here = pl.ds(base, count)
-        return acc[here, c, :] + (acc[here, 4 + c, :] + acc[here, 8 + c, :])
-
-    for c in range(4):
-        own_ref[:, c * 128 : (c + 1) * 128] = total(0, clusters, c)
-    charge = arrived_ref[:, 384:512]
-    whole = total(clusters, partners, 0)
-    for d in range(3):
-        near = slice(d * 128, (d + 1) * 128)
-        part_ref[:, near] = charge * (arrived_ref[:, near] * whole - total(clusters, partners, d + 1))
+    def totals(first):
+        parts = [
+            jnp.transpose(acc[pl.ds(first, 8), f : f + 8, :], (1, 0, 2)) for f in (0, 8)
+        ]
+        return [parts[0][c] + (parts[0][4 + c] + parts[1][c]) for c in range(4)]
+
+    @pl.loop(0, clusters // 8, unroll=4)
+    def _(g):
+        at = pl.multiple_of(g * 8, 8)
+        for c, total in enumerate(totals(at)):
+            own_ref[pl.ds(at, 8), c * 128 : (c + 1) * 128] = total
+
+    @pl.loop(0, partners // 8, unroll=4)
+    def _(g):
+        at = pl.multiple_of(g * 8, 8)
+        sums = totals(clusters + at)
+        here = arrived_ref[pl.ds(at, 8), :]
+        for d in range(3):
+            near = slice(d * 128, (d + 1) * 128)
+            part_ref[pl.ds(at, 8), near] = here[:, 384:512] * (here[:, near] * sums[0] - sums[d + 1])
 
 
 def shards(
@@ -739,7 +788,7 @@
     room = -(-(pairs + len(ORDER) * BATCH) // 1024) * 8
     still = lambda v: pltpu.with_memory_space_constraint(v, pltpu.HBM)
     ion_density, potential_prev, screening = map(still, (ion_density, potential_prev, screening))
-    data, arrived, update, resid, total, into, at_depth, order, *tables = pl.pallas_call(
+    data, arrived, update, resid, total, into, at_depth, edge, order, *tables = pl.pallas_call(
         functools.partial(send_kernel, groups, bricks),
         out_shape=(
             shape(clusters, 4 * psize),
@@ -749,13 +798,14 @@
             block,
             jax.ShapeDtypeStruct((nx * ny, clusters), BF16),
             shape(clusters, nz),
+            jax.ShapeDtypeStruct((2 * nx, clusters), BF16),
             jax.ShapeDtypeStruct((2, room + 1, 128), I32),
             shape(*table, 24, psize),
             shape(*table, 24, psize),
-            shape(*table, 16, psize),
+            jax.ShapeDtypeStruct((*table, 16, psize), BF16),
         ),
         in_specs=[smem] + [hbm] * 11,
-        out_specs=[vmem] * 11,
+        out_specs=[vmem] * 12,
         scratch_shapes=[
             pltpu.VMEM((clusters, 3, psize), F32),
             pltpu.VMEM((clusters, psize), F32),
@@ -813,7 +863,7 @@
     pull, pot, ion = pl.pallas_call(
         functools.partial(back_kernel, groups, bricks),
         out_shape=(shape(clusters, 3 * psize), padding, padding),
-        in_specs=[hbm] * 3 + [vmem] * 6,
+        in_specs=[hbm] * 3 + [vmem] * 8,
         out_specs=[vmem] * 3,
         scratch_shapes=[
             pltpu.VMEM((dirs, slots), I32),
@@ -821,6 +871,7 @@
             pltpu.VMEM((dirs * slots, 3 * psize), F32),
             pltpu.VMEM((nx, ny, nz), F32),
             pltpu.VMEM((nx, ny, nz), F32),
+            pltpu.VMEM((3, nx * ny, nz), F32),
             halo(late, 2, ny),
             halo(late, 2, ny),
             halo(late, 2, nx),
@@ -836,21 +887,20 @@
             collective_id=1, has_side_effects=True, vmem_limit_bytes=28 << 20
         ),
         name="back",
-    )(still(send_index), ion_density, screening, data, own_sums, part_sums, update, resid, total)
+    )(still(send_index), ion_density, screening, data, into, at_depth, own_sums, part_sums, update, resid, total)
     forces, potential, ion_next = pl.pallas_call(
         final_kernel,
         out_shape=(shape(clusters, 3, psize), block, block),
-        in_specs=[vmem] * 6,
+        in_specs=[vmem] * 7,
         out_specs=[hbm] * 3,
         scratch_shapes=[
             pltpu.VMEM((clusters, 3, psize), F32),
             pltpu.VMEM((nx, ny, nz), F32),
-            pltpu.VMEM((3, nx * ny, nz), F32),
-            pltpu.SemaphoreType.DMA((3,)),
+            pltpu.SemaphoreType.DMA((4,)),
         ],
         compiler_params=pltpu.CompilerParams(vmem_limit_bytes=28 << 20),
         name="final",
-    )(data, pull, pot, ion, into, at_depth)
+    )(data, pull, pot, ion, into, edge, at_depth)
     return (forces.transpose(1, 0, 2).reshape(3, -1), potential, ion_next)
 
 

time: 74.6 us -> 74.2 us (level)
    pallas_call x1, Pallas kernels: 20.4 us -> 29.5 us  [shards(): pl.pallas_call(pair_kernel, out_shape=(shape(clusters, 4 * psize), shape(...]
    pallas_call x1, Pallas kernels: 23.6 us -> 15 us  [shards(): pl.pallas_call(functools.partial(back_kernel, groups, bricks), out_shape=...]
where the time goes in v6:
time: 74.2 us; the launch traced here: 74 us
  Pallas kernels  73.4 us (99%)
    pallas_call x1, Pallas kernels, shards(): pl.pallas_call(pair_kernel, out_shape=(shape(clusters, 4 * psize), shape(...  29.5 us
    pallas_call x1, Pallas kernels, shards(): pl.pallas_call(functools.partial(send_kernel, groups, bricks), out_shape=...  25.9 us
    pallas_call x1, Pallas kernels, shards(): pl.pallas_call(functools.partial(back_kernel, groups, bricks), out_shape=...  15 us
    pallas_call x1, Pallas kernels, shards(): pl.pallas_call(final_kernel, out_shape=(shape(clusters, 3, psize), block,...  3.08 us

profile of v6, /device:TPU:1, one launch (start us, length us, event | category | flops | bytes accessed | tf_op | source)
XLA Modules:
  0.0 74.0 jit_solution(16477965529684585764)
XLA Ops:
  0.6 25.9 %send.1 = (f32[256,512]{1,0:T(8,128)S(1)}, f32[224,512]{1,0:T(8,128)S(1)}, f32[16,32,256]{2,1,0:T(8,128)S(1)}, f32[16,32,256]{2,1,0:T(8,128)S(1)}, f32[16,32,256...) custom-call(s32[1,7]{1,0:T(1,128)} %count_ref.1, ...), custom_call_target="tpu_custom_call" | custom-call | tf_op jit(solution)/shard_map/send/pallas_call | solution.py:791
  26.5 29.5 %pairs.1 = (f32[256,512]{1,0:T(8,128)S(1)}, f32[224,384]{1,0:T(8,128)S(1)}) custom-call(s32[2,17,128]{2,1,0:T(8,128)S(1)} %get-tuple-element.26.order, f32[224,512]{1,0:T(8,128)S(1)} %get-tuple-element.27.arrived_ref, f32[488,24,128]{2,1,0:T(8,128)S(1)} %get-tuple-element.28.row_feat, f32[488,24,128]{2,1,0:T(8,128)S(1)} %get-tuple-element.29.lane_feat, ...), custom_call_target="tpu_custom_call" | custom-call | tf_op jit(solution)/shard_map/pairs/pallas_call | solution.py:850
  56.0 15.0 %back.1 = (f32[256,384]{1,0:T(8,128)S(1)}, f32[18,48,256]{2,1,0:T(8,128)S(1)}, f32[18,48,256]{2,1,0:T(8,128)S(1)}) custom-call(s32[7,32]{1,0:T(8,128)} %index_hbm.3, f32[16,32,256]{2,1,0:T(8,128)} %ion_hbm.3, f32[16,32,256]{2,1,0:T(8,128)} %screen_hbm.3, f32[256,512]{1,0:T(8,128)S(1)} %get-tuple-element.23.data_ref, ...), custom_call_target="tpu_custom_call" | custom-call | tf_op jit(solution)/shard_map/back/pallas_call | solution.py:863
  71.0 3.1 %final.1 = (f32[256,3,128]{2,1,0:T(4,128)}, f32[16,32,256]{2,1,0:T(8,128)}, f32[16,32,256]{2,1,0:T(8,128)}) custom-call(f32[256,512]{1,0:T(8,128)S(1)} %get-tuple-element.23.data_ref, f32[256,384]{1,0:T(8,128)S(1)} %get-tuple-element.36.pull_ref, f32[18,48,256]{2,1,0:T(8,128)S(1)} %get-tuple-element.37.pot, f32[18,48,256]{2,1,0:T(8,128)S(1)} %get-tuple-element.38.ion, ...), custom_call_target="tpu_custom_call" | custom-call | tf_op jit(solution)/shard_map/final/pallas_call | solution.py:891

commit v7 on v6

--- a/solution.py
+++ b/solution.py
@@ -269,6 +269,7 @@
     update_ref,
     resid_ref,
     total_ref,
+    ion_ref,
     into_ref,
     depth_ref,
     edge_ref,
@@ -303,13 +304,13 @@
         pltpu.make_async_copy(src, dst, load.at[i])
         for i, (src, dst) in enumerate(
             (
+                (prev_hbm, pad.at[0, pl.ds(1, nx), pl.ds(TOP, ny), :]),
+                (ion_hbm, ion_ref.at[pl.ds(1, nx), pl.ds(TOP, ny), :]),
                 (index_hbm, index),
                 (fill_hbm, fill),
                 (cell_hbm, cells),
-                (prev_hbm, pad.at[0, pl.ds(1, nx), pl.ds(TOP, ny), :]),
                 (pos_hbm, pos),
                 (charge_hbm, charges),
-                (ion_hbm, resid_ref),
                 (screen_hbm, screen),
                 (local_hbm, pair_local),
                 (dir_hbm, pair_dir),
@@ -323,9 +324,14 @@
     inside = inside_flags(groups, bricks)
     clear_halos(pad.at[0])
     clear_halos(pad.at[1])
-    for copy in loads[:4]:
+    for copy in loads[:2]:
         copy.wait()
     exchange = (x_out, x_in, y_out, y_in, halo_send, halo_recv, groups, bricks)
+    pl.semaphore_wait(barrier, len(OFFSETS) - 1)
+    fields = [pad.at[0], ion_ref]
+    halos = start_halos(0, fields, 0, *exchange) + start_halos(1, fields, 0, *exchange)
+    for copy in loads[2:]:
+        copy.wait()
     clusters = charges.shape[0]
     slots = index.shape[1]
     wanted = slot_row(index)
@@ -334,14 +340,10 @@
     ).astype(BF16)
     fill_col = columns(fill[...])
     lane = lax.broadcasted_iota(I32, (clusters, 128), 1).astype(F32)
-    for copy in loads[4:]:
-        copy.wait()
     charge = charges[...] * jnp.where(lane < fill_col, 1.0, 0.0)
     for d in range(3):
         data_ref[:, d * 128 : (d + 1) * 128] = pos[:, d, :]
     data_ref[:, 384:512] = charge
-    pl.semaphore_wait(barrier, len(OFFSETS) - 1)
-    halos = start_halos(0, [pad.at[0]], 0, *exchange) + start_halos(1, [pad.at[0]], 0, *exchange)
     out_rows[...] = select_rows(chooser, data_ref[...], ((0,), (0,)))
     slot_id = lax.broadcasted_iota(I32, (slots, 128), 0)
     for k in range(len(OFFSETS)):
@@ -355,7 +357,8 @@
     edge_ref[...] = edge
     depth_ref[...] = at_depth
     deposit = select_rows(into, at_depth * jnp.sum(charge, axis=1, keepdims=True))
-    resid_ref[...] = resid_ref[...] + deposit_scale * deposit.reshape(nx, ny, nz)
+    density = ion_ref[1 : nx + 1, TOP : TOP + ny, :]
+    resid_ref[...] = density + deposit_scale * deposit.reshape(nx, ny, nz)
     for turn in range(EARLY):
         held, other = pad.at[turn % 2], pad.at[1 - turn % 2]
         if turn == EARLY - 2:
@@ -382,6 +385,8 @@
         if turn + 1 < EARLY:
             halos = start_halos(0, [other], turn + 1, *exchange)
             halos = halos + start_halos(1, [other], turn + 1, *exchange)
+        if turn == 0:
+            place_halos(ion_ref, (0, 1), x_in, y_in, inside)
     update_ref[...] = pad[EARLY % 2, 1 : nx + 1, TOP : TOP + ny, :]
 
 
@@ -389,7 +394,6 @@
     groups,
     bricks,
     index_hbm,
-    ion_hbm,
     screen_hbm,
     data_ref,
     into_ref,
@@ -401,7 +405,6 @@
     total_ref,
     pull_ref,
     pot_ref,
-    ion_ref,
     index,
     screen,
     back,
@@ -419,13 +422,10 @@
     halo_send,
     halo_recv,
 ):
-    nx, ny, nz = ion_hbm.shape
+    nx, ny, nz = screen_hbm.shape
     loads = [
-        pltpu.make_async_copy(
-            ion_hbm, ion_ref.at[pl.ds(1, nx), pl.ds(TOP, ny), :], load.at[0]
-        ),
-        pltpu.make_async_copy(screen_hbm, screen, load.at[1]),
-        pltpu.make_async_copy(index_hbm, index, load.at[2]),
+        pltpu.make_async_copy(screen_hbm, screen, load.at[0]),
+        pltpu.make_async_copy(index_hbm, index, load.at[1]),
     ]
     for copy in loads:
         copy.start()
@@ -436,13 +436,12 @@
     clear_halos(pad.at[1])
     clear_halos(pot_ref)
     first[1 : nx + 1, TOP : TOP + ny, :] = update_ref[...]
+    exchange = (x_out, x_in, y_out, y_in, halo_send, halo_recv, groups, bricks)
+    pl.semaphore_wait(barrier, len(OFFSETS) - 1)
+    halos = start_halos(0, [first], 0, *exchange) + start_halos(1, [first], 0, *exchange)
+    sends = send_rows(part_ref, back, 1, row_send, row_recv, groups, bricks)
     for copy in loads:
         copy.wait()
-    exchange = (x_out, x_in, y_out, y_in, halo_send, halo_recv, groups, bricks)
-    pl.semaphore_wait(barrier, len(OFFSETS) - 1)
-    halos = start_halos(0, [first, ion_ref], 0, *exchange)
-    halos = halos + start_halos(1, [first, ion_ref], 0, *exchange)
-    sends = send_rows(part_ref, back, 1, row_send, row_recv, groups, bricks)
     resid[...] = resid_ref[...]
     total[...] = total_ref[...]
     slots = part_ref.shape[0] // len(OFFSETS)
@@ -466,8 +465,6 @@
         add_halos(turn, turn - EARLY, other, resid, screen, total, x_in, y_in, inside)
         halos = start_halos(0, [other], turn + 1 - EARLY, *exchange)
         halos = halos + start_halos(1, [other], turn + 1 - EARLY, *exchange)
-        if turn == EARLY:
-            place_halos(ion_ref, (0, 1), x_in, y_in, inside)
 
     def field(i, carry):
         lo, hi = TOP, TOP + ny
@@ -788,7 +785,7 @@
     room = -(-(pairs + len(ORDER) * BATCH) // 1024) * 8
     still = lambda v: pltpu.with_memory_space_constraint(v, pltpu.HBM)
     ion_density, potential_prev, screening = map(still, (ion_density, potential_prev, screening))
-    data, arrived, update, resid, total, into, at_depth, edge, order, *tables = pl.pallas_call(
+    data, arrived, update, resid, total, ion, into, at_depth, edge, order, *tables = pl.pallas_call(
         functools.partial(send_kernel, groups, bricks),
         out_shape=(
             shape(clusters, 4 * psize),
@@ -796,6 +793,7 @@
             block,
             block,
             block,
+            shape(*padded),
             jax.ShapeDtypeStruct((nx * ny, clusters), BF16),
             shape(clusters, nz),
             jax.ShapeDtypeStruct((2 * nx, clusters), BF16),
@@ -805,7 +803,7 @@
             jax.ShapeDtypeStruct((*table, 16, psize), BF16),
         ),
         in_specs=[smem] + [hbm] * 11,
-        out_specs=[vmem] * 12,
+        out_specs=[vmem] * 13,
         scratch_shapes=[
             pltpu.VMEM((clusters, 3, psize), F32),
             pltpu.VMEM((clusters, psize), F32),
@@ -818,10 +816,10 @@
             pltpu.VMEM((nx, ny, nz), F32),
             pltpu.VMEM((dirs * slots, 4 * psize), F32),
             pltpu.VMEM((dirs * slots, 4 * psize), F32),
-            halo(EARLY, 1, ny),
-            halo(EARLY, 1, ny),
-            halo(EARLY, 1, nx),
-            halo(EARLY, 1, nx),
+            halo(EARLY, 2, ny),
+            halo(EARLY, 2, ny),
+            halo(EARLY, 2, nx),
+            halo(EARLY, 2, nx),
             pltpu.VMEM((2, *padded), F32),
             pltpu.SemaphoreType.DMA((11,)),
             pltpu.SemaphoreType.DMA((dirs - 1,)),
@@ -860,11 +858,11 @@
         name="pairs",
     )(order, arrived, *tables)
     padding = shape(*padded)
-    pull, pot, ion = pl.pallas_call(
+    pull, pot = pl.pallas_call(
         functools.partial(back_kernel, groups, bricks),
-        out_shape=(shape(clusters, 3 * psize), padding, padding),
-        in_specs=[hbm] * 3 + [vmem] * 8,
-        out_specs=[vmem] * 3,
+        out_shape=(shape(clusters, 3 * psize), padding),
+        in_specs=[hbm] * 2 + [vmem] * 8,
+        out_specs=[vmem] * 2,
         scratch_shapes=[
             pltpu.VMEM((dirs, slots), I32),
             pltpu.VMEM((nx, ny, nz), F32),
@@ -872,12 +870,12 @@
             pltpu.VMEM((nx, ny, nz), F32),
             pltpu.VMEM((nx, ny, nz), F32),
             pltpu.VMEM((3, nx * ny, nz), F32),
-            halo(late, 2, ny),
-            halo(late, 2, ny),
-            halo(late, 2, nx),
-            halo(late, 2, nx),
+            halo(late, 1, ny),
+            halo(late, 1, ny),
+            halo(late, 1, nx),
+            halo(late, 1, nx),
             pltpu.VMEM((2, *padded), F32),
-            pltpu.SemaphoreType.DMA((3,)),
+            pltpu.SemaphoreType.DMA((2,)),
             pltpu.SemaphoreType.DMA((dirs - 1,)),
             pltpu.SemaphoreType.DMA((dirs - 1,)),
             pltpu.SemaphoreType.DMA((late, 4)),
@@ -887,7 +885,7 @@
             collective_id=1, has_side_effects=True, vmem_limit_bytes=28 << 20
         ),
         name="back",
-    )(still(send_index), ion_density, screening, data, into, at_depth, own_sums, part_sums, update, resid, total)
+    )(still(send_index), screening, data, into, at_depth, own_sums, part_sums, update, resid, total)
     forces, potential, ion_next = pl.pallas_call(
         final_kernel,
         out_shape=(shape(clusters, 3, psize), block, block),

time: 74.2 us -> 70.6 us (0.951)
  the two profiles are of different devices: /device:TPU:1 before, /device:TPU:9 now
where the time goes in v7:
time: 70.6 us; the launch traced here: 70.4 us
  Pallas kernels  69.8 us (99%)
    pallas_call x1, Pallas kernels, shards(): pl.pallas_call(pair_kernel, out_shape=(shape(clusters, 4 * psize), shape(...  27.5 us
    pallas_call x1, Pallas kernels, shards(): pl.pallas_call(functools.partial(send_kernel, groups, bricks), out_shape=...  26.1 us
    pallas_call x1, Pallas kernels, shards(): pl.pallas_call(functools.partial(back_kernel, groups, bricks), out_shape=...  13.2 us
    pallas_call x1, Pallas kernels, shards(): pl.pallas_call(final_kernel, out_shape=(shape(clusters, 3, psize), block,...  3.08 us

profile of v7, /device:TPU:9, one launch (start us, length us, event | category | flops | bytes accessed | tf_op | source)
XLA Modules:
  0.0 70.4 jit_solution(4349713528354073445)
XLA Ops:
  0.6 26.1 %send.1 = (f32[256,512]{1,0:T(8,128)S(1)}, f32[224,512]{1,0:T(8,128)S(1)}, f32[16,32,256]{2,1,0:T(8,128)S(1)}, f32[16,32,256]{2,1,0:T(8,128)S(1)}, f32[16,32,256...) custom-call(s32[1,7]{1,0:T(1,128)} %count_ref.1, ...), custom_call_target="tpu_custom_call" | custom-call | tf_op jit(solution)/shard_map/send/pallas_call | solution.py:788
  26.7 27.5 %pairs.1 = (f32[256,512]{1,0:T(8,128)S(1)}, f32[224,384]{1,0:T(8,128)S(1)}) custom-call(s32[2,17,128]{2,1,0:T(8,128)S(1)} %get-tuple-element.26.order, f32[224,512]{1,0:T(8,128)S(1)} %get-tuple-element.27.arrived_ref, f32[488,24,128]{2,1,0:T(8,128)S(1)} %get-tuple-element.28.row_feat, f32[488,24,128]{2,1,0:T(8,128)S(1)} %get-tuple-element.29.lane_feat, ...), custom_call_target="tpu_custom_call" | custom-call | tf_op jit(solution)/shard_map/pairs/pallas_call | solution.py:848
  54.2 13.2 %back.1 = (f32[256,384]{1,0:T(8,128)S(1)}, f32[18,48,256]{2,1,0:T(8,128)S(1)}) custom-call(s32[7,32]{1,0:T(8,128)} %index_hbm.3, f32[16,32,256]{2,1,0:T(8,128)} %screen_hbm.3, f32[256,512]{1,0:T(8,128)S(1)} %get-tuple-element.23.data_ref, bf16[512,256]{1,0:T(8,128)(2,1)S(1)} %get-tuple-element.24.into_ref, f32[256,256]{1,0:T(8,128)S(1)} %get-tuple-element.25.depth_ref, ...), custom_call_target="tpu_custom_call" | custom-call | tf_op jit(solution)/shard_map/back/pallas_call | solution.py:861
  67.4 3.1 %final.1 = (f32[256,3,128]{2,1,0:T(4,128)}, f32[16,32,256]{2,1,0:T(8,128)}, f32[16,32,256]{2,1,0:T(8,128)}) custom-call(f32[256,512]{1,0:T(8,128)S(1)} %get-tuple-element.23.data_ref, f32[256,384]{1,0:T(8,128)S(1)} %get-tuple-element.36.pull_ref, f32[18,48,256]{2,1,0:T(8,128)S(1)} %get-tuple-element.37.pot, f32[18,48,256]{2,1,0:T(8,128)S(1)} %get-tuple-element.38.ion, ...), custom_call_target="tpu_custom_call" | custom-call | tf_op jit(solution)/shard_map/final/pallas_call | solution.py:889
